TPU v7x, 32 devices: a whole 2x2x4 slice. The times are simulated.
32 devices in a mesh: band: 4 (over y, x), domain: 8 (over z, core).
Axes of the slice: x: 2, y: 2, z: 4, core: 2. Of those that a mesh axis runs over, the one named last changes fastest.
Arguments:
- orbitals: float32 [6144, 512], P('domain', 'band'), may hold values from -6 to 6
- potential: float32 [6144], P('domain'), may hold values from -1 to 1
- occupation: float32 [512], P('band'), may hold values from 0 to 0.0068359375, as said below
- cell_matrix: bfloat16 [343, 343], replicated, may hold values from -1 to 2, as said below
- cell_nodes: int32 [32, 343], P('domain'), may hold values from 0 to 936, as said below
- face_order: int32 [8, 169], P('domain'), may hold values from 0 to 168, as said below
- pois_matrix: float32 [729, 729], replicated, may hold values from -1 to 2, as said below
- pois_nodes: int32 [16, 729], P('domain'), may hold values from 0 to 848, as said below
- pois_face: int32 [8, 81], P('domain'), may hold values from 0 to 80, as said below
- screening: float32 [6144], P('domain'), may hold values from 0.5 to 2
- block_owner: int32 [8, 8], P('domain'), may hold values from 0 to 7, as said below
Outputs:
- filtered: float32 [6144, 512], P('domain', 'band')
- hartree: float32 [6144], P('domain')
Inputs may be any that keep to these rules, and one draw needn't show every extreme that they name: `occupation`: positive weights. `cell_matrix`: symmetric. `pois_matrix`: symmetric. `cell_nodes`: cell c (counted from 0 within its domain) uses the local nodes (c * 234 + k) mod 937 for k < 343, in a drawn order. `pois_nodes`: cell c (counted from 0 within its domain) uses the local nodes (c * 424 + k) mod 849 for k < 729, in a drawn order. `face_order`: each row is a permutation. `pois_face`: each row is a permutation. `block_owner`: each row is a permutation.
All inputs are finite; a program needn't handle non-finite values.
Results may differ from a plain program's by a relative error of at most 0.0065.
The roundings to bfloat16 on the way count: a program that leaves them out, or rounds other values in their place, can miss the bound.
Values may be sent and summed in bfloat16 or wider, within the bound.
No kernel may reach another device: no remote copies, remote signals or barrier semaphores. Data moves between devices by JAX's collectives and lax.ppermute only.
A program may use at most 64 MiB of HBM per device.

v0:
```python
import jax
import jax.numpy as jnp
from jax import lax
from jax.sharding import PartitionSpec as P

filter_center = 1.8
filter_half = 2.7
solve_center = 3.25
solve_half = 2.75
solve_ratio = solve_center / solve_half
weight_zero = 1.0 / solve_ratio
weight_one = 1.0 / (2.0 * solve_ratio - weight_zero)
weight_two = 1.0 / (2.0 * solve_ratio - weight_one)


def from_behind(array, axis, by):
    length = lax.axis_size(axis)
    return lax.ppermute(array, axis, [(i, (i + by) % length) for i in range(length)])


def filter_step(applied, current, earlier):
    if earlier is None:
        return (applied - filter_center * current) / filter_half
    return 2.0 * (applied - filter_center * current) / filter_half - earlier


def next_rows(values, face_row):
    coming = from_behind(values, "domain", -1)
    return jnp.take(coming, face_row, axis=0)


def next_low_rows(values, face_row):
    coming = from_behind(values, "domain", -1)
    return jnp.take(coming, face_row, axis=0)


def fold_back(upper_rows, face_row):
    ordered = jnp.zeros_like(upper_rows).at[face_row].set(upper_rows)
    return from_behind(ordered, "domain", 1)


def assembled(owned_rows, face_row, terms):
    owned_count = owned_rows.shape[0]
    shared = face_row.shape[0]
    local_rows = jnp.concatenate([owned_rows, next_rows(owned_rows[:shared], face_row)], axis=0)
    partial_value = terms(local_rows)
    arrived = fold_back(partial_value[owned_count:], face_row)
    return partial_value[:owned_count].at[:shared].add(arrived)


def assembled_low(owned_rows, face_row, terms):
    owned_count = owned_rows.shape[0]
    shared = face_row.shape[0]
    low_rows = owned_rows.astype(jnp.bfloat16)
    local_rows = jnp.concatenate([low_rows, next_low_rows(low_rows[:shared], face_row)], axis=0)
    partial_value = terms(local_rows)
    arrived = fold_back(partial_value[owned_count:], face_row)
    return partial_value[:owned_count].at[:shared].add(arrived)


def cell_terms(local_rows, cell_matrix, node_ids):
    cell_vals = jnp.take(local_rows, node_ids, axis=0)
    product = jnp.einsum("pq,cqm->cpm", cell_matrix, cell_vals, preferred_element_type=jnp.float32)
    columns = local_rows.shape[1]
    return (
        jnp.zeros(local_rows.shape, jnp.float32)
        .at[node_ids.reshape(-1)]
        .add(product.reshape(-1, columns))
    )


def field_terms(local_rows, pois_matrix, node_ids):
    cell_vals = jnp.take(local_rows, node_ids, axis=0)
    product = jnp.einsum(
        "pq,cq->cp",
        pois_matrix,
        cell_vals,
        precision=lax.Precision.HIGHEST,
        preferred_element_type=jnp.float32,
    )
    return (
        jnp.zeros(local_rows.shape, jnp.float32).at[node_ids.reshape(-1)].add(product.reshape(-1))
    )


def reshuffle(blocks):
    return lax.all_to_all(blocks, "domain", split_axis=0, concat_axis=0, tiled=True)


def band_total(values):
    return lax.psum(values, "band")


def per_device(
    orbitals,
    potential,
    occupation,
    cell_matrix,
    cell_nodes,
    face_order,
    pois_matrix,
    pois_nodes,
    pois_face,
    screening,
    block_owner,
):
    domains = lax.axis_size("domain")
    owned_count = orbitals.shape[0]
    block_len = owned_count // domains
    face_row = face_order[0]
    owner_row = block_owner[0]
    field_face = pois_face[0]

    def orbital_terms(local_rows):
        return cell_terms(local_rows, cell_matrix, cell_nodes)

    def hamiltonian(vector, potential_in):
        return assembled_low(vector, face_row, orbital_terms) + potential_in[:, None] * vector

    filter_one = filter_step(hamiltonian(orbitals, potential), orbitals, None)
    filter_two = filter_step(hamiltonian(filter_one, potential), filter_one, orbitals)
    filter_three = filter_step(hamiltonian(filter_two, potential), filter_two, filter_one)
    partial_value = jnp.dot(
        filter_three * filter_three,
        occupation,
        precision=lax.Precision.HIGHEST,
        preferred_element_type=jnp.float32,
    )
    summed = band_total(partial_value)
    arranged = (
        jnp.zeros((domains, block_len), jnp.float32)
        .at[owner_row]
        .set(summed.reshape(domains, block_len))
    )
    source = reshuffle(arranged).reshape(owned_count)

    def field_operator(vector):
        return (
            assembled(
                vector,
                field_face,
                lambda local_rows: field_terms(local_rows, pois_matrix, pois_nodes),
            )
            + screening * vector
        )

    step_one = source / solve_center
    residual = source - field_operator(step_one)
    step_two = weight_one * weight_zero * step_one + 2.0 * weight_one / solve_half * residual
    residual = residual - field_operator(step_two)
    step_three = weight_two * weight_one * step_two + 2.0 * weight_two / solve_half * residual
    solution = step_one + step_two + step_three
    returned = reshuffle(solution.reshape(domains, block_len))
    hartree = jnp.take(returned, owner_row, axis=0).reshape(owned_count)
    potential_new = potential + hartree
    refilter_one = filter_step(hamiltonian(filter_three, potential_new), filter_three, None)
    refilter_two = filter_step(hamiltonian(refilter_one, potential_new), refilter_one, filter_three)
    return (refilter_two, hartree)


def solution(mesh):
    return jax.shard_map(
        per_device,
        mesh=mesh,
        in_specs=(
            P("domain", "band"),
            P("domain"),
            P("band"),
            P(),
            P("domain", None),
            P("domain", None),
            P(),
            P("domain", None),
            P("domain", None),
            P("domain"),
            P("domain", None),
        ),
        out_specs=(P("domain", "band"), P("domain")),
        check_vma=False,
    )
```

profile of v0, /device:TPU:0, one launch (start us, length us, event | category | flops | bytes accessed | tf_op | source)
XLA Modules:
  0.0 261.4 jit_solution(17496827061707327766)
XLA Ops:
  1.8 4.6 %collective-permute-start = (bf16[169,128]{1,0:T(8,128)(2,1)S(1)}, bf16[169,128]{1,0:T(8,128)(2,1)S(1)}, u32[]{:S(2)}, u32[]{:S(2)}) collective-permute-start(bf16[169,128]{1,0:T(8,128)(2,1)S(1)} %slice.251), channel_id=1, source_target_pairs={{0,7},{1,0},{2,1},{3,2},{4,3},{5,4},{6,5},{7,6},{8,15},{9,8},{10,9... | collective-permute-start | bytes 129800 | tf_op jit(solution)/shard_map/ppermute | solution.py:18
  13.0 3.3 %gather_fusion.2 = bf16[1372,128]{1,0:T(8,128)(2,1)S(1)} fusion(bf16[937,128]{1,0:T(8,128)(2,1)S(1)} %pad_maximum_fusion, s32[2048]{0:T(1024)S(1)} %pad_clamp_fusion.1), kind=kCustom, calls=%fused_computation.1.clone | custom fusion | bytes 707952 | tf_op jit(solution)/shard_map/jit(_take)/gather | solution.py:62
  17.9 2.0 reshape.513
  19.9 9.9 %scatter_custom_fusion = f32[937,128]{1,0:T(8,128)} fusion(s32[1372]{0:T(1024)S(1)} %fusion.51, f32[1372,128]{1,0:T(8,128)} %reshape.513, f32[]{:T(128)} %constant.233.clone.1), kind=kCustom, calls=%fused_computation.72 | custom fusion | flops 175616 | bytes 480256 | tf_op jit(solution)/shard_map/scatter-add | solution.py:68
  32.8 4.1 %collective-permute-done.1 = f32[169,128]{1,0:T(8,128)S(1)} collective-permute-done((f32[169,128]{1,0:T(8,128)S(1)}, f32[169,128]{1,0:T(8,128)S(1)}, u32[]{:S(2)}, u32[]{:S(2)}) %collective-permute-start.1) | collective-permute-done | bytes 86560 | tf_op jit(solution)/shard_map/ppermute | solution.py:18
  43.7 4.4 %gather_fusion.4 = bf16[1372,128]{1,0:T(8,128)(2,1)} fusion(bf16[937,128]{1,0:T(8,128)(2,1)S(1)} %pad_maximum_fusion.1, s32[2048]{0:T(1024)} %copy-done.7), kind=kCustom, calls=%fused_computation.8.clone | custom fusion | bytes 707952 | tf_op jit(solution)/shard_map/jit(_take)/gather | solution.py:62
  48.1 1.8 reshape.661
  49.9 2.4 convolution_bitcast_fusion.3
  52.4 2.1 reshape.529
  54.4 9.9 %scatter_custom_fusion.2 = f32[937,128]{1,0:T(8,128)} fusion(s32[1372]{0:T(1024)} %copy-done.25, f32[1372,128]{1,0:T(8,128)} %reshape.529, f32[]{:T(128)} %constant.233.clone.1), kind=kCustom, calls=%fused_computation.70 | custom fusion | flops 175616 | bytes 480256 | tf_op jit(solution)/shard_map/scatter-add | solution.py:68
  66.3 1.8 slice.256
  68.1 3.4 %collective-permute-done.3 = f32[169,128]{1,0:T(8,128)S(1)} collective-permute-done((f32[169,128]{1,0:T(8,128)S(1)}, f32[169,128]{1,0:T(8,128)S(1)}, u32[]{:S(2)}, u32[]{:S(2)}) %collective-permute-start.3) | collective-permute-done | bytes 86560 | tf_op jit(solution)/shard_map/ppermute | solution.py:18
  72.4 1.6 scatter-add.87
  79.0 4.0 %gather_fusion.6 = bf16[1372,128]{1,0:T(8,128)(2,1)} fusion(bf16[937,128]{1,0:T(8,128)(2,1)S(1)} %pad_maximum_fusion.2, s32[2048]{0:T(1024)S(1)} %copy-done.8), kind=kCustom, calls=%fused_computation.9.clone | custom fusion | bytes 707952 | tf_op jit(solution)/shard_map/jit(_take)/gather | solution.py:62
  85.6 2.0 reshape.545
  87.6 9.9 %scatter_custom_fusion.4 = f32[937,128]{1,0:T(8,128)} fusion(s32[1372]{0:T(1024)} %copy-done.25, f32[1372,128]{1,0:T(8,128)} %reshape.545, f32[]{:T(128)} %constant.233.clone.1), kind=kCustom, calls=%fused_computation.68 | custom fusion | flops 175616 | bytes 480256 | tf_op jit(solution)/shard_map/scatter-add | solution.py:68
  98.9 1.8 slice.260
  100.7 4.0 %collective-permute-done.5 = f32[169,128]{1,0:T(8,128)S(1)} collective-permute-done((f32[169,128]{1,0:T(8,128)S(1)}, f32[169,128]{1,0:T(8,128)S(1)}, u32[]{:S(2)}, u32[]{:S(2)}) %collective-permute-start.5) | collective-permute-done | bytes 86560 | tf_op jit(solution)/shard_map/ppermute | solution.py:18
  105.5 1.6 scatter-add.89
  109.9 9.9 %psum.7 = f32[8,96]{1,0:T(8,128)S(1)} all-reduce(f32[8,96]{1,0:T(8,128)S(1)} %reshape.383), channel_id=1, replica_groups=mesh['band'=4,'domain'=8] {'band'}, use_global_device_ids=true, to_apply=%region_8.11 | all-reduce | flops 768 | bytes 6144 | tf_op jit(solution)/shard_map/psum | solution.py:91
  121.1 3.3 %all-to-all-start = ((f32[8,1,96]{2,1,0:T(1,128)}), f32[8,1,96]{2,1,0:T(1,128)S(1)}, u32[]{:S(2)}, u32[]{:S(2)}) async-start(f32[8,1,96]{2,1,0:T(1,128)} %bitcast.12), calls=%async_computation | async-start | bytes 8192 | tf_op jit(solution)/shard_map/all_to_all | solution.py:87
  124.4 5.4 %all-to-all-done = f32[8,1,96]{2,1,0:T(1,128)S(1)} async-done(((f32[8,1,96]{2,1,0:T(1,128)}), f32[8,1,96]{2,1,0:T(1,128)S(1)}, u32[]{:S(2)}, u32[]{:S(2)}) %all-to-all-start) | async-done | bytes 3104 | tf_op jit(solution)/shard_map/all_to_all | solution.py:87
  134.3 5.6 %gather_fusion.10 = f32[1458]{0:T(1024)S(1)} fusion(f32[849]{0:T(1024)S(1)} %pad_maximum_fusion.5, s32[2048]{0:T(1024)S(1)} %pad_clamp_fusion), kind=kCustom, calls=%fused_computation.3.clone | custom fusion | bytes 17496 | tf_op jit(solution)/shard_map/jit(_take)/gather | solution.py:73
  140.1 1.9 fusion.49
  142.2 11.0 %scatter_custom_fusion.9 = f32[849]{0:T(1024)S(1)} fusion(s32[1458]{0:T(1024)S(1)} %fusion.46, f32[1458]{0:T(1024)S(1)} %reshape.585, f32[]{:T(128)} %constant.233.clone.1), kind=kCustom, calls=%fused_computation.137 | custom fusion | flops 1458 | bytes 3400 | tf_op jit(solution)/shard_map/scatter-add | solution.py:82
  155.7 3.3 %collective-permute-done.9 = f32[81]{0:T(128)S(1)} collective-permute-done((f32[81]{0:T(128)S(1)}, f32[81]{0:T(128)S(1)}, u32[]{:S(2)}, u32[]{:S(2)}) %collective-permute-start.9) | collective-permute-done | bytes 356 | tf_op jit(solution)/shard_map/ppermute | solution.py:18
  161.9 5.7 %gather_fusion.12 = f32[1458]{0:T(1024)S(1)} fusion(f32[849]{0:T(1024)S(1)} %pad_maximum_fusion.6, s32[2048]{0:T(1024)S(1)} %pad_clamp_fusion), kind=kCustom, calls=%fused_computation.13.clone | custom fusion | bytes 17496 | tf_op jit(solution)/shard_map/jit(_take)/gather | solution.py:73
  167.7 1.9 fusion.47
  169.7 11.0 %scatter_custom_fusion.11 = f32[849]{0:T(1024)S(1)} fusion(s32[1458]{0:T(1024)S(1)} %fusion.46, f32[1458]{0:T(1024)S(1)} %reshape.601, f32[]{:T(128)} %constant.233.clone.1), kind=kCustom, calls=%fused_computation.135 | custom fusion | flops 1458 | bytes 3400 | tf_op jit(solution)/shard_map/scatter-add | solution.py:82
  181.8 4.7 %collective-permute-done.11 = f32[81]{0:T(128)S(1)} collective-permute-done((f32[81]{0:T(128)S(1)}, f32[81]{0:T(128)S(1)}, u32[]{:S(2)}, u32[]{:S(2)}) %collective-permute-start.11) | collective-permute-done | bytes 356 | tf_op jit(solution)/shard_map/ppermute | solution.py:18
  187.3 3.3 %all-to-all-start.1 = ((f32[8,1,96]{2,1,0:T(1,128)}), f32[8,1,96]{2,1,0:T(1,128)S(1)}, u32[]{:S(2)}, u32[]{:S(2)}) async-start(f32[8,1,96]{2,1,0:T(1,128)} %all_to_all.16), calls=%async_computation.1 | async-start | bytes 8192 | tf_op jit(solution)/shard_map/all_to_all | solution.py:87
  190.6 3.5 %collective-permute-start.6 = (bf16[169,128]{1,0:T(8,128)(2,1)S(1)}, bf16[169,128]{1,0:T(8,128)(2,1)S(1)}, u32[]{:S(2)}, u32[]{:S(2)}) collective-permute-start(bf16[169,128]{1,0:T(8,128)(2,1)S(1)} %slice.263), channel_id=1, source_target_pairs={{0,7},{1,0},{2,1},{3,2},{4,3},{5,4},{6,5},{7,6},{8,15},{9,8},{10,9... | collective-permute-start | bytes 129800 | tf_op jit(solution)/shard_map/ppermute | solution.py:18
  194.1 1.9 all-to-all-done.1
  197.6 4.0 %gather_fusion.8 = bf16[1372,128]{1,0:T(8,128)(2,1)} fusion(bf16[937,128]{1,0:T(8,128)(2,1)S(1)} %pad_maximum_fusion.3, s32[2048]{0:T(1024)S(1)} %copy-done.8), kind=kCustom, calls=%fused_computation.10.clone | custom fusion | bytes 707952 | tf_op jit(solution)/shard_map/jit(_take)/gather | solution.py:62
  204.2 2.0 reshape.561
  206.2 9.3 %scatter_custom_fusion.6 = f32[937,128]{1,0:T(8,128)S(1)} fusion(s32[1372]{0:T(1024)} %copy-done.25, f32[1372,128]{1,0:T(8,128)} %reshape.561, f32[]{:T(128)} %constant.233.clone.1), kind=kCustom, calls=%fused_computation.66 | custom fusion | flops 175616 | bytes 480256 | tf_op jit(solution)/shard_map/scatter-add | solution.py:68
  215.4 1.7 scatter_custom_fusion.7
  218.8 4.3 %collective-permute-done.7 = f32[169,128]{1,0:T(8,128)S(1)} collective-permute-done((f32[169,128]{1,0:T(8,128)}, f32[169,128]{1,0:T(8,128)S(1)}, u32[]{:S(2)}, u32[]{:S(2)}) %collective-permute-start.7) | collective-permute-done | bytes 86560 | tf_op jit(solution)/shard_map/ppermute | solution.py:18
  225.6 1.7 collective-permute-done.12
  229.2 4.4 %gather_fusion.14 = bf16[1372,128]{1,0:T(8,128)(2,1)} fusion(bf16[937,128]{1,0:T(8,128)(2,1)S(1)} %pad_maximum_fusion.4, s32[2048]{0:T(1024)} %copy-done.7), kind=kCustom, calls=%fused_computation.11.clone | custom fusion | bytes 707952 | tf_op jit(solution)/shard_map/jit(_take)/gather | solution.py:62
  233.5 1.8 reshape.691
  235.4 2.4 convolution_bitcast_fusion
  237.7 2.0 reshape.617
  239.7 9.9 %scatter_custom_fusion.13 = f32[937,128]{1,0:T(8,128)} fusion(s32[1372]{0:T(1024)} %copy-done.25, f32[1372,128]{1,0:T(8,128)} %reshape.617, f32[]{:T(128)} %constant.233.clone.1), kind=kCustom, calls=%fused_computation.64 | custom fusion | flops 175616 | bytes 480256 | tf_op jit(solution)/shard_map/scatter-add | solution.py:68
  251.1 1.8 slice.268
  252.8 4.0 %collective-permute-done.13 = f32[169,128]{1,0:T(8,128)S(1)} collective-permute-done((f32[169,128]{1,0:T(8,128)S(1)}, f32[169,128]{1,0:T(8,128)S(1)}, u32[]{:S(2)}, u32[]{:S(2)}) %collective-permute-start.13) | collective-permute-done | bytes 86560 | tf_op jit(solution)/shard_map/ppermute | solution.py:18
  257.7 1.6 scatter-add.97
  259.4 2.0 multiply_subtract_fusion
  (182 shorter events, 59.9 us)
Async XLA Ops:
  0.6 139.5 %copy-start = (f32[729,729]{1,0:T(8,128)S(1)}, f32[729,729]{1,0:T(8,128)}, u32[]{:S(2)}) copy-start(f32[729,729]{1,0:T(8,128)} %param.39) | copy-start | bytes 6377296
  1.8 10.3 %collective-permute-start = (bf16[169,128]{1,0:T(8,128)(2,1)S(1)}, bf16[169,128]{1,0:T(8,128)(2,1)S(1)}, u32[]{:S(2)}, u32[]{:S(2)}) collective-permute-start(bf16[169,128]{1,0:T(8,128)(2,1)S(1)} %slice.251), channel_id=1, source_target_pairs={{0,7},{1,0},{2,1},{3,2},{4,3},{5,4},{6,5},{7,6},{8,15},{9,8},{10,9... | collective-permute-start | bytes 129800 | tf_op jit(solution)/shard_map/ppermute | solution.py:18
  7.8 8.7 %copy-start.23 = (pred[169]{0:T(512)(128)(4,1)}, pred[169]{0:T(512)(128)(4,1)S(1)}, u32[]{:S(2)}) copy-start(pred[169]{0:T(512)(128)(4,1)S(1)} %compare_and_fusion.3) | copy-start | bytes 511
  9.2 7.3 %copy-start.12 = (pred[4,343]{1,0:T(4,128)(4,1)}, pred[4,343]{1,0:T(4,128)(4,1)S(1)}, u32[]{:S(2)}) copy-start(pred[4,343]{1,0:T(4,128)(4,1)S(1)} %compare_and_fusion.1) | copy-start | bytes 4120
  10.6 19.2 %copy-start.26 = (s32[169,1]{0,1:T(1,128)}, s32[169,1]{0,1:T(1,128)S(1)}, u32[]{:S(2)}) copy-start(s32[169,1]{0,1:T(1,128)S(1)} %compare_select_fusion.4) | copy-start | bytes 2032
  10.7 2.3 copy-start.7
  10.8 9.1 %copy-start.25 = (s32[1372]{0:T(1024)}, s32[1372]{0:T(1024)S(1)}, u32[]{:S(2)}) copy-start(s32[1372]{0:T(1024)S(1)} %fusion.51) | copy-start | bytes 16468
  12.1 4.4 %copy-start.18 = (s32[1024]{0:T(1024)}, s32[1024]{0:T(1024)S(1)}, u32[]{:S(2)}) copy-start(s32[1024]{0:T(1024)S(1)} %pad_clamp_fusion.4) | copy-start | bytes 12292
  12.9 3.6 %copy-start.1 = (bf16[343,343]{1,0:T(8,128)(2,1)S(1)}, bf16[343,343]{1,0:T(8,128)(2,1)}, u32[]{:S(2)}) copy-start(bf16[343,343]{1,0:T(8,128)(2,1)} %param.36) | copy-start | bytes 705898
  16.3 14.9 %copy-start.9 = (f32[768]{0:T(1024)S(1)}, f32[768]{0:T(1024)}, u32[]{:S(2)}) copy-start(f32[768]{0:T(1024)} %param.34) | copy-start | bytes 9220
  16.5 22.1 %copy-start.2 = (f32[768,128]{1,0:T(8,128)S(1)}, f32[768,128]{1,0:T(8,128)}, u32[]{:S(2)}) copy-start(f32[768,128]{1,0:T(8,128)} %param.33) | copy-start | bytes 1179652
  31.1 5.8 %collective-permute-start.1 = (f32[169,128]{1,0:T(8,128)S(1)}, f32[169,128]{1,0:T(8,128)S(1)}, u32[]{:S(2)}, u32[]{:S(2)}) collective-permute-start(f32[169,128]{1,0:T(8,128)S(1)} %scatter_custom_fusion.1), channel_id=1, source_target_pairs={{0,1},{1,2},{2,3},{3,4},{4,5},{5,6},{6,7},{7,0},{8,9},{9,10},{10,1... | collective-permute-start | bytes 259592 | tf_op jit(solution)/shard_map/ppermute | solution.py:18
  38.6 4.2 %copy-start.3 = (f32[768,128]{1,0:T(8,128)}, f32[768,128]{1,0:T(8,128)S(1)}, u32[]{:S(2)}) copy-start(f32[768,128]{1,0:T(8,128)S(1)} %scatter-add.85) | copy-start | bytes 1179652
  39.5 1.8 collective-permute-start.2
  48.1 17.6 %copy-start.28 = (s32[1,81]{1,0:T(1,128)S(1)}, s32[1,81]{1,0:T(1,128)}, u32[]{:S(2)}) copy-start(s32[1,81]{1,0:T(1,128)} %param.41) | copy-start | bytes 976
  49.9 24.1 %copy-start.4 = (f32[768,128]{1,0:T(8,128)S(1)}, f32[768,128]{1,0:T(8,128)}, u32[]{:S(2)}) copy-start(f32[768,128]{1,0:T(8,128)} %copy-done.3) | copy-start | bytes 1179652
  49.9 24.1 %copy-start.10 = (f32[768]{0:T(1024)S(1)}, f32[768]{0:T(1024)}, u32[]{:S(2)}) copy-start(f32[768]{0:T(1024)} %param.34) | copy-start | bytes 9220
  49.9 24.1 %copy-start.14 = (f32[768]{0:T(1024)S(1)}, f32[768]{0:T(1024)}, u32[]{:S(2)}) copy-start(f32[768]{0:T(1024)} %broadcast_multiply_fusion.2) | copy-start | bytes 9220
  52.3 23.4 %copy-start.30 = (s32[1,8]{1,0:T(1,128)S(1)}, s32[1,8]{1,0:T(1,128)}, u32[]{:S(2)}) copy-start(s32[1,8]{1,0:T(1,128)} %param.43) | copy-start | bytes 100
  52.4 23.9 %copy-start.11 = (s32[2,729]{1,0:T(2,128)S(1)}, s32[2,729]{1,0:T(2,128)}, u32[]{:S(2)}) copy-start(s32[2,729]{1,0:T(2,128)} %param.40) | copy-start | bytes 17500
  52.4 24.0 %copy-start.17 = (s32[2,729]{1,0:T(2,128)S(1)}, s32[2,729]{1,0:T(2,128)}, u32[]{:S(2)}) copy-start(s32[2,729]{1,0:T(2,128)} %compare_select_fusion.2) | copy-start | bytes 17500
  54.4 24.6 %copy-start.8 = (s32[2048]{0:T(1024)S(1)}, s32[2048]{0:T(1024)}, u32[]{:S(2)}) copy-start(s32[2048]{0:T(1024)} %copy-done.7) | copy-start | bytes 24580
  65.7 5.8 %collective-permute-start.3 = (f32[169,128]{1,0:T(8,128)S(1)}, f32[169,128]{1,0:T(8,128)S(1)}, u32[]{:S(2)}, u32[]{:S(2)}) collective-permute-start(f32[169,128]{1,0:T(8,128)S(1)} %scatter_custom_fusion.3), channel_id=1, source_target_pairs={{0,1},{1,2},{2,3},{3,4},{4,5},{5,6},{6,7},{7,0},{8,9},{9,10},{10,1... | collective-permute-start | bytes 259592 | tf_op jit(solution)/shard_map/ppermute | solution.py:18
  75.3 2.1 collective-permute-start.4
  78.3 5.8 %copy-start.13 = (pred[4,343]{1,0:T(4,128)(4,1)S(1)}, pred[4,343]{1,0:T(4,128)(4,1)}, u32[]{:S(2)}) copy-start(pred[4,343]{1,0:T(4,128)(4,1)} %copy-done.12) | copy-start | bytes 4120
  98.8 5.8 %collective-permute-start.5 = (f32[169,128]{1,0:T(8,128)S(1)}, f32[169,128]{1,0:T(8,128)S(1)}, u32[]{:S(2)}, u32[]{:S(2)}) collective-permute-start(f32[169,128]{1,0:T(8,128)S(1)} %scatter_custom_fusion.5), channel_id=1, source_target_pairs={{0,1},{1,2},{2,3},{3,4},{4,5},{5,6},{6,7},{7,0},{8,9},{9,10},{10,1... | collective-permute-start | bytes 259592 | tf_op jit(solution)/shard_map/ppermute | solution.py:18
  121.1 8.8 %all-to-all-start = ((f32[8,1,96]{2,1,0:T(1,128)}), f32[8,1,96]{2,1,0:T(1,128)S(1)}, u32[]{:S(2)}, u32[]{:S(2)}) async-start(f32[8,1,96]{2,1,0:T(1,128)} %bitcast.12), calls=%async_computation | async-start | bytes 8192 | tf_op jit(solution)/shard_map/all_to_all | solution.py:87
  131.1 1.3 collective-permute-start.8
  140.0 19.0 %copy-start.21 = (f32[768]{0:T(1024)S(1)}, f32[768]{0:T(1024)}, u32[]{:S(2)}) copy-start(f32[768]{0:T(1024)} %param.42) | copy-start | bytes 9220
  140.0 21.8 %copy-start.29 = (s32[1,81]{1,0:T(1,128)S(1)}, s32[1,81]{1,0:T(1,128)}, u32[]{:S(2)}) copy-start(s32[1,81]{1,0:T(1,128)} %param.41) | copy-start | bytes 976
  154.2 4.8 %collective-permute-start.9 = (f32[81]{0:T(128)S(1)}, f32[81]{0:T(128)S(1)}, u32[]{:S(2)}, u32[]{:S(2)}) collective-permute-start(f32[81]{0:T(128)S(1)} %scatter_custom_fusion.10), channel_id=1, source_target_pairs={{0,1},{1,2},{2,3},{3,4},{4,5},{5,6},{6,7},{7,0},{8,9},{9,10},{10,1... | collective-permute-start | bytes 980 | tf_op jit(solution)/shard_map/ppermute | solution.py:18
  159.0 1.6 collective-permute-start.10
  167.5 14.3 %copy-start.31 = (s32[1,8]{1,0:T(1,128)S(1)}, s32[1,8]{1,0:T(1,128)}, u32[]{:S(2)}) copy-start(s32[1,8]{1,0:T(1,128)} %param.43) | copy-start | bytes 100
  167.6 23.0 %copy-start.27 = (s32[8]{0:T(128)S(1)}, s32[8]{0:T(128)}, u32[]{:S(2)}) copy-start(s32[8]{0:T(128)} %fusion.60) | copy-start | bytes 100
  167.6 29.2 %copy-start.19 = (s32[1024]{0:T(1024)S(1)}, s32[1024]{0:T(1024)}, u32[]{:S(2)}) copy-start(s32[1024]{0:T(1024)} %copy-done.18) | copy-start | bytes 12292
  167.6 29.9 %copy-start.24 = (pred[169]{0:T(512)(128)(4,1)S(1)}, pred[169]{0:T(512)(128)(4,1)}, u32[]{:S(2)}) copy-start(pred[169]{0:T(512)(128)(4,1)} %copy-done.23) | copy-start | bytes 511
  181.7 4.8 %collective-permute-start.11 = (f32[81]{0:T(128)S(1)}, f32[81]{0:T(128)S(1)}, u32[]{:S(2)}, u32[]{:S(2)}) collective-permute-start(f32[81]{0:T(128)S(1)} %scatter_custom_fusion.12), channel_id=1, source_target_pairs={{0,1},{1,2},{2,3},{3,4},{4,5},{5,6},{6,7},{7,0},{8,9},{9,10},{10,1... | collective-permute-start | bytes 980 | tf_op jit(solution)/shard_map/ppermute | solution.py:18
  187.3 8.8 %all-to-all-start.1 = ((f32[8,1,96]{2,1,0:T(1,128)}), f32[8,1,96]{2,1,0:T(1,128)S(1)}, u32[]{:S(2)}, u32[]{:S(2)}) async-start(f32[8,1,96]{2,1,0:T(1,128)} %all_to_all.16), calls=%async_computation.1 | async-start | bytes 8192 | tf_op jit(solution)/shard_map/all_to_all | solution.py:87
  190.6 6.1 %collective-permute-start.6 = (bf16[169,128]{1,0:T(8,128)(2,1)S(1)}, bf16[169,128]{1,0:T(8,128)(2,1)S(1)}, u32[]{:S(2)}, u32[]{:S(2)}) collective-permute-start(bf16[169,128]{1,0:T(8,128)(2,1)S(1)} %slice.263), channel_id=1, source_target_pairs={{0,7},{1,0},{2,1},{3,2},{4,3},{5,4},{6,5},{7,6},{8,15},{9,8},{10,9... | collective-permute-start | bytes 129800 | tf_op jit(solution)/shard_map/ppermute | solution.py:18
  196.7 20.4 %copy-start.22 = (f32[768]{0:T(1024)}, f32[768]{0:T(1024)S(1)}, u32[]{:S(2)}) copy-start(f32[768]{0:T(1024)S(1)} %select_n.110) | copy-start | bytes 9220
  215.4 1.7 copy-start.5
  217.2 6.0 %collective-permute-start.7 = (f32[169,128]{1,0:T(8,128)}, f32[169,128]{1,0:T(8,128)S(1)}, u32[]{:S(2)}, u32[]{:S(2)}) collective-permute-start(f32[169,128]{1,0:T(8,128)} %scatter_custom_fusion.7), channel_id=1, source_target_pairs={{0,1},{1,2},{2,3},{3,4},{4,5},{5,6},{6,7},{7,0},{8,9},{9,10},{10,1... | collective-permute-start | bytes 259592 | tf_op jit(solution)/shard_map/ppermute | solution.py:18
  217.8 10.4 %copy-start.15 = (f32[768]{0:T(1024)}, f32[768]{0:T(1024)S(1)}, u32[]{:S(2)}) copy-start(f32[768]{0:T(1024)S(1)} %get-tuple-element.91) | copy-start | bytes 9220
  224.9 0.7 copy-start.6
  225.6 1.7 collective-permute-start.12
  235.4 24.0 %copy-start.16 = (f32[768]{0:T(1024)S(1)}, f32[768]{0:T(1024)}, u32[]{:S(2)}) copy-start(f32[768]{0:T(1024)} %copy-done.15) | copy-start | bytes 9220
  235.4 24.0 %copy-start.20 = (f32[768]{0:T(1024)S(1)}, f32[768]{0:T(1024)}, u32[]{:S(2)}) copy-start(f32[768]{0:T(1024)} %get-tuple-element.90) | copy-start | bytes 9220
  251.0 5.8 %collective-permute-start.13 = (f32[169,128]{1,0:T(8,128)S(1)}, f32[169,128]{1,0:T(8,128)S(1)}, u32[]{:S(2)}, u32[]{:S(2)}) collective-permute-start(f32[169,128]{1,0:T(8,128)S(1)} %scatter_custom_fusion.14), channel_id=1, source_target_pairs={{0,1},{1,2},{2,3},{3,4},{4,5},{5,6},{6,7},{7,0},{8,9},{9,10},{10,1... | collective-permute-start | bytes 259592 | tf_op jit(solution)/shard_map/ppermute | solution.py:18
where the time goes:
time: 263 us; the launch traced here: 261 us
  other arithmetic  95.7 us (36%)
  local copies, waits for them, and re-layouts  82.8 us (31%)
  waiting for transfers between devices  40.3 us (15%)
  starting transfers between devices  17.3 us (7%)
  matrix products  13.9 us (5%)
  blocking collectives  9.88 us (4%)
    scatter-add x5, other arithmetic, cell_terms(): return jnp.zeros(local_rows.shape, jnp.float32).at[node_ids.reshape(-1)]....  48.8 us
    ppermute x14, waiting for transfers between devices, from_behind(): lax.ppermute(array, axis, [(i, (i + by) % length) for i in range(length)])  33 us
    gather x10, local copies, waits for them, and re-layouts, cell_terms(): cell_vals = jnp.take(local_rows, node_ids, axis=0)  26.1 us
    scatter-add x2, other arithmetic, field_terms(): jnp.zeros(local_rows.shape, jnp.float32).at[node_ids.reshape(-1)]  22.1 us
    gather x4, local copies, waits for them, and re-layouts, field_terms(): cell_vals = jnp.take(local_rows, node_ids, axis=0)  11.5 us
    ppermute x14, starting transfers between devices, from_behind(): lax.ppermute(array, axis, [(i, (i + by) % length) for i in range(length)])  10.7 us
    reshape x5, local copies, waits for them, and re-layouts, cell_terms(): product.reshape(-1, columns)  10.1 us
    psum x1, blocking collectives, band_total(): return lax.psum(values, 'band')  9.88 us
  transfers between devices with their start and end apart: 16, of which 14 were waited for; matrix products, arithmetic and copies ran while one was open for 7% of the time, Pallas kernels for 0%

commit v1 on v0

v1 whole, which is shorter than its diff:
```python
import functools

import jax
import jax.numpy as jnp
from jax import lax
from jax.experimental import pallas as pl
from jax.experimental.pallas import tpu as pltpu
from jax.sharding import PartitionSpec as P

filter_center = 1.8
filter_half = 2.7
solve_center = 3.25
solve_half = 2.75
solve_ratio = solve_center / solve_half
weight_zero = 1.0 / solve_ratio
weight_one = 1.0 / (2.0 * solve_ratio - weight_zero)
weight_two = 1.0 / (2.0 * solve_ratio - weight_one)

BF = jnp.bfloat16
F32 = jnp.float32
I32 = jnp.int32
LANES = 128
SUBLANES = 8


def up_to(n, m):
    return -(-n // m) * m


def from_behind(array, axis, by):
    length = lax.axis_size(axis)
    return lax.ppermute(array, axis, [(i, (i + by) % length) for i in range(length)])


class Window:
    def __init__(self, start, npc, own, nloc):
        end = start + npc
        self.lo = start // 16 * 16
        self.hi = min(up_to(min(end, own), 16), own)
        self.touches = end > own
        self.low = up_to(max(0, end - nloc), 16)
        self.rows = self.hi - self.lo + self.low


class Geometry:
    def __init__(self, own, share, cells, npc):
        self.own, self.share, self.cells, self.npc = own, share, cells, npc
        nloc = own + share
        stride = nloc // cells
        self.sp = up_to(share, 16)
        self.npl = up_to(npc, LANES)
        self.windows = [Window(c * stride, npc, own, nloc) for c in range(cells)]
        self.touching = [c for c in range(cells) if self.windows[c].touches]
        self.dn_lo = min(self.windows[c].lo for c in self.touching)
        self.low = max(w.low for w in self.windows)
        self.dn_rows = own - self.dn_lo + self.low


def dot(a, b):
    return lax.dot_general(a, b, (((1,), (0,)), ((), ())), preferred_element_type=F32)


def dot_t(a, b):
    return lax.dot_general(a, b, (((1,), (1,)), ((), ())), preferred_element_type=F32)


def vmem_call(kernel, out_shape, scratch=(), in_specs=None, cost=None):
    kwargs = {}
    if in_specs is not None:
        kwargs["in_specs"] = in_specs
    return pl.pallas_call(
        kernel,
        out_shape=out_shape,
        scratch_shapes=list(scratch),
        cost_estimate=cost,
        compiler_params=pltpu.CompilerParams(vmem_limit_bytes=56 * 1024 * 1024),
        **kwargs,
    )


def sds(shape, dtype):
    return jax.ShapeDtypeStruct(shape, dtype)


def one_hot_rows(count, first, nodes):
    ids = lax.broadcasted_iota(I32, (count, nodes.shape[1]), 0) + first
    return jnp.where(ids == nodes, 1.0, 0.0).astype(BF)


def place_tables(geo, nodes_ref, face_ref, matrix_ref, nodes_pad, face_pad, matrix_pad):
    nodes_pad[...] = jnp.full(nodes_pad.shape, -1, I32)
    nodes_pad[0 : geo.cells, 0 : geo.npc] = nodes_ref[...]
    face_pad[...] = jnp.full(face_pad.shape, -1, I32)
    face_pad[0:1, 0 : geo.share] = face_ref[...]
    matrix_pad[...] = jnp.zeros(matrix_pad.shape, F32)
    matrix_pad[0 : geo.npc, 0 : geo.npc] = matrix_ref[...].astype(F32)


def table_scratch(geo):
    return [
        pltpu.VMEM((up_to(geo.cells, SUBLANES), geo.npl), I32),
        pltpu.VMEM((SUBLANES, up_to(geo.share, LANES)), I32),
        pltpu.VMEM((geo.npl, geo.npl), F32),
    ]


def owned_picks(geo, c, nodes):
    w = geo.windows[c]
    picks = one_hot_rows(w.hi - w.lo, w.lo, nodes)
    if w.low:
        picks = jnp.concatenate([picks, one_hot_rows(w.low, 0, nodes)], axis=0)
    return picks


def upper_picks(geo, nodes, face):
    by_local = one_hot_rows(face.shape[1], geo.own, nodes)
    by_owner = one_hot_rows(geo.sp, 0, face)
    return dot(by_owner, by_local).astype(BF)


def own_matrices_kernel(geo, *refs):
    nodes_ref, face_ref, matrix_ref, pot_ref = refs[:4]
    outs = refs[4:-3]
    nodes_pad, face_pad, matrix_pad = refs[-3:]
    place_tables(geo, nodes_ref, face_ref, matrix_ref, nodes_pad, face_pad, matrix_pad)
    matrix = matrix_pad[...].astype(BF)
    face = face_pad[0:1, :]
    for c in range(geo.cells):
        nodes = nodes_pad[c : c + 1, :]
        own = owned_picks(geo, c, nodes)
        left = dot(own, matrix).astype(BF)
        outs[c][...] = dot_t(left, own).astype(BF)
        if c in geo.touching:
            at = geo.cells + geo.touching.index(c)
            outs[at][...] = dot_t(left, upper_picks(geo, nodes, face)).astype(BF)
    column = outs[-1]
    for r in range(geo.own // LANES):
        row = jnp.broadcast_to(pot_ref[r : r + 1, :], (LANES, LANES))
        column[r * LANES : (r + 1) * LANES, :] = row.T


def own_matrices(geo, cell_nodes, face_order, cell_matrix, potential):
    shapes = [sds((w.rows, w.rows), BF) for w in geo.windows]
    shapes += [sds((geo.windows[c].rows, geo.sp), BF) for c in geo.touching]
    shapes += [sds((geo.own, LANES), F32)]
    outs = vmem_call(
        functools.partial(own_matrices_kernel, geo), shapes, table_scratch(geo), cost=cost_of(3.0)
    )(cell_nodes, face_order, cell_matrix, potential.reshape(geo.own // LANES, LANES))
    n = geo.cells
    return outs[:n], outs[n:-1], outs[-1]


def behind_matrices_kernel(geo, *refs):
    nodes_ref, face_ref, matrix_ref = refs[:3]
    outs = refs[3:-3]
    nodes_pad, face_pad, matrix_pad = refs[-3:]
    place_tables(geo, nodes_ref, face_ref, matrix_ref, nodes_pad, face_pad, matrix_pad)
    matrix = matrix_pad[...].astype(BF)
    face = face_pad[0:1, :]
    count = len(geo.touching)
    for at, c in enumerate(geo.touching):
        nodes = nodes_pad[c : c + 1, :]
        upper = upper_picks(geo, nodes, face)
        left = dot(upper, matrix).astype(BF)
        outs[at][...] = dot_t(left, owned_picks(geo, c, nodes)).astype(BF)
        outs[count + at][...] = dot_t(left, upper).astype(BF)


def behind_matrices(geo, nodes, face, cell_matrix):
    shapes = [sds((geo.sp, geo.windows[c].rows), BF) for c in geo.touching]
    shapes += [sds((geo.sp, geo.sp), BF) for _ in geo.touching]
    outs = vmem_call(
        functools.partial(behind_matrices_kernel, geo), shapes, table_scratch(geo), cost=cost_of(1.5)
    )(nodes, face, cell_matrix)
    n = len(geo.touching)
    return outs[:n], outs[n:]


def cost_of(us):
    return pl.CostEstimate(flops=0, bytes_accessed=int(us * 3.0e6), transcendentals=0)


def write_sends(geo, y_ref, dn_ref, up_ref):
    top = geo.own - geo.dn_lo
    dn_ref[0:top, :] = y_ref[geo.dn_lo : geo.own, :].astype(BF)
    dn_ref[top : top + geo.low, :] = y_ref[0 : geo.low, :].astype(BF)
    up_ref[...] = y_ref[0 : geo.sp, :].astype(BF)


def send_shapes(geo, columns):
    return [sds((geo.dn_rows, columns), BF), sds((geo.sp, columns), BF)]


def pack_kernel(geo, y_ref, dn_ref, up_ref):
    write_sends(geo, y_ref, dn_ref, up_ref)


def pack(geo, y):
    return vmem_call(
        functools.partial(pack_kernel, geo), send_shapes(geo, y.shape[1]), cost=cost_of(0.5)
    )(y)


def owned_part_kernel(geo, scale, has_prev, has_field, has_upper, *refs):
    refs = list(refs)
    base_ref = refs.pop()
    y_ref = refs.pop(0)
    prev_ref = refs.pop(0) if has_prev else None
    pot_ref = refs.pop(0)
    field_ref = refs.pop(0) if has_field else None
    mats = [refs.pop(0) for _ in range(geo.cells)]
    y = y_ref[...]
    factor = pot_ref[...]
    if has_field:
        factor = factor + field_ref[...]
    value = ((factor - filter_center) * scale) * y
    if has_prev:
        value = value - prev_ref[...]
    base_ref[...] = value
    x = y.astype(BF)
    for c in range(geo.cells):
        w = geo.windows[c]
        own = w.hi - w.lo
        rows = x[w.lo : w.hi, :]
        if w.low:
            rows = jnp.concatenate([rows, x[0 : w.low, :]], axis=0)
        product = dot(mats[c][...], rows) * scale
        base_ref[w.lo : w.hi, :] += product[:own]
        if w.low:
            base_ref[0 : w.low, :] += product[own:]
    if has_upper:
        for upper in refs:
            base_ref[0 : geo.sp, :] += dot(upper[...], x[0 : geo.sp, :]) * scale


def owned_part(geo, scale, y, prev, pot, field, mats, uppers):
    args = [y] + ([prev] if prev is not None else []) + [pot]
    args += [field] if field is not None else []
    args += list(mats) + list(uppers)
    return vmem_call(
        functools.partial(
            owned_part_kernel, geo, scale, prev is not None, field is not None, bool(uppers)
        ),
        sds(y.shape, F32),
        cost=cost_of(2.0),
    )(*args)


def add_halo(geo, scale, y_ref, up_ref, dn_ref, crosses, behinds, uppers, own_up_ref):
    h_up = up_ref[...]
    h_dn = dn_ref[...]
    for at, c in enumerate(geo.touching):
        w = geo.windows[c]
        own = w.hi - w.lo
        product = dot(crosses[at][...], h_up) * scale
        y_ref[w.lo : w.hi, :] += product[:own]
        if w.low:
            y_ref[0 : w.low, :] += product[own:]
    total = None
    for at, c in enumerate(geo.touching):
        w = geo.windows[c]
        first = w.lo - geo.dn_lo
        term = dot(behinds[at][...], h_dn[first : first + w.rows, :])
        total = term if total is None else total + term
        if uppers:
            total = total + dot(uppers[at][...], own_up_ref[...])
    y_ref[0 : geo.sp, :] += total * scale


def write_density(y_ref, occ_ref, dens_ref, row_pad):
    parts, blocks, _ = dens_ref.shape
    own = y_ref.shape[0]
    length = own // blocks
    y = y_ref[...]
    terms = y * y * occ_ref[...]
    high = terms.astype(BF)
    low = (terms - high.astype(F32)).astype(BF)
    ones = jnp.ones((SUBLANES, terms.shape[1]), BF)
    summed = dot_t(ones, high) + dot_t(ones, low)
    row_pad[...] = jnp.zeros(row_pad.shape, F32)
    for j in range(blocks):
        row_pad[j : j + 1, 0:length] = summed[0:1, j * length : (j + 1) * length]
    dens_ref[...] = jnp.broadcast_to(row_pad[...][None], dens_ref.shape)


def finish_kernel(geo, scale, has_upper, mode, *refs):
    refs = list(refs)
    n = len(geo.touching)
    base_ref, up_ref, dn_ref = refs[:3]
    refs = refs[3:]
    crosses, refs = refs[:n], refs[n:]
    behinds, refs = refs[:n], refs[n:]
    uppers, own_up = [], None
    if has_upper:
        uppers, refs = refs[:n], refs[n:]
        own_up = refs.pop(0)
    occ_ref = refs.pop(0) if mode == "density" else None
    y_ref = refs.pop(0)
    y_ref[...] = base_ref[...]
    add_halo(geo, scale, y_ref, up_ref, dn_ref, crosses, behinds, uppers, own_up)
    if mode != "last":
        write_sends(geo, y_ref, refs[0], refs[1])
    if mode == "density":
        write_density(y_ref, occ_ref, refs[2], refs[3])


def finish(geo, scale, base, halo, crosses, behinds, uppers=(), own_up=None, occ=None, parts=None, last=False):
    columns = base.shape[1]
    args = [base, halo[0], halo[1], *crosses, *behinds, *uppers]
    if uppers:
        args.append(own_up)
    shapes = [sds(base.shape, F32)]
    scratch = []
    mode = "plain"
    if last:
        mode = "last"
    else:
        shapes += send_shapes(geo, columns)
    if occ is not None:
        mode = "density"
        args.append(occ)
        shapes.append(sds(parts, F32))
        scratch.append(pltpu.VMEM(parts[1:], F32))
    return vmem_call(
        functools.partial(finish_kernel, geo, scale, bool(uppers), mode),
        shapes,
        scratch,
        cost=cost_of(1.0),
    )(*args)


class FieldGeometry:
    def __init__(self, domains, own, share, cells, npc):
        self.domains, self.own, self.share, self.cells, self.npc = domains, own, share, cells, npc
        self.block = own // domains
        self.rows = up_to(npc, LANES) // LANES
        self.blocks = domains + 1
        self.at_inverse = cells * self.rows
        self.at_face = self.at_inverse + cells * self.blocks
        self.at_face_inverse = self.at_face + 1
        self.at_owner = self.at_face + 2
        self.at_screen = self.at_face + 3
        self.table_rows = up_to(self.at_screen + domains, SUBLANES)
        self.fits = (
            domains == SUBLANES
            and own % domains == 0
            and share <= self.block <= LANES
        )


def column_of(row):
    return jnp.broadcast_to(row, (LANES, LANES)).T


def field_tables_kernel(fg, nodes_ref, face_ref, owner_ref, screen_ref, matrix_ref, table_ref, high_ref, low_ref, pad, one, wide):
    lane = lax.broadcasted_iota(I32, (1, LANES), 1)
    one[...] = jnp.full(one.shape, -1.0, F32)
    pad[...] = jnp.full(pad.shape, -1, I32)
    pad[0 : fg.cells, 0 : fg.npc] = nodes_ref[...]
    sub = lax.broadcasted_iota(I32, (LANES, LANES), 0)
    wide_lane = lax.broadcasted_iota(I32, (LANES, LANES), 1)
    for c in range(fg.cells):
        columns = []
        for r in range(fg.rows):
            nodes = pad[c : c + 1, r * LANES : (r + 1) * LANES]
            block = jnp.zeros((1, LANES), I32)
            for b in range(1, fg.blocks):
                block = block + jnp.where(nodes >= b * fg.block, 1, 0)
            code = jnp.where(nodes < 0, -1, nodes + block * (LANES - fg.block))
            code = code.astype(F32)
            at = c * fg.rows + r
            one[at : at + 1, :] = code
            columns.append(column_of(code))
        for b in range(fg.blocks):
            target = (wide_lane + b * LANES).astype(F32)
            found = jnp.zeros((LANES, LANES), F32)
            for r in range(fg.rows):
                position = (sub + (r * LANES + 1)).astype(F32)
                found = found + jnp.where(columns[r] == target, position, 0.0)
            at = fg.at_inverse + c * fg.blocks + b
            one[at : at + 1, :] = jnp.sum(found, axis=0, keepdims=True) - 1.0
    one[fg.at_face : fg.at_face + 1, 0 : fg.share] = face_ref[...].astype(F32)
    column = column_of(one[fg.at_face : fg.at_face + 1, :])
    hits = jnp.where(column == wide_lane.astype(F32), (sub + 1).astype(F32), 0.0)
    one[fg.at_face_inverse : fg.at_face_inverse + 1, :] = jnp.sum(hits, axis=0, keepdims=True) - 1.0
    one[fg.at_owner : fg.at_owner + 1, 0 : fg.domains] = owner_ref[...].astype(F32)
    one[fg.at_screen : fg.at_screen + fg.domains, 0 : fg.block] = screen_ref[...]
    table_ref[...] = jnp.broadcast_to(one[...][None], table_ref.shape)
    wide[...] = jnp.zeros(wide.shape, F32)
    wide[0 : fg.npc, 0 : fg.npc] = matrix_ref[...]
    full = wide[...]
    high = full.astype(BF)
    high_ref[...] = high
    low_ref[...] = (full - high.astype(F32)).astype(BF)


def field_tables(fg, pois_nodes, pois_face, block_owner, screening, pois_matrix):
    size = fg.rows * LANES
    return vmem_call(
        functools.partial(field_tables_kernel, fg),
        [
            sds((fg.domains, fg.table_rows, LANES), F32),
            sds((size, size), BF),
            sds((size, size), BF),
        ],
        [
            pltpu.VMEM((up_to(fg.cells, SUBLANES), size), I32),
            pltpu.VMEM((fg.table_rows, LANES), F32),
            pltpu.VMEM((size, size), F32),
        ],
        cost=cost_of(3.0),
    )(pois_nodes, pois_face, block_owner, screening.reshape(fg.domains, fg.block), pois_matrix)


def lanes_of(values, index):
    return jnp.take_along_axis(values, index, axis=1, mode="promise_in_bounds")


def field_solve(fg, dens_ref, table_ref, high_ref, low_ref, codes, rows):
    domains, cells = fg.domains, fg.cells
    bands = dens_ref.shape[0] // domains
    valid = lax.broadcasted_iota(I32, (domains, LANES), 1) < fg.block

    def table(at):
        return table_ref[:, at, :]

    for at in range(fg.at_owner):
        codes[at] = table(at).astype(I32)
    owner = table(fg.at_owner)
    part = lax.broadcasted_iota(I32, (domains, LANES), 0).astype(F32)
    source = []
    for q in range(domains):
        density = dens_ref[q]
        for b in range(1, bands):
            density = density + dens_ref[b * domains + q]
        placed = jnp.zeros((domains, LANES), F32)
        for j in range(domains):
            who = jnp.broadcast_to(owner[q : q + 1, j : j + 1], (domains, LANES))
            placed = placed + jnp.where(who == part, jnp.broadcast_to(density[j : j + 1, :], (domains, LANES)), 0.0)
        source.append(placed)
    screen = [table(fg.at_screen + q) for q in range(domains)]

    def lookup(sources, code):
        lane = jnp.bitwise_and(code, LANES - 1)
        which = jnp.right_shift(code, 7)
        total = jnp.zeros((domains, LANES), F32)
        for b, values in enumerate(sources):
            total = jnp.where(which == b, lanes_of(values, lane), total)
        return total

    def operator(field):
        ahead = pltpu.roll(field[0], domains - 1, 0)
        face = codes[fg.at_face]
        upper = lookup([ahead], face)
        local = list(field) + [upper]
        for c in range(cells):
            for r in range(fg.rows):
                rows[c * domains : (c + 1) * domains, r * LANES : (r + 1) * LANES] = lookup(local, codes[c * fg.rows + r])
        picked = rows[...]
        high = picked.astype(BF)
        low = (picked - high.astype(F32)).astype(BF)
        product = dot(high, high_ref[...]) + (dot(low, high_ref[...]) + dot(high, low_ref[...]))
        out = []
        for b in range(fg.blocks):
            total = None
            for c in range(cells):
                sources = [
                    product[c * domains : (c + 1) * domains, r * LANES : (r + 1) * LANES]
                    for r in range(fg.rows)
                ]
                term = lookup(sources, codes[fg.at_inverse + c * fg.blocks + b])
                total = term if total is None else total + term
            out.append(total)
        arriving = pltpu.roll(out[domains], 1, 0)
        home = pltpu.roll(codes[fg.at_face_inverse], 1, 0)
        out[0] = out[0] + lookup([arriving], home)
        return [jnp.where(valid, screen[q] * field[q] + out[q], 0.0) for q in range(domains)]

    step_one = [s * (1.0 / solve_center) for s in source]
    applied = operator(step_one)
    residual = [s - a for s, a in zip(source, applied)]
    a1, b1 = weight_one * weight_zero, 2.0 * weight_one / solve_half
    step_two = [a1 * e + b1 * r for e, r in zip(step_one, residual)]
    applied = operator(step_two)
    residual = [r - a for r, a in zip(residual, applied)]
    a2, b2 = weight_two * weight_one, 2.0 * weight_two / solve_half
    step_three = [a2 * e + b2 * r for e, r in zip(step_two, residual)]
    return [(x + y) + z for x, y, z in zip(step_one, step_two, step_three)]


def field_kernel(geo, fg, scale, *refs):
    refs = list(refs)
    n = len(geo.touching)
    dens_ref, table_ref, high_ref, low_ref, owner_ref = refs[:5]
    base_ref, up_ref, dn_ref, y_ref = refs[5:9]
    refs = refs[9:]
    crosses, refs = refs[:n], refs[n:]
    behinds, refs = refs[:n], refs[n:]
    z_ref, dn_out, up_out, column_ref, hartree_ref = refs[:5]
    codes, rows, phi = refs[5:]
    blocks = field_solve(fg, dens_ref, table_ref, high_ref, low_ref, codes, rows)
    for q in range(fg.domains):
        phi[q] = blocks[q]
    here = lax.axis_index("domain")
    for j in range(fg.domains):
        hartree_ref[j : j + 1, :] = phi[here, pl.ds(owner_ref[0, j], 1), :]
    for j in range(fg.domains):
        column = column_of(hartree_ref[j : j + 1, :])
        column_ref[j * fg.block : (j + 1) * fg.block, :] = column[0 : fg.block, :]
    z_ref[...] = base_ref[...] + (column_ref[...] * scale) * y_ref[...]
    add_halo(geo, scale, z_ref, up_ref, dn_ref, crosses, behinds, [], None)
    write_sends(geo, z_ref, dn_out, up_out)


def field_step(geo, fg, scale, dens, table, high, low, block_owner, base, halo, y, crosses, behinds):
    columns = y.shape[1]
    vmem = pl.BlockSpec(memory_space=pltpu.VMEM)
    args = [dens, table, high, low, block_owner, base, halo[0], halo[1], y, *crosses, *behinds]
    specs = [vmem] * len(args)
    specs[4] = pl.BlockSpec(memory_space=pltpu.SMEM)
    return vmem_call(
        functools.partial(field_kernel, geo, fg, scale),
        [sds(y.shape, F32), *send_shapes(geo, columns), sds((geo.own, LANES), F32), sds((fg.domains, LANES), F32)],
        [
            pltpu.VMEM((fg.at_owner, fg.domains, LANES), I32),
            pltpu.VMEM((fg.cells * fg.domains, fg.rows * LANES), F32),
            pltpu.VMEM((fg.domains, fg.domains, LANES), F32),
        ],
        in_specs=specs,
        cost=cost_of(5.0),
    )(*args)


def assembled(owned_rows, face_row, terms):
    owned_count = owned_rows.shape[0]
    shared = face_row.shape[0]
    coming = jnp.take(from_behind(owned_rows[:shared], "domain", -1), face_row, axis=0)
    partial_value = terms(jnp.concatenate([owned_rows, coming], axis=0))
    upper_rows = partial_value[owned_count:]
    ordered = jnp.zeros_like(upper_rows).at[face_row].set(upper_rows)
    arrived = from_behind(ordered, "domain", 1)
    return partial_value[:owned_count].at[:shared].add(arrived)


def field_terms(local_rows, pois_matrix, node_ids):
    cell_vals = jnp.take(local_rows, node_ids, axis=0)
    product = jnp.einsum(
        "pq,cq->cp",
        pois_matrix,
        cell_vals,
        precision=lax.Precision.HIGHEST,
        preferred_element_type=F32,
    )
    return jnp.zeros(local_rows.shape, F32).at[node_ids.reshape(-1)].add(product.reshape(-1))


def reshuffle(blocks):
    return lax.all_to_all(blocks, "domain", split_axis=0, concat_axis=0, tiled=True)


def distributed_field(y, occupation, owner_row, pois_matrix, pois_nodes, field_face, screening):
    owned_count = y.shape[0]
    domains = lax.axis_size("domain")
    block_len = owned_count // domains
    partial_value = jnp.dot(
        y * y, occupation, precision=lax.Precision.HIGHEST, preferred_element_type=F32
    )
    summed = lax.psum(partial_value, "band")
    arranged = (
        jnp.zeros((domains, block_len), F32)
        .at[owner_row]
        .set(summed.reshape(domains, block_len))
    )
    source = reshuffle(arranged).reshape(owned_count)

    def field_operator(vector):
        return (
            assembled(
                vector, field_face, lambda local: field_terms(local, pois_matrix, pois_nodes)
            )
            + screening * vector
        )

    step_one = source / solve_center
    residual = source - field_operator(step_one)
    step_two = weight_one * weight_zero * step_one + 2.0 * weight_one / solve_half * residual
    residual = residual - field_operator(step_two)
    step_three = weight_two * weight_one * step_two + 2.0 * weight_two / solve_half * residual
    solved = step_one + step_two + step_three
    returned = reshuffle(solved.reshape(domains, block_len))
    return jnp.take(returned, owner_row, axis=0).reshape(owned_count)


def exchange(sends):
    dn, up = sends
    h_dn = from_behind(dn, "domain", 1)
    h_up = from_behind(up, "domain", -1)
    return h_up, h_dn


def per_device(
    orbitals,
    potential,
    occupation,
    cell_matrix,
    cell_nodes,
    face_order,
    pois_matrix,
    pois_nodes,
    pois_face,
    screening,
    block_owner,
):
    domains = lax.axis_size("domain")
    bands = lax.axis_size("band")
    own, columns = orbitals.shape
    geo = Geometry(own, face_order.shape[1], cell_nodes.shape[0], cell_nodes.shape[1])
    fg = FieldGeometry(domains, own, pois_face.shape[1], pois_nodes.shape[0], pois_nodes.shape[1])
    first, later = 1.0 / filter_half, 2.0 / filter_half

    sends = pack(geo, orbitals)
    halo = exchange(sends)
    behind_nodes = from_behind(cell_nodes, "domain", 1)
    behind_face = from_behind(face_order, "domain", 1)
    mats, crosses, pot = own_matrices(geo, cell_nodes, face_order, cell_matrix, potential)
    if fg.fits:
        table, high, low = field_tables(fg, pois_nodes, pois_face, block_owner, screening, pois_matrix)
        tables = lax.all_to_all(table, "domain", 0, 0, tiled=True)

    base = owned_part(geo, first, orbitals, None, pot, None, mats, ())
    behinds, uppers = behind_matrices(geo, behind_nodes, behind_face, cell_matrix)
    y1, *sends1 = finish(geo, first, base, halo, crosses, behinds, uppers, sends[1])

    halo = exchange(sends1)
    base = owned_part(geo, later, y1, orbitals, pot, None, mats, uppers)
    y2, *sends2 = finish(geo, later, base, halo, crosses, behinds)

    halo = exchange(sends2)
    base = owned_part(geo, later, y2, y1, pot, None, mats, uppers)
    if fg.fits:
        parts = (domains * bands, domains, LANES)
        y3, dn, up, spread = finish(
            geo, later, base, halo, crosses, behinds, occ=occupation.reshape(1, columns), parts=parts
        )
        dens = lax.all_to_all(spread, ("band", "domain"), 0, 0, tiled=True)
        halo = exchange((dn, up))
        base = owned_part(geo, first, y3, None, pot, None, mats, uppers)
        z1, dn, up, column, packed = field_step(
            geo, fg, first, dens, tables, high, low, block_owner, base, halo, y3, crosses, behinds
        )
        hartree = packed[:, : fg.block].reshape(own)
        sends4 = (dn, up)
    else:
        y3, *sends3 = finish(geo, later, base, halo, crosses, behinds)
        halo = exchange(sends3)
        hartree = distributed_field(
            y3, occupation, block_owner[0], pois_matrix, pois_nodes, pois_face[0], screening
        )
        column = jnp.broadcast_to(hartree[:, None], (own, LANES))
        base = owned_part(geo, first, y3, None, pot, column, mats, uppers)
        z1, *sends4 = finish(geo, first, base, halo, crosses, behinds)

    halo = exchange(sends4)
    base = owned_part(geo, later, z1, y3, pot, column, mats, uppers)
    (filtered,) = finish(geo, later, base, halo, crosses, behinds, last=True)
    return filtered, hartree


def solution(mesh):
    return jax.shard_map(
        per_device,
        mesh=mesh,
        in_specs=(
            P("domain", "band"),
            P("domain"),
            P("band"),
            P(),
            P("domain", None),
            P("domain", None),
            P(),
            P("domain", None),
            P("domain", None),
            P("domain"),
            P("domain", None),
        ),
        out_specs=(P("domain", "band"), P("domain")),
        check_vma=False,
    )
```

time: 263 us -> 83.4 us (0.32)
  other arithmetic: 95.7 us -> 0 us
  local copies, waits for them, and re-layouts: 82.8 us -> 8.35 us
  Pallas kernels: 0 us -> 42 us
  waiting for transfers between devices: 40.3 us -> 2.5 us
  matrix products: 13.9 us -> 0 us
  starting transfers between devices: 17.3 us -> 29.1 us
  blocking collectives: 9.88 us -> 0 us
    scatter-add x9 -> x0, other arithmetic: 70.9 us -> none  [the longest x5 48.8 us: cell_terms(): return jnp.zeros(local_rows.shape, jnp.float32).at[node_ids.reshape(-1)]....]
    gather x22 -> x0, local copies, waits for them, and re-layouts: 45.2 us -> none  [the longest x10 26.1 us: cell_terms(): cell_vals = jnp.take(local_rows, node_ids, axis=0)]
    pallas_call x0 -> x14, Pallas kernels: none -> 42 us  [the longest x5 13.6 us: owned_part(): vmem_call(functools.partial(owned_part_kernel, geo, scale, prev is not No...]
    ppermute x14 -> x12, waiting for transfers between devices: 33 us -> 2.5 us  [from_behind(): lax.ppermute(array, axis, [(i, (i + by) % length) for i in range(length)])]
    dot_general x8 -> x0, matrix products: 13.9 us -> none  [the longest x5 8.98 us: cell_terms(): jnp.einsum('pq,cqm->cpm', cell_matrix, cell_vals, preferred_element_type=...]
    scatter x8 -> x0, local copies, waits for them, and re-layouts: 10.2 us -> none  [the longest x7 8.96 us: fold_back(): ordered = jnp.zeros_like(upper_rows).at[face_row].set(upper_rows)]
    psum x1 -> x0, blocking collectives: 9.88 us -> none  [band_total(): return lax.psum(values, 'band')]
    reshape x11 -> x2, local copies, waits for them, and re-layouts: 11.4 us -> 2.7 us  [the longest x1 1.35 us: field_tables(): screening.reshape(fg.domains, fg.block)]
  transfers between devices with their start and end apart: 16 -> 14, of which waited for: 14 -> 2; matrix products, arithmetic and copies ran while one was open for 7% -> 2% of each run, Pallas kernels for 0% -> 35%
where the time goes in v1:
time: 83.4 us; the launch traced here: 82.7 us
  Pallas kernels  42 us (50%)
  starting transfers between devices  29.1 us (35%)
  local copies, waits for them, and re-layouts  8.35 us (10%)
  waiting for transfers between devices  2.5 us (3%)
    ppermute x12, starting transfers between devices, from_behind(): lax.ppermute(array, axis, [(i, (i + by) % length) for i in range(length)])  18.1 us
    pallas_call x5, Pallas kernels, owned_part(): vmem_call(functools.partial(owned_part_kernel, geo, scale, prev is not No...  13.6 us
    pallas_call x4, Pallas kernels, finish(): vmem_call(functools.partial(finish_kernel, geo, scale, bool(uppers), mode...  9.65 us
    all_to_all x1, starting transfers between devices, per_device(): tables = lax.all_to_all(table, 'domain', 0, 0, tiled=True)  6.35 us
    pallas_call x1, Pallas kernels, field_step(): vmem_call(functools.partial(field_kernel, geo, fg, scale), [sds(y.shape,...  6.25 us
    unnamed x32, local copies, waits for them, and re-layouts  5.65 us
    all_to_all x1, starting transfers between devices, per_device(): dens = lax.all_to_all(spread, ('band', 'domain'), 0, 0, tiled=True)  4.68 us
    pallas_call x1, Pallas kernels, field_tables(): vmem_call(functools.partial(field_tables_kernel, fg), [sds((fg.domains, f...  4.4 us
  transfers between devices with their start and end apart: 14, of which 2 were waited for; matrix products, arithmetic and copies ran while one was open for 2% of the time, Pallas kernels for 35%

profile of v1, /device:TPU:0, one launch (start us, length us, event | category | flops | bytes accessed | tf_op | source)
XLA Modules:
  0.0 82.7 jit_solution(6992155342132807122)
XLA Ops:
  0.6 1.4 %reshape.18.screen_ref = f32[8,96]{1,0:T(8,128)} reshape(f32[768]{0:T(1024)} %param.20) | data formatting | bytes 6144 | tf_op jit(solution)/shard_map/reshape | solution.py:412
  2.0 4.4 %shard_map.131 = (f32[8,48,128]{2,1,0:T(8,128)}, bf16[768,768]{1,0:T(8,128)(2,1)}, bf16[768,768]{1,0:T(8,128)(2,1)}) custom-call(s32[2,729]{1,0:T(2,128)} %nodes_ref.1, s32[1,81]{1,0:T(1,128)} %face_ref.1, s32[1,8]{1,0:T(1,128)} %refs_4_.1, f32[8,96]{1,0:T(8,128)} %reshape.18.screen_ref, f32[729,729]{1,0:T(8,128)} %matrix_ref.1), custom_call_target="tpu_custom_call" | custom-call | bytes 9000000 | tf_op jit(solution)/shard_map/pallas_call | solution.py:399
  6.4 6.4 %all-to-all-start.1 = ((f32[8,48,128]{2,1,0:T(8,128)}), f32[8,48,128]{2,1,0:T(8,128)S(1)}, u32[]{:S(2)}, u32[]{:S(2)}) async-start(f32[8,48,128]{2,1,0:T(8,128)} %get-tuple-element.53), calls=%async_computation.1 | async-start | bytes 393216 | tf_op jit(solution)/shard_map/all_to_all | solution.py:628
  12.7 1.7 %shard_map.124 = (bf16[416,128]{1,0:T(8,128)(2,1)}, bf16[176,128]{1,0:T(8,128)(2,1)}) custom-call(f32[768,128]{1,0:T(8,128)} %refs_1_.3), custom_call_target="tpu_custom_call" | custom-call | bytes 1500000 | tf_op jit(solution)/shard_map/pallas_call | solution.py:199
  14.4 0.5 collective-permute-start.1
  14.9 3.0 %collective-permute-start = (bf16[176,128]{1,0:T(8,128)(2,1)}, bf16[176,128]{1,0:T(8,128)(2,1)S(1)}, u32[]{:S(2)}, u32[]{:S(2)}) collective-permute-start(bf16[176,128]{1,0:T(8,128)(2,1)} %get-tuple-element.38.refs_9_), channel_id=1, source_target_pairs={{0,7},{1,0},{2,1},{3,2},{4,3},{5,4},{6,5},{7,6},{8,15},{9,8},{10,9... | collective-permute-start | bytes 135176 | tf_op jit(solution)/shard_map/ppermute | solution.py:32
  17.9 0.0 collective-permute-start.2
  18.0 0.3 collective-permute-start.3
  18.3 3.8 %shard_map.122 = (bf16[352,352]{1,0:T(8,128)(2,1)}, bf16[368,368]{1,0:T(8,128)(2,1)}, bf16[304,304]{1,0:T(8,128)(2,1)}, bf16[192,192]{1,0:T(8,128)(2,1)}, bf16[3...) custom-call(s32[4,343]{1,0:T(4,128)} %refs_0_.2, s32[1,169]{1,0:T(1,128)} %refs_1_.2, ...), custom_call_target="tpu_custom_call" | custom-call | bytes 9000000 | tf_op jit(solution)/shard_map/pallas_call | solution.py:146
  22.0 2.5 %shard_map.123.refs_0_ = f32[768,128]{1,0:T(8,128)} custom-call(f32[768,128]{1,0:T(8,128)} %refs_1_.3, f32[768,128]{1,0:T(8,128)} %get-tuple-element.33.refs_1_.refs_2_, bf16[352,352]{1,0:T(8,128)(2,1)} %get-tuple-element.34.refs_2_.refs_3_.refs_4_, bf16[368,368]{1,0:T(8,128)(2,1)} %get-tuple-element.35.refs_3_.refs_4_.refs_5_, ...), custom_call_target="tpu_custom_call" | custom-call | bytes 6000000 | tf_op jit(solution)/shard_map/pallas_call | solution.py:240
  24.6 0.0 collective-permute-done.3.refs_1_
  24.6 0.0 collective-permute-done.2.refs_0_
  24.6 0.6 copy-done.15
  25.1 0.6 copy-done.13
  25.7 2.7 %shard_map.125 = (bf16[176,304]{1,0:T(8,128)(2,1)}, bf16[176,192]{1,0:T(8,128)(2,1)}, bf16[176,176]{1,0:T(8,128)(2,1)}, bf16[176,176]{1,0:T(8,128)(2,1)}) custom-call(s32[4,343]{1,0:T(4,128)} %copy-done.13, s32[1,169]{1,0:T(1,128)} %copy-done.15, bf16[343,343]{1,0:T(8,128)(2,1)} %refs_2_.3), custom_call_target="tpu_custom_call" | custom-call | bytes 4500000 | tf_op jit(solution)/shard_map/pallas_call | solution.py:172
  28.5 0.0 collective-permute-done.1.refs_2_
  28.5 0.6 copy-done.7
  29.1 0.1 copy-done.2
  29.1 2.5 %shard_map.126 = (f32[768,128]{1,0:T(8,128)}, bf16[416,128]{1,0:T(8,128)(2,1)}, bf16[176,128]{1,0:T(8,128)(2,1)}) custom-call(f32[768,128]{1,0:T(8,128)} %shard_map.123.refs_0_, bf16[176,128]{1,0:T(8,128)(2,1)} %copy-done.7, bf16[416,128]{1,0:T(8,128)(2,1)} %copy-done.2, bf16[304,176]{1,0:T(8,128)(2,1)} %get-tuple-element.40.refs_3_.refs_9_, ...), custom_call_target="tpu_custom_call" | custom-call | bytes 3000000 | tf_op jit(solution)/shard_map/pallas_call | solution.py:324
  31.6 0.0 collective-permute-start.5
  31.6 3.5 %collective-permute-start.4 = (bf16[176,128]{1,0:T(8,128)(2,1)}, bf16[176,128]{1,0:T(8,128)(2,1)S(1)}, u32[]{:S(2)}, u32[]{:S(2)}) collective-permute-start(bf16[176,128]{1,0:T(8,128)(2,1)} %get-tuple-element.47), channel_id=1, source_target_pairs={{0,7},{1,0},{2,1},{3,2},{4,3},{5,4},{6,5},{7,6},{8,15},{9,8},{10,9... | collective-permute-start | bytes 135176 | tf_op jit(solution)/shard_map/ppermute | solution.py:32
  35.1 2.8 %shard_map.127.refs_0_ = f32[768,128]{1,0:T(8,128)} custom-call(f32[768,128]{1,0:T(8,128)} %get-tuple-element.46.refs_0_.refs_1_, f32[768,128]{1,0:T(8,128)} %refs_1_.3, f32[768,128]{1,0:T(8,128)} %get-tuple-element.33.refs_1_.refs_2_, bf16[352,352]{1,0:T(8,128)(2,1)} %get-tuple-element.34.refs_2_.refs_3_.refs_4_, ...), custom_call_target="tpu_custom_call" | custom-call | bytes 6000000 | tf_op jit(solution)/shard_map/pallas_call | solution.py:240
  37.9 0.6 copy-done.10
  38.5 0.6 copy-done.6
  39.2 2.4 %shard_map.128 = (f32[768,128]{1,0:T(8,128)}, bf16[416,128]{1,0:T(8,128)(2,1)}, bf16[176,128]{1,0:T(8,128)(2,1)}) custom-call(f32[768,128]{1,0:T(8,128)} %shard_map.127.refs_0_, bf16[176,128]{1,0:T(8,128)(2,1)} %copy-done.10, bf16[416,128]{1,0:T(8,128)(2,1)} %copy-done.6, bf16[304,176]{1,0:T(8,128)(2,1)} %get-tuple-element.40.refs_3_.refs_9_, ...), custom_call_target="tpu_custom_call" | custom-call | bytes 3000000 | tf_op jit(solution)/shard_map/pallas_call | solution.py:324
  41.5 0.1 collective-permute-start.7
  41.6 3.4 %collective-permute-start.6 = (bf16[176,128]{1,0:T(8,128)(2,1)}, bf16[176,128]{1,0:T(8,128)(2,1)S(1)}, u32[]{:S(2)}, u32[]{:S(2)}) collective-permute-start(bf16[176,128]{1,0:T(8,128)(2,1)} %get-tuple-element.50), channel_id=1, source_target_pairs={{0,7},{1,0},{2,1},{3,2},{4,3},{5,4},{6,5},{7,6},{8,15},{9,8},{10,9... | collective-permute-start | bytes 135176 | tf_op jit(solution)/shard_map/ppermute | solution.py:32
  45.1 2.8 %shard_map.129.refs_0_ = f32[768,128]{1,0:T(8,128)} custom-call(f32[768,128]{1,0:T(8,128)} %get-tuple-element.49.refs_0_, f32[768,128]{1,0:T(8,128)} %get-tuple-element.46.refs_0_.refs_1_, f32[768,128]{1,0:T(8,128)} %get-tuple-element.33.refs_1_.refs_2_, bf16[352,352]{1,0:T(8,128)(2,1)} %get-tuple-element.34.refs_2_.refs_3_.refs_4_, ...), custom_call_target="tpu_custom_call" | custom-call | bytes 6000000 | tf_op jit(solution)/shard_map/pallas_call | solution.py:240
  47.8 0.0 collective-permute-done.6.refs_1_
  47.8 0.3 collective-permute-done.7.refs_2_
  48.1 0.3 copy-done.9
  48.4 0.4 copy-done.3
  48.8 2.6 %shard_map.130 = (f32[768,128]{1,0:T(8,128)}, bf16[416,128]{1,0:T(8,128)(2,1)}, bf16[176,128]{1,0:T(8,128)(2,1)}, f32[32,8,128]{2,1,0:T(8,128)}) custom-call(f32[768,128]{1,0:T(8,128)} %shard_map.129.refs_0_, bf16[176,128]{1,0:T(8,128)(2,1)} %copy-done.9, bf16[416,128]{1,0:T(8,128)(2,1)} %copy-done.3, bf16[304,176]{1,0:T(8,128)(2,1)} %get-tuple-element.40.refs_3_.refs_9_, ...), custom_call_target="tpu_custom_call" | custom-call | bytes 3000000 | tf_op jit(solution)/shard_map/pallas_call | solution.py:324
  51.4 4.7 %all-to-all-start = ((f32[32,8,128]{2,1,0:T(8,128)}), f32[32,8,128]{2,1,0:T(8,128)S(1)}, u32[]{:S(2)}, u32[]{:S(2)}) async-start(f32[32,8,128]{2,1,0:T(8,128)} %get-tuple-element.52), calls=%async_computation | async-start | bytes 262144 | tf_op jit(solution)/shard_map/all_to_all | solution.py:645
  56.0 0.3 collective-permute-start.9
  56.3 3.3 %collective-permute-start.8 = (bf16[176,128]{1,0:T(8,128)(2,1)}, bf16[176,128]{1,0:T(8,128)(2,1)S(1)}, u32[]{:S(2)}, u32[]{:S(2)}) collective-permute-start(bf16[176,128]{1,0:T(8,128)(2,1)} %get-tuple-element.57), channel_id=1, source_target_pairs={{0,7},{1,0},{2,1},{3,2},{4,3},{5,4},{6,5},{7,6},{8,15},{9,8},{10,9... | collective-permute-start | bytes 135176 | tf_op jit(solution)/shard_map/ppermute | solution.py:32
  59.6 2.6 %shard_map.132.refs_5_ = f32[768,128]{1,0:T(8,128)} custom-call(f32[768,128]{1,0:T(8,128)} %get-tuple-element.56.refs_0_.refs_8_.refs_1_, f32[768,128]{1,0:T(8,128)} %get-tuple-element.33.refs_1_.refs_2_, bf16[352,352]{1,0:T(8,128)(2,1)} %get-tuple-element.34.refs_2_.refs_3_.refs_4_, bf16[368,368]{1,0:T(8,128)(2,1)} %get-tuple-element.35.refs_3_.refs_4_.refs_5_, ...), custom_call_target="tpu_custom_call" | custom-call | bytes 6000000 | tf_op jit(solution)/shard_map/pallas_call | solution.py:240
  62.3 2.2 %collective-permute-done.9.refs_7_ = bf16[416,128]{1,0:T(8,128)(2,1)S(1)} collective-permute-done((bf16[416,128]{1,0:T(8,128)(2,1)}, bf16[416,128]{1,0:T(8,128)(2,1)S(1)}, u32[]{:S(2)}, u32[]{:S(2)}) %collective-permute-start.9) | collective-permute-done | bytes 106528 | tf_op jit(solution)/shard_map/ppermute | solution.py:32
  64.5 0.6 copy-done.5
  65.1 0.1 copy-done.1
  65.2 6.3 %shard_map.133 = (f32[768,128]{1,0:T(8,128)}, bf16[416,128]{1,0:T(8,128)(2,1)}, bf16[176,128]{1,0:T(8,128)(2,1)}, f32[768,128]{1,0:T(8,128)}, f32[8,128]{1,0:T(8,128)}) custom-call(f32[32,8,128]{2,1,0:T(8,128)} %copy-done.1, f32[8,48,128]{2,1,0:T(8,128)} %copy-done, bf16[768,768]{1,0:T(8,128)(2,1)} %get-tuple-element.54.refs_2_, ...), custom_call_target="tpu_custom_call" | custom-call | bytes 15000000 | tf_op jit(solution)/shard_map/pallas_call | solution.py:521
  71.4 0.6 collective-permute-start.11
  72.0 3.0 %collective-permute-start.10 = (bf16[176,128]{1,0:T(8,128)(2,1)}, bf16[176,128]{1,0:T(8,128)(2,1)S(1)}, u32[]{:S(2)}, u32[]{:S(2)}) collective-permute-start(bf16[176,128]{1,0:T(8,128)(2,1)} %get-tuple-element.61), channel_id=1, source_target_pairs={{0,7},{1,0},{2,1},{3,2},{4,3},{5,4},{6,5},{7,6},{8,15},{9,8},{10,9... | collective-permute-start | bytes 135176 | tf_op jit(solution)/shard_map/ppermute | solution.py:32
  75.0 1.3 %reshape.19 = f32[768]{0:T(1024)} reshape(f32[8,96]{1,0:T(8,128)} %bitcast.4) | data formatting | bytes 6144 | tf_op jit(solution)/shard_map/reshape | solution.py:651
  76.3 2.9 %shard_map.134.refs_0_ = f32[768,128]{1,0:T(8,128)} custom-call(f32[768,128]{1,0:T(8,128)} %get-tuple-element.59.refs_0_, f32[768,128]{1,0:T(8,128)} %get-tuple-element.56.refs_0_.refs_8_.refs_1_, f32[768,128]{1,0:T(8,128)} %get-tuple-element.33.refs_1_.refs_2_, f32[768,128]{1,0:T(8,128)} %get-tuple-element.60.refs_3_, ...), custom_call_target="tpu_custom_call" | custom-call | bytes 6000000 | tf_op jit(solution)/shard_map/pallas_call | solution.py:240
  79.2 0.6 copy-done.8
  79.8 0.6 copy-done.4
  80.5 2.3 %shard_map.135 = f32[768,128]{1,0:T(8,128)} custom-call(f32[768,128]{1,0:T(8,128)} %shard_map.134.refs_0_, bf16[176,128]{1,0:T(8,128)(2,1)} %copy-done.8, bf16[416,128]{1,0:T(8,128)(2,1)} %copy-done.4, bf16[304,176]{1,0:T(8,128)(2,1)} %get-tuple-element.40.refs_3_.refs_9_, bf16[192,176]{1,0:T(8,128)(2,1)} %get-tuple-element.41.refs_4_.refs_10_, ...), custom_call_target="tpu_custom_call" | custom-call | bytes 3000000 | tf_op jit(solution)/shard_map/pallas_call | solution.py:324
  (28 shorter events, 0.1 us)
Async XLA Ops:
  2.0 16.0 %copy-start.12 = (s32[4,343]{1,0:T(4,128)S(1)}, s32[4,343]{1,0:T(4,128)}, u32[]{:S(2)}) copy-start(s32[4,343]{1,0:T(4,128)} %refs_0_.2) | copy-start | bytes 16468
  2.0 16.0 %copy-start.14 = (s32[1,169]{1,0:T(1,128)S(1)}, s32[1,169]{1,0:T(1,128)}, u32[]{:S(2)}) copy-start(s32[1,169]{1,0:T(1,128)} %refs_1_.2) | copy-start | bytes 2032
  6.4 45.0 %all-to-all-start.1 = ((f32[8,48,128]{2,1,0:T(8,128)}), f32[8,48,128]{2,1,0:T(8,128)S(1)}, u32[]{:S(2)}, u32[]{:S(2)}) async-start(f32[8,48,128]{2,1,0:T(8,128)} %get-tuple-element.53), calls=%async_computation.1 | async-start | bytes 393216 | tf_op jit(solution)/shard_map/all_to_all | solution.py:628
  14.4 14.1 %collective-permute-start.1 = (bf16[416,128]{1,0:T(8,128)(2,1)}, bf16[416,128]{1,0:T(8,128)(2,1)S(1)}, u32[]{:S(2)}, u32[]{:S(2)}) collective-permute-start(bf16[416,128]{1,0:T(8,128)(2,1)} %get-tuple-element.39), channel_id=1, source_target_pairs={{0,1},{1,2},{2,3},{3,4},{4,5},{5,6},{6,7},{7,0},{8,9},{9,10},{10,1... | collective-permute-start | bytes 319496 | tf_op jit(solution)/shard_map/ppermute | solution.py:32
  14.9 13.5 %collective-permute-start = (bf16[176,128]{1,0:T(8,128)(2,1)}, bf16[176,128]{1,0:T(8,128)(2,1)S(1)}, u32[]{:S(2)}, u32[]{:S(2)}) collective-permute-start(bf16[176,128]{1,0:T(8,128)(2,1)} %get-tuple-element.38.refs_9_), channel_id=1, source_target_pairs={{0,7},{1,0},{2,1},{3,2},{4,3},{5,4},{6,5},{7,6},{8,15},{9,8},{10,9... | collective-permute-start | bytes 135176 | tf_op jit(solution)/shard_map/ppermute | solution.py:32
  17.9 6.6 %collective-permute-start.2 = (s32[4,343]{1,0:T(4,128)S(1)}, s32[4,343]{1,0:T(4,128)S(1)}, u32[]{:S(2)}, u32[]{:S(2)}) collective-permute-start(s32[4,343]{1,0:T(4,128)S(1)} %copy-done.12), channel_id=1, source_target_pairs={{0,1},{1,2},{2,3},{3,4},{4,5},{5,6},{6,7},{7,0},{8,9},{9,10},{10,1... | collective-permute-start | bytes 16472 | tf_op jit(solution)/shard_map/ppermute | solution.py:32
  18.0 6.6 %collective-permute-start.3 = (s32[1,169]{1,0:T(1,128)S(1)}, s32[1,169]{1,0:T(1,128)S(1)}, u32[]{:S(2)}, u32[]{:S(2)}) collective-permute-start(s32[1,169]{1,0:T(1,128)S(1)} %copy-done.14), channel_id=1, source_target_pairs={{0,1},{1,2},{2,3},{3,4},{4,5},{5,6},{6,7},{7,0},{8,9},{9,10},{10,1... | collective-permute-start | bytes 2036 | tf_op jit(solution)/shard_map/ppermute | solution.py:32
  24.6 0.6 copy-start.15
  25.1 0.6 copy-start.13
  28.4 0.6 copy-start.7
  28.5 0.7 copy-start.2
  31.6 6.3 %collective-permute-start.5 = (bf16[416,128]{1,0:T(8,128)(2,1)}, bf16[416,128]{1,0:T(8,128)(2,1)S(1)}, u32[]{:S(2)}, u32[]{:S(2)}) collective-permute-start(bf16[416,128]{1,0:T(8,128)(2,1)} %get-tuple-element.48), channel_id=1, source_target_pairs={{0,1},{1,2},{2,3},{3,4},{4,5},{5,6},{6,7},{7,0},{8,9},{9,10},{10,1... | collective-permute-start | bytes 319496 | tf_op jit(solution)/shard_map/ppermute | solution.py:32
  31.6 6.3 %collective-permute-start.4 = (bf16[176,128]{1,0:T(8,128)(2,1)}, bf16[176,128]{1,0:T(8,128)(2,1)S(1)}, u32[]{:S(2)}, u32[]{:S(2)}) collective-permute-start(bf16[176,128]{1,0:T(8,128)(2,1)} %get-tuple-element.47), channel_id=1, source_target_pairs={{0,7},{1,0},{2,1},{3,2},{4,3},{5,4},{6,5},{7,6},{8,15},{9,8},{10,9... | collective-permute-start | bytes 135176 | tf_op jit(solution)/shard_map/ppermute | solution.py:32
  37.9 0.6 copy-start.10
  38.5 0.6 copy-start.6
  41.5 6.6 %collective-permute-start.7 = (bf16[416,128]{1,0:T(8,128)(2,1)}, bf16[416,128]{1,0:T(8,128)(2,1)S(1)}, u32[]{:S(2)}, u32[]{:S(2)}) collective-permute-start(bf16[416,128]{1,0:T(8,128)(2,1)} %get-tuple-element.51), channel_id=1, source_target_pairs={{0,1},{1,2},{2,3},{3,4},{4,5},{5,6},{6,7},{7,0},{8,9},{9,10},{10,1... | collective-permute-start | bytes 319496 | tf_op jit(solution)/shard_map/ppermute | solution.py:32
  41.6 6.2 %collective-permute-start.6 = (bf16[176,128]{1,0:T(8,128)(2,1)}, bf16[176,128]{1,0:T(8,128)(2,1)S(1)}, u32[]{:S(2)}, u32[]{:S(2)}) collective-permute-start(bf16[176,128]{1,0:T(8,128)(2,1)} %get-tuple-element.50), channel_id=1, source_target_pairs={{0,7},{1,0},{2,1},{3,2},{4,3},{5,4},{6,5},{7,6},{8,15},{9,8},{10,9... | collective-permute-start | bytes 135176 | tf_op jit(solution)/shard_map/ppermute | solution.py:32
  47.8 0.6 copy-start.9
  48.1 0.7 copy-start.3
  51.3 10.9 %copy-start = (f32[8,48,128]{2,1,0:T(8,128)}, f32[8,48,128]{2,1,0:T(8,128)S(1)}, u32[]{:S(2)}) copy-start(f32[8,48,128]{2,1,0:T(8,128)S(1)} %all-to-all-done.1.refs_1_) | copy-start | bytes 589828
  51.4 13.1 %all-to-all-start = ((f32[32,8,128]{2,1,0:T(8,128)}), f32[32,8,128]{2,1,0:T(8,128)S(1)}, u32[]{:S(2)}, u32[]{:S(2)}) async-start(f32[32,8,128]{2,1,0:T(8,128)} %get-tuple-element.52), calls=%async_computation | async-start | bytes 262144 | tf_op jit(solution)/shard_map/all_to_all | solution.py:645
  56.0 8.4 %collective-permute-start.9 = (bf16[416,128]{1,0:T(8,128)(2,1)}, bf16[416,128]{1,0:T(8,128)(2,1)S(1)}, u32[]{:S(2)}, u32[]{:S(2)}) collective-permute-start(bf16[416,128]{1,0:T(8,128)(2,1)} %get-tuple-element.58), channel_id=1, source_target_pairs={{0,1},{1,2},{2,3},{3,4},{4,5},{5,6},{6,7},{7,0},{8,9},{9,10},{10,1... | collective-permute-start | bytes 319496 | tf_op jit(solution)/shard_map/ppermute | solution.py:32
  56.3 5.9 %collective-permute-start.8 = (bf16[176,128]{1,0:T(8,128)(2,1)}, bf16[176,128]{1,0:T(8,128)(2,1)S(1)}, u32[]{:S(2)}, u32[]{:S(2)}) collective-permute-start(bf16[176,128]{1,0:T(8,128)(2,1)} %get-tuple-element.57), channel_id=1, source_target_pairs={{0,7},{1,0},{2,1},{3,2},{4,3},{5,4},{6,5},{7,6},{8,15},{9,8},{10,9... | collective-permute-start | bytes 135176 | tf_op jit(solution)/shard_map/ppermute | solution.py:32
  62.3 2.2 %copy-start.11 = (bf16[176,128]{1,0:T(8,128)(2,1)}, bf16[176,128]{1,0:T(8,128)(2,1)S(1)}, u32[]{:S(2)}) copy-start(bf16[176,128]{1,0:T(8,128)(2,1)S(1)} %collective-permute-done.8.refs_6_) | copy-start | bytes 135172
  64.5 0.6 copy-start.5
  64.5 0.7 copy-start.1
  71.4 7.8 %collective-permute-start.11 = (bf16[416,128]{1,0:T(8,128)(2,1)}, bf16[416,128]{1,0:T(8,128)(2,1)S(1)}, u32[]{:S(2)}, u32[]{:S(2)}) collective-permute-start(bf16[416,128]{1,0:T(8,128)(2,1)} %get-tuple-element.62), channel_id=1, source_target_pairs={{0,1},{1,2},{2,3},{3,4},{4,5},{5,6},{6,7},{7,0},{8,9},{9,10},{10,1... | collective-permute-start | bytes 319496 | tf_op jit(solution)/shard_map/ppermute | solution.py:32
  72.0 7.2 %collective-permute-start.10 = (bf16[176,128]{1,0:T(8,128)(2,1)}, bf16[176,128]{1,0:T(8,128)(2,1)S(1)}, u32[]{:S(2)}, u32[]{:S(2)}) collective-permute-start(bf16[176,128]{1,0:T(8,128)(2,1)} %get-tuple-element.61), channel_id=1, source_target_pairs={{0,7},{1,0},{2,1},{3,2},{4,3},{5,4},{6,5},{7,6},{8,15},{9,8},{10,9... | collective-permute-start | bytes 135176 | tf_op jit(solution)/shard_map/ppermute | solution.py:32
  79.2 0.6 copy-start.8
  79.8 0.6 copy-start.4

commit v2 on v1

--- a/solution.py
+++ b/solution.py
@@ -73,7 +73,7 @@
         out_shape=out_shape,
         scratch_shapes=list(scratch),
         cost_estimate=cost,
-        compiler_params=pltpu.CompilerParams(vmem_limit_bytes=56 * 1024 * 1024),
+        compiler_params=pltpu.CompilerParams(vmem_limit_bytes=16 * 1024 * 1024),
         **kwargs,
     )
 

time: 83.4 us -> 70.8 us (0.85)
  Pallas kernels: 42 us -> 14.8 us
  waiting for transfers between devices: 2.5 us -> 11.9 us
  local copies, waits for them, and re-layouts: 8.35 us -> 13.5 us
    pallas_call x5, Pallas kernels: 13.6 us -> 2.41 us  [owned_part(): vmem_call(functools.partial(owned_part_kernel, geo, scale, prev is not No...]
    ppermute x12, waiting for transfers between devices: 2.5 us -> 11.9 us  [from_behind(): lax.ppermute(array, axis, [(i, (i + by) % length) for i in range(length)])]
    pallas_call x4, Pallas kernels: 9.65 us -> 3.03 us  [finish(): vmem_call(functools.partial(finish_kernel, geo, scale, bool(uppers), mode...]
    unnamed x32 -> x38, local copies, waits for them, and re-layouts: 5.65 us -> 12.1 us
    pallas_call x1, Pallas kernels: 4.4 us -> 1.95 us  [field_tables(): vmem_call(functools.partial(field_tables_kernel, fg), [sds((fg.domains, f...]
    pallas_call x1, Pallas kernels: 6.25 us -> 4.38 us  [field_step(): vmem_call(functools.partial(field_kernel, geo, fg, scale), [sds(y.shape,...]
    pallas_call x1, Pallas kernels: 3.75 us -> 1.98 us  [own_matrices(): vmem_call(functools.partial(own_matrices_kernel, geo), shapes, table_scra...]
    pallas_call x1, Pallas kernels: 2.71 us -> 1.04 us  [behind_matrices(): vmem_call(functools.partial(behind_matrices_kernel, geo), shapes, table_s...]
  transfers between devices with their start and end apart: 14 -> 14, of which waited for: 2 -> 8; matrix products, arithmetic and copies ran while one was open for 2% -> 1% of each run, Pallas kernels for 35% -> 11%
where the time goes in v2:
time: 70.8 us; the launch traced here: 70.2 us
  starting transfers between devices  29.2 us (41%)
  Pallas kernels  14.8 us (21%)
  local copies, waits for them, and re-layouts  13.5 us (19%)
  waiting for transfers between devices  11.9 us (17%)
  between operations  0.79 us (1%)
    ppermute x12, starting transfers between devices, from_behind(): lax.ppermute(array, axis, [(i, (i + by) % length) for i in range(length)])  18.2 us
    unnamed x38, local copies, waits for them, and re-layouts  12.1 us
    ppermute x12, waiting for transfers between devices, from_behind(): lax.ppermute(array, axis, [(i, (i + by) % length) for i in range(length)])  11.9 us
    all_to_all x1, starting transfers between devices, per_device(): tables = lax.all_to_all(table, 'domain', 0, 0, tiled=True)  6.35 us
    all_to_all x1, starting transfers between devices, per_device(): dens = lax.all_to_all(spread, ('band', 'domain'), 0, 0, tiled=True)  4.65 us
    pallas_call x1, Pallas kernels, field_step(): vmem_call(functools.partial(field_kernel, geo, fg, scale), [sds(y.shape,...  4.38 us
    pallas_call x4, Pallas kernels, finish(): vmem_call(functools.partial(finish_kernel, geo, scale, bool(uppers), mode...  3.03 us
    pallas_call x5, Pallas kernels, owned_part(): vmem_call(functools.partial(owned_part_kernel, geo, scale, prev is not No...  2.41 us
  transfers between devices with their start and end apart: 14, of which 8 were waited for; matrix products, arithmetic and copies ran while one was open for 1% of the time, Pallas kernels for 11%

profile of v2, /device:TPU:0, one launch (start us, length us, event | category | flops | bytes accessed | tf_op | source)
XLA Modules:
  0.0 70.2 jit_solution(3107071850550689811)
XLA Ops:
  0.6 0.8 %reshape.18.screen_ref = f32[8,96]{1,0:T(8,128)S(1)} reshape(f32[768]{0:T(1024)} %param.20) | data formatting | bytes 6144 | tf_op jit(solution)/shard_map/reshape | solution.py:412
  1.4 1.6 %copy-done.1 = f32[729,729]{1,0:T(8,128)S(1)} copy-done((f32[729,729]{1,0:T(8,128)S(1)}, f32[729,729]{1,0:T(8,128)}, u32[]{:S(2)}) %copy-start.1) | copy-done | bytes 2125788
  3.0 0.7 copy-done.11
  3.7 0.7 copy-done.14
  4.4 0.7 copy-done.18
  5.1 1.9 %shard_map.131 = (f32[8,48,128]{2,1,0:T(8,128)}, bf16[768,768]{1,0:T(8,128)(2,1)S(1)}, bf16[768,768]{1,0:T(8,128)(2,1)S(1)}) custom-call(s32[2,729]{1,0:T(2,128)S(1)} %copy-done.11, s32[1,81]{1,0:T(1,128)S(1)} %copy-done.18, s32[1,8]{1,0:T(1,128)S(1)} %copy-done.14, f32[8,96]{1,0:T(8,128)S(1)} %reshape.18.screen_ref, f32[729,729]{1,0:T(8,128)S(1)} %copy-done.1), custom_call_target="tpu_custom_call" | custom-call | bytes 9000000 | tf_op jit(solution)/shard_map/pallas_call | solution.py:399
  7.0 1.0 %copy-done.2 = bf16[768,768]{1,0:T(8,128)(2,1)} copy-done((bf16[768,768]{1,0:T(8,128)(2,1)}, bf16[768,768]{1,0:T(8,128)(2,1)S(1)}, u32[]{:S(2)}) %copy-start.2) | copy-done | bytes 1179672
  8.0 1.0 %copy-done.4 = bf16[768,768]{1,0:T(8,128)(2,1)} copy-done((bf16[768,768]{1,0:T(8,128)(2,1)}, bf16[768,768]{1,0:T(8,128)(2,1)S(1)}, u32[]{:S(2)}) %copy-start.4) | copy-done | bytes 1179672
  9.1 6.4 %all-to-all-start.1 = ((f32[8,48,128]{2,1,0:T(8,128)}), f32[8,48,128]{2,1,0:T(8,128)S(1)}, u32[]{:S(2)}, u32[]{:S(2)}) async-start(f32[8,48,128]{2,1,0:T(8,128)} %get-tuple-element.53), calls=%async_computation.1 | async-start | bytes 393216 | tf_op jit(solution)/shard_map/all_to_all | solution.py:628
  15.4 0.5 collective-permute-start.1
  16.0 3.1 %collective-permute-start = (bf16[176,128]{1,0:T(8,128)(2,1)S(1)}, bf16[176,128]{1,0:T(8,128)(2,1)S(1)}, u32[]{:S(2)}, u32[]{:S(2)}) collective-permute-start(bf16[176,128]{1,0:T(8,128)(2,1)S(1)} %get-tuple-element.38.refs_9_), channel_id=1, source_target_pairs={{0,7},{1,0},{2,1},{3,2},{4,3},{5,4},{6,5},{7,6},{8,15},{9,8},{10,9... | collective-permute-start | bytes 135176 | tf_op jit(solution)/shard_map/ppermute | solution.py:32
  19.1 0.3 collective-permute-start.3
  19.4 2.0 %shard_map.122 = (bf16[352,352]{1,0:T(8,128)(2,1)S(1)}, bf16[368,368]{1,0:T(8,128)(2,1)S(1)}, bf16[304,304]{1,0:T(8,128)(2,1)S(1)}, bf16[192,192]{1,0:T(8,128)(2...) custom-call(s32[4,343]{1,0:T(4,128)S(1)} %copy-done.12, ...), custom_call_target="tpu_custom_call" | custom-call | bytes 9000000 | tf_op jit(solution)/shard_map/pallas_call | solution.py:146
  21.4 0.4 shard_map.123.refs_0_
  21.8 3.5 %collective-permute-done.3.refs_1_ = s32[1,169]{1,0:T(1,128)S(1)} collective-permute-done((s32[1,169]{1,0:T(1,128)S(1)}, s32[1,169]{1,0:T(1,128)S(1)}, u32[]{:S(2)}, u32[]{:S(2)}) %collective-permute-start.3) | collective-permute-done | bytes 708 | tf_op jit(solution)/shard_map/ppermute | solution.py:32
  25.3 1.0 %shard_map.125 = (bf16[176,304]{1,0:T(8,128)(2,1)S(1)}, bf16[176,192]{1,0:T(8,128)(2,1)S(1)}, bf16[176,176]{1,0:T(8,128)(2,1)S(1)}, bf16[176,176]{1,0:T(8,128)(2,1)S(1)}) custom-call(s32[4,343]{1,0:T(4,128)S(1)} %collective-permute-done.2.refs_0_, s32[1,169]{1,0:T(1,128)S(1)} %collective-permute-done.3.refs_1_, bf16[343,343]{1,0:T(8,128)(2,1)S(1)} %copy-done.6), custom_call_target="tpu_custom_call" | custom-call | bytes 4500000 | tf_op jit(solution)/shard_map/pallas_call | solution.py:172
  26.4 0.3 shard_map.126
  26.7 0.1 collective-permute-start.5
  26.8 3.5 %collective-permute-start.4 = (bf16[176,128]{1,0:T(8,128)(2,1)S(1)}, bf16[176,128]{1,0:T(8,128)(2,1)S(1)}, u32[]{:S(2)}, u32[]{:S(2)}) collective-permute-start(bf16[176,128]{1,0:T(8,128)(2,1)S(1)} %get-tuple-element.47), channel_id=1, source_target_pairs={{0,7},{1,0},{2,1},{3,2},{4,3},{5,4},{6,5},{7,6},{8,15},{9,8},{10,9... | collective-permute-start | bytes 135176 | tf_op jit(solution)/shard_map/ppermute | solution.py:32
  30.3 0.5 shard_map.127.refs_0_
  30.8 1.2 %collective-permute-done.4.refs_1_ = bf16[176,128]{1,0:T(8,128)(2,1)S(1)} collective-permute-done((bf16[176,128]{1,0:T(8,128)(2,1)S(1)}, bf16[176,128]{1,0:T(8,128)(2,1)S(1)}, u32[]{:S(2)}, u32[]{:S(2)}) %collective-permute-start.4) | collective-permute-done | bytes 45088 | tf_op jit(solution)/shard_map/ppermute | solution.py:32
  32.0 0.7 collective-permute-done.5.refs_2_
  32.7 0.3 shard_map.128
  33.1 3.5 %collective-permute-start.6 = (bf16[176,128]{1,0:T(8,128)(2,1)S(1)}, bf16[176,128]{1,0:T(8,128)(2,1)S(1)}, u32[]{:S(2)}, u32[]{:S(2)}) collective-permute-start(bf16[176,128]{1,0:T(8,128)(2,1)S(1)} %get-tuple-element.50), channel_id=1, source_target_pairs={{0,7},{1,0},{2,1},{3,2},{4,3},{5,4},{6,5},{7,6},{8,15},{9,8},{10,9... | collective-permute-start | bytes 135176 | tf_op jit(solution)/shard_map/ppermute | solution.py:32
  36.6 0.5 shard_map.129.refs_0_
  37.1 1.2 %collective-permute-done.6.refs_1_ = bf16[176,128]{1,0:T(8,128)(2,1)S(1)} collective-permute-done((bf16[176,128]{1,0:T(8,128)(2,1)S(1)}, bf16[176,128]{1,0:T(8,128)(2,1)S(1)}, u32[]{:S(2)}, u32[]{:S(2)}) %collective-permute-start.6) | collective-permute-done | bytes 45088 | tf_op jit(solution)/shard_map/ppermute | solution.py:32
  38.3 1.2 %collective-permute-done.7.refs_2_ = bf16[416,128]{1,0:T(8,128)(2,1)S(1)} collective-permute-done((bf16[416,128]{1,0:T(8,128)(2,1)S(1)}, bf16[416,128]{1,0:T(8,128)(2,1)S(1)}, u32[]{:S(2)}, u32[]{:S(2)}) %collective-permute-start.7) | collective-permute-done | bytes 106528 | tf_op jit(solution)/shard_map/ppermute | solution.py:32
  39.5 1.3 %shard_map.130 = (f32[768,128]{1,0:T(8,128)S(1)}, bf16[416,128]{1,0:T(8,128)(2,1)S(1)}, bf16[176,128]{1,0:T(8,128)(2,1)S(1)}, f32[32,8,128]{2,1,0:T(8,128)}) custom-call(f32[768,128]{1,0:T(8,128)S(1)} %shard_map.129.refs_0_, bf16[176,128]{1,0:T(8,128)(2,1)S(1)} %collective-permute-done.6.refs_1_, bf16[416,128]{1,0:T(8,128)(2,1)S(1)} %collective-permute-done.7.refs_2_, ...), custom_call_target="tpu_custom_call" | custom-call | bytes 3000000 | tf_op jit(solution)/shard_map/pallas_call | solution.py:324
  40.8 4.7 %all-to-all-start = ((f32[32,8,128]{2,1,0:T(8,128)}), f32[32,8,128]{2,1,0:T(8,128)S(1)}, u32[]{:S(2)}, u32[]{:S(2)}) async-start(f32[32,8,128]{2,1,0:T(8,128)} %get-tuple-element.52), calls=%async_computation | async-start | bytes 262144 | tf_op jit(solution)/shard_map/all_to_all | solution.py:645
  45.5 0.3 collective-permute-start.9
  45.8 3.3 %collective-permute-start.8 = (bf16[176,128]{1,0:T(8,128)(2,1)S(1)}, bf16[176,128]{1,0:T(8,128)(2,1)S(1)}, u32[]{:S(2)}, u32[]{:S(2)}) collective-permute-start(bf16[176,128]{1,0:T(8,128)(2,1)S(1)} %get-tuple-element.57), channel_id=1, source_target_pairs={{0,7},{1,0},{2,1},{3,2},{4,3},{5,4},{6,5},{7,6},{8,15},{9,8},{10,9... | collective-permute-start | bytes 135176 | tf_op jit(solution)/shard_map/ppermute | solution.py:32
  49.1 0.5 shard_map.132.refs_5_
  49.6 1.2 %collective-permute-done.8.refs_6_ = bf16[176,128]{1,0:T(8,128)(2,1)S(1)} collective-permute-done((bf16[176,128]{1,0:T(8,128)(2,1)S(1)}, bf16[176,128]{1,0:T(8,128)(2,1)S(1)}, u32[]{:S(2)}, u32[]{:S(2)}) %collective-permute-start.8) | collective-permute-done | bytes 45088 | tf_op jit(solution)/shard_map/ppermute | solution.py:32
  50.8 0.6 copy-done.9
  51.4 2.5 %collective-permute-done.9.refs_7_ = bf16[416,128]{1,0:T(8,128)(2,1)S(1)} collective-permute-done((bf16[416,128]{1,0:T(8,128)(2,1)S(1)}, bf16[416,128]{1,0:T(8,128)(2,1)S(1)}, u32[]{:S(2)}, u32[]{:S(2)}) %collective-permute-start.9) | collective-permute-done | bytes 106528 | tf_op jit(solution)/shard_map/ppermute | solution.py:32
  53.9 1.3 %copy-done.3 = bf16[768,768]{1,0:T(8,128)(2,1)S(1)} copy-done((bf16[768,768]{1,0:T(8,128)(2,1)S(1)}, bf16[768,768]{1,0:T(8,128)(2,1)}, u32[]{:S(2)}) %copy-start.3) | copy-done | bytes 1179672
  55.2 1.3 %copy-done.5 = bf16[768,768]{1,0:T(8,128)(2,1)S(1)} copy-done((bf16[768,768]{1,0:T(8,128)(2,1)S(1)}, bf16[768,768]{1,0:T(8,128)(2,1)}, u32[]{:S(2)}) %copy-start.5) | copy-done | bytes 1179672
  56.5 0.8 %copy-done.10 = bf16[176,128]{1,0:T(8,128)(2,1)S(1)} copy-done((bf16[176,128]{1,0:T(8,128)(2,1)S(1)}, bf16[176,128]{1,0:T(8,128)(2,1)}, u32[]{:S(2)}) %copy-start.10) | copy-done | bytes 45080
  57.2 0.7 copy-done.15
  57.9 4.4 %shard_map.133 = (f32[768,128]{1,0:T(8,128)S(1)}, bf16[416,128]{1,0:T(8,128)(2,1)}, bf16[176,128]{1,0:T(8,128)(2,1)}, f32[768,128]{1,0:T(8,128)S(1)}, f32[8,128]{1,0:T(8,128)S(1)}) custom-call(f32[32,8,128]{2,1,0:T(8,128)S(1)} %all-to-all-done.refs_0_, f32[8,48,128]{2,1,0:T(8,128)S(1)} %all-to-all-done.1.refs_1_, bf16[768,768]{1,0:T(8,128)(2,1)S(1)} %copy-done.3, ...), custom_call_target="tpu_custom_call" | custom-call | bytes 15000000 | tf_op jit(solution)/shard_map/pallas_call | solution.py:521
  62.3 0.7 %copy-done.7 = f32[768,128]{1,0:T(8,128)} copy-done((f32[768,128]{1,0:T(8,128)}, f32[768,128]{1,0:T(8,128)S(1)}, u32[]{:S(2)}) %copy-start.7) | copy-done | bytes 393240
  63.0 0.6 collective-permute-start.11
  63.6 2.9 %collective-permute-start.10 = (bf16[176,128]{1,0:T(8,128)(2,1)}, bf16[176,128]{1,0:T(8,128)(2,1)S(1)}, u32[]{:S(2)}, u32[]{:S(2)}) collective-permute-start(bf16[176,128]{1,0:T(8,128)(2,1)} %get-tuple-element.61), channel_id=1, source_target_pairs={{0,7},{1,0},{2,1},{3,2},{4,3},{5,4},{6,5},{7,6},{8,15},{9,8},{10,9... | collective-permute-start | bytes 135176 | tf_op jit(solution)/shard_map/ppermute | solution.py:32
  66.6 0.7 reshape.19
  67.2 1.0 %copy-done.8 = f32[768,128]{1,0:T(8,128)S(1)} copy-done((f32[768,128]{1,0:T(8,128)S(1)}, f32[768,128]{1,0:T(8,128)}, u32[]{:S(2)}) %copy-start.8) | copy-done | bytes 393240
  68.2 0.5 shard_map.134.refs_0_
  68.7 0.4 collective-permute-done.11.refs_2_
  69.2 1.1 %shard_map.135 = f32[768,128]{1,0:T(8,128)} custom-call(f32[768,128]{1,0:T(8,128)S(1)} %shard_map.134.refs_0_, bf16[176,128]{1,0:T(8,128)(2,1)S(1)} %collective-permute-done.10.refs_1_, bf16[416,128]{1,0:T(8,128)(2,1)S(1)} %collective-permute-done.11.refs_2_, bf16[304,176]{1,0:T(8,128)(2,1)S(1)} %get-tuple-element.40.refs_3_.refs_9_, ...), custom_call_target="tpu_custom_call" | custom-call | bytes 3000000 | tf_op jit(solution)/shard_map/pallas_call | solution.py:324
  (34 shorter events, 0.1 us)
Async XLA Ops:
  1.4 1.6 %copy-start.1 = (f32[729,729]{1,0:T(8,128)S(1)}, f32[729,729]{1,0:T(8,128)}, u32[]{:S(2)}) copy-start(f32[729,729]{1,0:T(8,128)} %matrix_ref.1) | copy-start | bytes 6377296
  3.0 0.7 copy-start.11
  3.7 0.7 copy-start.14
  4.4 0.7 copy-start.18
  5.0 10.4 %copy-start = (f32[768,128]{1,0:T(8,128)S(1)}, f32[768,128]{1,0:T(8,128)}, u32[]{:S(2)}) copy-start(f32[768,128]{1,0:T(8,128)} %refs_1_.3) | copy-start | bytes 1179652
  5.0 14.1 %copy-start.12 = (s32[4,343]{1,0:T(4,128)S(1)}, s32[4,343]{1,0:T(4,128)}, u32[]{:S(2)}) copy-start(s32[4,343]{1,0:T(4,128)} %refs_0_.2) | copy-start | bytes 16468
  5.0 14.1 %copy-start.16 = (s32[1,169]{1,0:T(1,128)S(1)}, s32[1,169]{1,0:T(1,128)}, u32[]{:S(2)}) copy-start(s32[1,169]{1,0:T(1,128)} %refs_1_.2) | copy-start | bytes 2032
  5.0 14.3 %copy-start.6 = (bf16[343,343]{1,0:T(8,128)(2,1)S(1)}, bf16[343,343]{1,0:T(8,128)(2,1)}, u32[]{:S(2)}) copy-start(bf16[343,343]{1,0:T(8,128)(2,1)} %refs_2_.3) | copy-start | bytes 705898
  5.0 14.3 %copy-start.13 = (f32[768]{0:T(1024)S(1)}, f32[768]{0:T(1024)}, u32[]{:S(2)}) copy-start(f32[768]{0:T(1024)} %param.12) | copy-start | bytes 9220
  7.0 1.0 %copy-start.2 = (bf16[768,768]{1,0:T(8,128)(2,1)}, bf16[768,768]{1,0:T(8,128)(2,1)S(1)}, u32[]{:S(2)}) copy-start(bf16[768,768]{1,0:T(8,128)(2,1)S(1)} %get-tuple-element.54.refs_2_) | copy-start | bytes 3538948
  8.0 1.0 %copy-start.4 = (bf16[768,768]{1,0:T(8,128)(2,1)}, bf16[768,768]{1,0:T(8,128)(2,1)S(1)}, u32[]{:S(2)}) copy-start(bf16[768,768]{1,0:T(8,128)(2,1)S(1)} %get-tuple-element.55.refs_3_) | copy-start | bytes 3538948
  9.1 31.8 %all-to-all-start.1 = ((f32[8,48,128]{2,1,0:T(8,128)}), f32[8,48,128]{2,1,0:T(8,128)S(1)}, u32[]{:S(2)}, u32[]{:S(2)}) async-start(f32[8,48,128]{2,1,0:T(8,128)} %get-tuple-element.53), calls=%async_computation.1 | async-start | bytes 393216 | tf_op jit(solution)/shard_map/all_to_all | solution.py:628
  15.4 10.9 %collective-permute-start.1 = (bf16[416,128]{1,0:T(8,128)(2,1)S(1)}, bf16[416,128]{1,0:T(8,128)(2,1)S(1)}, u32[]{:S(2)}, u32[]{:S(2)}) collective-permute-start(bf16[416,128]{1,0:T(8,128)(2,1)S(1)} %get-tuple-element.39), channel_id=1, source_target_pairs={{0,1},{1,2},{2,3},{3,4},{4,5},{5,6},{6,7},{7,0},{8,9},{9,10},{10,1... | collective-permute-start | bytes 319496 | tf_op jit(solution)/shard_map/ppermute | solution.py:32
  16.0 10.4 %collective-permute-start = (bf16[176,128]{1,0:T(8,128)(2,1)S(1)}, bf16[176,128]{1,0:T(8,128)(2,1)S(1)}, u32[]{:S(2)}, u32[]{:S(2)}) collective-permute-start(bf16[176,128]{1,0:T(8,128)(2,1)S(1)} %get-tuple-element.38.refs_9_), channel_id=1, source_target_pairs={{0,7},{1,0},{2,1},{3,2},{4,3},{5,4},{6,5},{7,6},{8,15},{9,8},{10,9... | collective-permute-start | bytes 135176 | tf_op jit(solution)/shard_map/ppermute | solution.py:32
  19.1 6.2 %collective-permute-start.2 = (s32[4,343]{1,0:T(4,128)S(1)}, s32[4,343]{1,0:T(4,128)S(1)}, u32[]{:S(2)}, u32[]{:S(2)}) collective-permute-start(s32[4,343]{1,0:T(4,128)S(1)} %copy-done.12), channel_id=1, source_target_pairs={{0,1},{1,2},{2,3},{3,4},{4,5},{5,6},{6,7},{7,0},{8,9},{9,10},{10,1... | collective-permute-start | bytes 16472 | tf_op jit(solution)/shard_map/ppermute | solution.py:32
  19.1 6.2 %collective-permute-start.3 = (s32[1,169]{1,0:T(1,128)S(1)}, s32[1,169]{1,0:T(1,128)S(1)}, u32[]{:S(2)}, u32[]{:S(2)}) collective-permute-start(s32[1,169]{1,0:T(1,128)S(1)} %copy-done.16), channel_id=1, source_target_pairs={{0,1},{1,2},{2,3},{3,4},{4,5},{5,6},{6,7},{7,0},{8,9},{9,10},{10,1... | collective-permute-start | bytes 2036 | tf_op jit(solution)/shard_map/ppermute | solution.py:32
  26.7 6.0 %collective-permute-start.5 = (bf16[416,128]{1,0:T(8,128)(2,1)S(1)}, bf16[416,128]{1,0:T(8,128)(2,1)S(1)}, u32[]{:S(2)}, u32[]{:S(2)}) collective-permute-start(bf16[416,128]{1,0:T(8,128)(2,1)S(1)} %get-tuple-element.48), channel_id=1, source_target_pairs={{0,1},{1,2},{2,3},{3,4},{4,5},{5,6},{6,7},{7,0},{8,9},{9,10},{10,1... | collective-permute-start | bytes 319496 | tf_op jit(solution)/shard_map/ppermute | solution.py:32
  26.8 5.2 %collective-permute-start.4 = (bf16[176,128]{1,0:T(8,128)(2,1)S(1)}, bf16[176,128]{1,0:T(8,128)(2,1)S(1)}, u32[]{:S(2)}, u32[]{:S(2)}) collective-permute-start(bf16[176,128]{1,0:T(8,128)(2,1)S(1)} %get-tuple-element.47), channel_id=1, source_target_pairs={{0,7},{1,0},{2,1},{3,2},{4,3},{5,4},{6,5},{7,6},{8,15},{9,8},{10,9... | collective-permute-start | bytes 135176 | tf_op jit(solution)/shard_map/ppermute | solution.py:32
  33.0 6.5 %collective-permute-start.7 = (bf16[416,128]{1,0:T(8,128)(2,1)S(1)}, bf16[416,128]{1,0:T(8,128)(2,1)S(1)}, u32[]{:S(2)}, u32[]{:S(2)}) collective-permute-start(bf16[416,128]{1,0:T(8,128)(2,1)S(1)} %get-tuple-element.51), channel_id=1, source_target_pairs={{0,1},{1,2},{2,3},{3,4},{4,5},{5,6},{6,7},{7,0},{8,9},{9,10},{10,1... | collective-permute-start | bytes 319496 | tf_op jit(solution)/shard_map/ppermute | solution.py:32
  33.1 5.2 %collective-permute-start.6 = (bf16[176,128]{1,0:T(8,128)(2,1)S(1)}, bf16[176,128]{1,0:T(8,128)(2,1)S(1)}, u32[]{:S(2)}, u32[]{:S(2)}) collective-permute-start(bf16[176,128]{1,0:T(8,128)(2,1)S(1)} %get-tuple-element.50), channel_id=1, source_target_pairs={{0,7},{1,0},{2,1},{3,2},{4,3},{5,4},{6,5},{7,6},{8,15},{9,8},{10,9... | collective-permute-start | bytes 135176 | tf_op jit(solution)/shard_map/ppermute | solution.py:32
  36.6 2.9 %copy-start.17 = (f32[128]{0:T(128)S(1)}, f32[128]{0:T(128)}, u32[]{:S(2)}) copy-start(f32[128]{0:T(128)} %param.13) | copy-start | bytes 1540
  40.8 13.1 %all-to-all-start = ((f32[32,8,128]{2,1,0:T(8,128)}), f32[32,8,128]{2,1,0:T(8,128)S(1)}, u32[]{:S(2)}, u32[]{:S(2)}) async-start(f32[32,8,128]{2,1,0:T(8,128)} %get-tuple-element.52), calls=%async_computation | async-start | bytes 262144 | tf_op jit(solution)/shard_map/all_to_all | solution.py:645
  45.5 8.4 %collective-permute-start.9 = (bf16[416,128]{1,0:T(8,128)(2,1)S(1)}, bf16[416,128]{1,0:T(8,128)(2,1)S(1)}, u32[]{:S(2)}, u32[]{:S(2)}) collective-permute-start(bf16[416,128]{1,0:T(8,128)(2,1)S(1)} %get-tuple-element.58), channel_id=1, source_target_pairs={{0,1},{1,2},{2,3},{3,4},{4,5},{5,6},{6,7},{7,0},{8,9},{9,10},{10,1... | collective-permute-start | bytes 319496 | tf_op jit(solution)/shard_map/ppermute | solution.py:32
  45.8 5.0 %collective-permute-start.8 = (bf16[176,128]{1,0:T(8,128)(2,1)S(1)}, bf16[176,128]{1,0:T(8,128)(2,1)S(1)}, u32[]{:S(2)}, u32[]{:S(2)}) collective-permute-start(bf16[176,128]{1,0:T(8,128)(2,1)S(1)} %get-tuple-element.57), channel_id=1, source_target_pairs={{0,7},{1,0},{2,1},{3,2},{4,3},{5,4},{6,5},{7,6},{8,15},{9,8},{10,9... | collective-permute-start | bytes 135176 | tf_op jit(solution)/shard_map/ppermute | solution.py:32
  50.8 0.6 copy-start.9
  53.9 1.3 %copy-start.3 = (bf16[768,768]{1,0:T(8,128)(2,1)S(1)}, bf16[768,768]{1,0:T(8,128)(2,1)}, u32[]{:S(2)}) copy-start(bf16[768,768]{1,0:T(8,128)(2,1)} %copy-done.2) | copy-start | bytes 3538948
  55.2 1.3 %copy-start.5 = (bf16[768,768]{1,0:T(8,128)(2,1)S(1)}, bf16[768,768]{1,0:T(8,128)(2,1)}, u32[]{:S(2)}) copy-start(bf16[768,768]{1,0:T(8,128)(2,1)} %copy-done.4) | copy-start | bytes 3538948
  56.4 0.8 %copy-start.10 = (bf16[176,128]{1,0:T(8,128)(2,1)S(1)}, bf16[176,128]{1,0:T(8,128)(2,1)}, u32[]{:S(2)}) copy-start(bf16[176,128]{1,0:T(8,128)(2,1)} %copy-done.9) | copy-start | bytes 135172
  57.2 0.7 copy-start.15
  62.3 0.7 %copy-start.7 = (f32[768,128]{1,0:T(8,128)}, f32[768,128]{1,0:T(8,128)S(1)}, u32[]{:S(2)}) copy-start(f32[768,128]{1,0:T(8,128)S(1)} %get-tuple-element.60.refs_3_) | copy-start | bytes 1179652
  63.0 6.1 %collective-permute-start.11 = (bf16[416,128]{1,0:T(8,128)(2,1)}, bf16[416,128]{1,0:T(8,128)(2,1)S(1)}, u32[]{:S(2)}, u32[]{:S(2)}) collective-permute-start(bf16[416,128]{1,0:T(8,128)(2,1)} %get-tuple-element.62), channel_id=1, source_target_pairs={{0,1},{1,2},{2,3},{3,4},{4,5},{5,6},{6,7},{7,0},{8,9},{9,10},{10,1... | collective-permute-start | bytes 319496 | tf_op jit(solution)/shard_map/ppermute | solution.py:32
  63.6 5.1 %collective-permute-start.10 = (bf16[176,128]{1,0:T(8,128)(2,1)}, bf16[176,128]{1,0:T(8,128)(2,1)S(1)}, u32[]{:S(2)}, u32[]{:S(2)}) collective-permute-start(bf16[176,128]{1,0:T(8,128)(2,1)} %get-tuple-element.61), channel_id=1, source_target_pairs={{0,7},{1,0},{2,1},{3,2},{4,3},{5,4},{6,5},{7,6},{8,15},{9,8},{10,9... | collective-permute-start | bytes 135176 | tf_op jit(solution)/shard_map/ppermute | solution.py:32
  67.2 1.0 %copy-start.8 = (f32[768,128]{1,0:T(8,128)S(1)}, f32[768,128]{1,0:T(8,128)}, u32[]{:S(2)}) copy-start(f32[768,128]{1,0:T(8,128)} %copy-done.7) | copy-start | bytes 1179652

commit v3 on v2

--- a/solution.py
+++ b/solution.py
@@ -54,6 +54,9 @@
         self.dn_lo = min(self.windows[c].lo for c in self.touching)
         self.low = max(w.low for w in self.windows)
         self.dn_rows = own - self.dn_lo + self.low
+        self.table_rows = up_to(cells + 1, SUBLANES)
+        self.table_lanes = up_to(max(npc, share), LANES)
+        self.table_tiles = self.table_lanes // LANES
 
 
 def dot(a, b):
@@ -73,9 +76,13 @@
         out_shape=out_shape,
         scratch_shapes=list(scratch),
         cost_estimate=cost,
-        compiler_params=pltpu.CompilerParams(vmem_limit_bytes=16 * 1024 * 1024),
+        compiler_params=pltpu.CompilerParams(vmem_limit_bytes=12 * 1024 * 1024),
         **kwargs,
     )
+
+
+def in_hbm(*arrays):
+    return [pltpu.with_memory_space_constraint(a, pltpu.HBM) for a in arrays]
 
 
 def sds(shape, dtype):
@@ -87,21 +94,32 @@
     return jnp.where(ids == nodes, 1.0, 0.0).astype(BF)
 
 
-def place_tables(geo, nodes_ref, face_ref, matrix_ref, nodes_pad, face_pad, matrix_pad):
-    nodes_pad[...] = jnp.full(nodes_pad.shape, -1, I32)
-    nodes_pad[0 : geo.cells, 0 : geo.npc] = nodes_ref[...]
-    face_pad[...] = jnp.full(face_pad.shape, -1, I32)
-    face_pad[0:1, 0 : geo.share] = face_ref[...]
+def place_table(geo, nodes_ref, face_ref, table):
+    table[...] = jnp.full(table.shape, -1, I32)
+    table[0 : geo.cells, 0 : geo.npc] = nodes_ref[...]
+    table[geo.cells : geo.cells + 1, 0 : geo.share] = face_ref[...]
+
+
+def place_matrix(geo, matrix_ref, matrix_pad):
     matrix_pad[...] = jnp.zeros(matrix_pad.shape, F32)
     matrix_pad[0 : geo.npc, 0 : geo.npc] = matrix_ref[...].astype(F32)
+    return matrix_pad[...].astype(BF)
 
 
 def table_scratch(geo):
-    return [
-        pltpu.VMEM((up_to(geo.cells, SUBLANES), geo.npl), I32),
-        pltpu.VMEM((SUBLANES, up_to(geo.share, LANES)), I32),
-        pltpu.VMEM((geo.npl, geo.npl), F32),
-    ]
+    return pltpu.VMEM((geo.table_rows, geo.table_lanes), I32)
+
+
+def matrix_scratch(geo):
+    return pltpu.VMEM((geo.npl, geo.npl), F32)
+
+
+def nodes_of(geo, table, c):
+    return table[c : c + 1, 0 : geo.npl]
+
+
+def face_of(geo, table):
+    return table[geo.cells : geo.cells + 1, 0 : up_to(geo.share, LANES)]
 
 
 def owned_picks(geo, c, nodes):
@@ -119,14 +137,16 @@
 
 
 def own_matrices_kernel(geo, *refs):
-    nodes_ref, face_ref, matrix_ref, pot_ref = refs[:4]
-    outs = refs[4:-3]
-    nodes_pad, face_pad, matrix_pad = refs[-3:]
-    place_tables(geo, nodes_ref, face_ref, matrix_ref, nodes_pad, face_pad, matrix_pad)
-    matrix = matrix_pad[...].astype(BF)
-    face = face_pad[0:1, :]
+    outs = refs[4:-7]
+    nodes_ref, face_ref, matrix_ref, pot_ref, table, matrix_pad, sems = refs[-7:]
+    copies = fetch(list(zip(refs[:4], (nodes_ref, face_ref, matrix_ref, pot_ref))), sems)
+    for copy in copies:
+        copy.wait()
+    place_table(geo, nodes_ref, face_ref, table)
+    matrix = place_matrix(geo, matrix_ref, matrix_pad)
+    face = face_of(geo, table)
     for c in range(geo.cells):
-        nodes = nodes_pad[c : c + 1, :]
+        nodes = nodes_of(geo, table, c)
         own = owned_picks(geo, c, nodes)
         left = dot(own, matrix).astype(BF)
         outs[c][...] = dot_t(left, own).astype(BF)
@@ -144,34 +164,53 @@
     shapes += [sds((geo.windows[c].rows, geo.sp), BF) for c in geo.touching]
     shapes += [sds((geo.own, LANES), F32)]
     outs = vmem_call(
-        functools.partial(own_matrices_kernel, geo), shapes, table_scratch(geo), cost=cost_of(3.0)
-    )(cell_nodes, face_order, cell_matrix, potential.reshape(geo.own // LANES, LANES))
+        functools.partial(own_matrices_kernel, geo),
+        shapes,
+        [
+            pltpu.VMEM(cell_nodes.shape, I32),
+            pltpu.VMEM(face_order.shape, I32),
+            pltpu.VMEM(cell_matrix.shape, BF),
+            pltpu.VMEM((geo.own // LANES, LANES), F32),
+            table_scratch(geo),
+            matrix_scratch(geo),
+            pltpu.SemaphoreType.DMA((4,)),
+        ],
+        in_specs=[pl.BlockSpec(memory_space=pltpu.HBM)] * 4,
+        cost=cost_of(2.0),
+    )(*in_hbm(cell_nodes, face_order, cell_matrix, potential.reshape(geo.own // LANES, LANES)))
     n = geo.cells
     return outs[:n], outs[n:-1], outs[-1]
 
 
 def behind_matrices_kernel(geo, *refs):
-    nodes_ref, face_ref, matrix_ref = refs[:3]
-    outs = refs[3:-3]
-    nodes_pad, face_pad, matrix_pad = refs[-3:]
-    place_tables(geo, nodes_ref, face_ref, matrix_ref, nodes_pad, face_pad, matrix_pad)
-    matrix = matrix_pad[...].astype(BF)
-    face = face_pad[0:1, :]
+    sent_ref, matrix_ref = refs[:2]
+    outs = refs[2:-2]
+    table, matrix_pad = refs[-2:]
+    for t in range(geo.table_tiles):
+        at = geo.dn_rows + 2 * t * geo.table_rows
+        digits = sent_ref[at : at + 2 * geo.table_rows, :].astype(F32)
+        value = digits[: geo.table_rows] * LANES + digits[geo.table_rows :] - 1.0
+        table[:, t * LANES : (t + 1) * LANES] = value.astype(I32)
+    matrix = place_matrix(geo, matrix_ref, matrix_pad)
+    face = face_of(geo, table)
     count = len(geo.touching)
     for at, c in enumerate(geo.touching):
-        nodes = nodes_pad[c : c + 1, :]
+        nodes = nodes_of(geo, table, c)
         upper = upper_picks(geo, nodes, face)
         left = dot(upper, matrix).astype(BF)
         outs[at][...] = dot_t(left, owned_picks(geo, c, nodes)).astype(BF)
         outs[count + at][...] = dot_t(left, upper).astype(BF)
 
 
-def behind_matrices(geo, nodes, face, cell_matrix):
+def behind_matrices(geo, sent, cell_matrix):
     shapes = [sds((geo.sp, geo.windows[c].rows), BF) for c in geo.touching]
     shapes += [sds((geo.sp, geo.sp), BF) for _ in geo.touching]
     outs = vmem_call(
-        functools.partial(behind_matrices_kernel, geo), shapes, table_scratch(geo), cost=cost_of(1.5)
-    )(nodes, face, cell_matrix)
+        functools.partial(behind_matrices_kernel, geo),
+        shapes,
+        [table_scratch(geo), matrix_scratch(geo)],
+        cost=cost_of(1.0),
+    )(sent, cell_matrix)
     n = len(geo.touching)
     return outs[:n], outs[n:]
 
@@ -191,14 +230,49 @@
     return [sds((geo.dn_rows, columns), BF), sds((geo.sp, columns), BF)]
 
 
-def pack_kernel(geo, y_ref, dn_ref, up_ref):
-    write_sends(geo, y_ref, dn_ref, up_ref)
-
-
-def pack(geo, y):
+def fetch(pairs, sems):
+    copies = [pltpu.make_async_copy(src, dst, sems.at[i]) for i, (src, dst) in enumerate(pairs)]
+    for copy in copies:
+        copy.start()
+    return copies
+
+
+def pack_kernel(geo, y_hbm, nodes_hbm, face_hbm, dn_ref, up_ref, y, nodes, face, table, sems):
+    cuts = sorted({0, max(geo.sp, geo.low), geo.dn_lo, geo.own})
+    spans = list(zip(cuts[:-1], cuts[1:]))
+    pairs = [(nodes_hbm, nodes), (face_hbm, face)]
+    pairs += [(y_hbm.at[pl.ds(a, b - a)], y.at[pl.ds(a, b - a)]) for a, b in spans]
+    copies = fetch(pairs, sems)
+    copies[0].wait()
+    copies[1].wait()
+    place_table(geo, nodes, face, table)
+    for t in range(geo.table_tiles):
+        at = geo.dn_rows + 2 * t * geo.table_rows
+        value = table[:, t * LANES : (t + 1) * LANES] + 1
+        high = jnp.right_shift(value, 7).astype(F32)
+        low = jnp.bitwise_and(value, LANES - 1).astype(F32)
+        digits = jnp.concatenate([high, low], axis=0).astype(BF)
+        dn_ref[at : at + 2 * geo.table_rows, :] = digits
+    for copy in copies[2:]:
+        copy.wait()
+    write_sends(geo, y, dn_ref, up_ref)
+
+
+def pack(geo, y, cell_nodes, face_order):
+    _, up = send_shapes(geo, y.shape[1])
+    rows = geo.dn_rows + 2 * geo.table_rows * geo.table_tiles
     return vmem_call(
-        functools.partial(pack_kernel, geo), send_shapes(geo, y.shape[1]), cost=cost_of(0.5)
-    )(y)
+        functools.partial(pack_kernel, geo),
+        [sds((rows, y.shape[1]), BF), up, sds(y.shape, F32)],
+        [
+            pltpu.VMEM(cell_nodes.shape, I32),
+            pltpu.VMEM(face_order.shape, I32),
+            table_scratch(geo),
+            pltpu.SemaphoreType.DMA((5,)),
+        ],
+        in_specs=[pl.BlockSpec(memory_space=pltpu.HBM)] * 3,
+        cost=cost_of(1.0),
+    )(*in_hbm(y, cell_nodes, face_order))
 
 
 def owned_part_kernel(geo, scale, has_prev, has_field, has_upper, *refs):
@@ -268,7 +342,7 @@
 
 
 def write_density(y_ref, occ_ref, dens_ref, row_pad):
-    parts, blocks, _ = dens_ref.shape
+    _, blocks, _ = dens_ref.shape
     own = y_ref.shape[0]
     length = own // blocks
     y = y_ref[...]
@@ -295,8 +369,13 @@
         uppers, refs = refs[:n], refs[n:]
         own_up = refs.pop(0)
     occ_ref = refs.pop(0) if mode == "density" else None
+    if mode == "field":
+        column_ref, before_ref = refs.pop(0), refs.pop(0)
     y_ref = refs.pop(0)
-    y_ref[...] = base_ref[...]
+    if mode == "field":
+        y_ref[...] = base_ref[...] + (column_ref[...] * scale) * before_ref[...]
+    else:
+        y_ref[...] = base_ref[...]
     add_halo(geo, scale, y_ref, up_ref, dn_ref, crosses, behinds, uppers, own_up)
     if mode != "last":
         write_sends(geo, y_ref, refs[0], refs[1])
@@ -304,7 +383,7 @@
         write_density(y_ref, occ_ref, refs[2], refs[3])
 
 
-def finish(geo, scale, base, halo, crosses, behinds, uppers=(), own_up=None, occ=None, parts=None, last=False):
+def finish(geo, scale, base, halo, crosses, behinds, uppers=(), own_up=None, occ=None, parts=None, field=None, last=False):
     columns = base.shape[1]
     args = [base, halo[0], halo[1], *crosses, *behinds, *uppers]
     if uppers:
@@ -316,6 +395,9 @@
         mode = "last"
     else:
         shapes += send_shapes(geo, columns)
+    if field is not None:
+        mode = "field"
+        args += list(field)
     if occ is not None:
         mode = "density"
         args.append(occ)
@@ -339,21 +421,45 @@
         self.at_face = self.at_inverse + cells * self.blocks
         self.at_face_inverse = self.at_face + 1
         self.at_owner = self.at_face + 2
-        self.at_screen = self.at_face + 3
+        self.codes = self.at_face + 3
+        self.at_screen = up_to(self.codes, 2) // 2
         self.table_rows = up_to(self.at_screen + domains, SUBLANES)
+        self.size = self.rows * LANES
         self.fits = (
             domains == SUBLANES
-            and own % domains == 0
+            and own % (domains * SUBLANES) == 0
+            and own % LANES == 0
             and share <= self.block <= LANES
+            and max(npc, self.blocks * LANES) < CODE_BASE - 1
         )
+
+
+CODE_BASE = 2048
+CODE_BITS = 11
+
+
+def pieces(length, blocks):
+    found = []
+    for j in range(blocks):
+        done = 0
+        while done < length:
+            at = j * length + done
+            count = min(length - done, LANES - at % LANES)
+            found.append((at // LANES, at % LANES, j, done, count))
+            done += count
+    return found
 
 
 def column_of(row):
     return jnp.broadcast_to(row, (LANES, LANES)).T
 
 
-def field_tables_kernel(fg, nodes_ref, face_ref, owner_ref, screen_ref, matrix_ref, table_ref, high_ref, low_ref, pad, one, wide):
-    lane = lax.broadcasted_iota(I32, (1, LANES), 1)
+def field_tables_kernel(fg, *refs):
+    sources, table_ref = refs[:4], refs[5]
+    nodes_ref, face_ref, owner_ref, screen_ref, pad, one, packed, sems = refs[6:]
+    copies = fetch(list(zip(sources, (nodes_ref, face_ref, owner_ref, screen_ref))), sems)
+    for copy in copies:
+        copy.wait()
     one[...] = jnp.full(one.shape, -1.0, F32)
     pad[...] = jnp.full(pad.shape, -1, I32)
     pad[0 : fg.cells, 0 : fg.npc] = nodes_ref[...]
@@ -376,7 +482,7 @@
             found = jnp.zeros((LANES, LANES), F32)
             for r in range(fg.rows):
                 position = (sub + (r * LANES + 1)).astype(F32)
-                found = found + jnp.where(columns[r] == target, position, 0.0)
+                found = jnp.where(columns[r] == target, position, found)
             at = fg.at_inverse + c * fg.blocks + b
             one[at : at + 1, :] = jnp.sum(found, axis=0, keepdims=True) - 1.0
     one[fg.at_face : fg.at_face + 1, 0 : fg.share] = face_ref[...].astype(F32)
@@ -384,49 +490,51 @@
     hits = jnp.where(column == wide_lane.astype(F32), (sub + 1).astype(F32), 0.0)
     one[fg.at_face_inverse : fg.at_face_inverse + 1, :] = jnp.sum(hits, axis=0, keepdims=True) - 1.0
     one[fg.at_owner : fg.at_owner + 1, 0 : fg.domains] = owner_ref[...].astype(F32)
-    one[fg.at_screen : fg.at_screen + fg.domains, 0 : fg.block] = screen_ref[...]
-    table_ref[...] = jnp.broadcast_to(one[...][None], table_ref.shape)
-    wide[...] = jnp.zeros(wide.shape, F32)
-    wide[0 : fg.npc, 0 : fg.npc] = matrix_ref[...]
-    full = wide[...]
-    high = full.astype(BF)
-    high_ref[...] = high
-    low_ref[...] = (full - high.astype(F32)).astype(BF)
-
-
-def field_tables(fg, pois_nodes, pois_face, block_owner, screening, pois_matrix):
-    size = fg.rows * LANES
+    packed[...] = jnp.zeros(packed.shape, F32)
+    half = fg.at_screen
+    packed[0:half, :] = (one[0:half, :] + 1.0) + (one[half : 2 * half, :] + 1.0) * CODE_BASE
+    for row, lane, j, offset, count in pieces(fg.block, fg.domains):
+        at = fg.at_screen + j
+        packed[at : at + 1, offset : offset + count] = screen_ref[row : row + 1, lane : lane + count]
+    table_ref[...] = jnp.broadcast_to(packed[...][None], table_ref.shape)
+
+
+def field_tables(fg, pois_nodes, pois_face, block_owner, screening, after):
+    specs = [pl.BlockSpec(memory_space=pltpu.HBM)] * 4 + [pl.BlockSpec(memory_space=pl.ANY)]
+    lines = screening.reshape(fg.own // LANES, LANES)
     return vmem_call(
         functools.partial(field_tables_kernel, fg),
+        sds((fg.domains, fg.table_rows, LANES), F32),
         [
-            sds((fg.domains, fg.table_rows, LANES), F32),
-            sds((size, size), BF),
-            sds((size, size), BF),
+            pltpu.VMEM(pois_nodes.shape, I32),
+            pltpu.VMEM(pois_face.shape, I32),
+            pltpu.VMEM(block_owner.shape, I32),
+            pltpu.VMEM(lines.shape, F32),
+            pltpu.VMEM((up_to(fg.cells, SUBLANES), fg.size), I32),
+            pltpu.VMEM((up_to(2 * fg.at_screen, SUBLANES), LANES), F32),
+            pltpu.VMEM((fg.table_rows, LANES), F32),
+            pltpu.SemaphoreType.DMA((4,)),
         ],
-        [
-            pltpu.VMEM((up_to(fg.cells, SUBLANES), size), I32),
-            pltpu.VMEM((fg.table_rows, LANES), F32),
-            pltpu.VMEM((size, size), F32),
-        ],
-        cost=cost_of(3.0),
-    )(pois_nodes, pois_face, block_owner, screening.reshape(fg.domains, fg.block), pois_matrix)
+        in_specs=specs,
+        cost=cost_of(1.5),
+    )(*in_hbm(pois_nodes, pois_face, block_owner, lines), after)
 
 
 def lanes_of(values, index):
     return jnp.take_along_axis(values, index, axis=1, mode="promise_in_bounds")
 
 
-def field_solve(fg, dens_ref, table_ref, high_ref, low_ref, codes, rows):
+def field_solve(fg, dens_ref, table_ref, matrix_ref, high_ref, low_ref, codes, rows, copies):
     domains, cells = fg.domains, fg.cells
     bands = dens_ref.shape[0] // domains
     valid = lax.broadcasted_iota(I32, (domains, LANES), 1) < fg.block
 
-    def table(at):
-        return table_ref[:, at, :]
-
-    for at in range(fg.at_owner):
-        codes[at] = table(at).astype(I32)
-    owner = table(fg.at_owner)
+    half = fg.at_screen
+    for at in range(half):
+        both = table_ref[:, at, :].astype(I32)
+        codes[at] = jnp.bitwise_and(both, CODE_BASE - 1) - 1
+        codes[half + at] = jnp.right_shift(both, CODE_BITS) - 1
+    owner = codes[fg.at_owner].astype(F32)
     part = lax.broadcasted_iota(I32, (domains, LANES), 0).astype(F32)
     source = []
     for q in range(domains):
@@ -438,7 +546,7 @@
             who = jnp.broadcast_to(owner[q : q + 1, j : j + 1], (domains, LANES))
             placed = placed + jnp.where(who == part, jnp.broadcast_to(density[j : j + 1, :], (domains, LANES)), 0.0)
         source.append(placed)
-    screen = [table(fg.at_screen + q) for q in range(domains)]
+    screen = [table_ref[:, fg.at_screen + q, :] for q in range(domains)]
 
     def lookup(sources, code):
         lane = jnp.bitwise_and(code, LANES - 1)
@@ -456,16 +564,24 @@
         for c in range(cells):
             for r in range(fg.rows):
                 rows[c * domains : (c + 1) * domains, r * LANES : (r + 1) * LANES] = lookup(local, codes[c * fg.rows + r])
-        picked = rows[...]
+        if copies:
+            copies.pop().wait()
+            full = matrix_ref[...]
+            top = full.astype(BF)
+            high_ref[...] = top
+            low_ref[...] = (full - top.astype(F32)).astype(BF)
+        picked = rows[:, 0 : fg.npc]
         high = picked.astype(BF)
         low = (picked - high.astype(F32)).astype(BF)
-        product = dot(high, high_ref[...]) + (dot(low, high_ref[...]) + dot(high, low_ref[...]))
+        both = dot(jnp.concatenate([high, low], axis=0), high_ref[...])
+        half_rows = cells * domains
+        rows[:, 0 : fg.npc] = both[:half_rows] + (both[half_rows:] + dot(high, low_ref[...]))
         out = []
         for b in range(fg.blocks):
             total = None
             for c in range(cells):
                 sources = [
-                    product[c * domains : (c + 1) * domains, r * LANES : (r + 1) * LANES]
+                    rows[c * domains : (c + 1) * domains, r * LANES : (r + 1) * LANES]
                     for r in range(fg.rows)
                 ]
                 term = lookup(sources, codes[fg.at_inverse + c * fg.blocks + b])
@@ -488,47 +604,42 @@
     return [(x + y) + z for x, y, z in zip(step_one, step_two, step_three)]
 
 
-def field_kernel(geo, fg, scale, *refs):
-    refs = list(refs)
-    n = len(geo.touching)
-    dens_ref, table_ref, high_ref, low_ref, owner_ref = refs[:5]
-    base_ref, up_ref, dn_ref, y_ref = refs[5:9]
-    refs = refs[9:]
-    crosses, refs = refs[:n], refs[n:]
-    behinds, refs = refs[:n], refs[n:]
-    z_ref, dn_out, up_out, column_ref, hartree_ref = refs[:5]
-    codes, rows, phi = refs[5:]
-    blocks = field_solve(fg, dens_ref, table_ref, high_ref, low_ref, codes, rows)
+def field_kernel(fg, dens_ref, table_ref, matrix_hbm, owner_ref, column_ref, hartree_ref, codes, rows, phi, mine, matrix_ref, high_ref, low_ref, sems):
+    copies = fetch([(matrix_hbm, matrix_ref)], sems)
+    blocks = field_solve(fg, dens_ref, table_ref, matrix_ref, high_ref, low_ref, codes, rows, copies)
     for q in range(fg.domains):
         phi[q] = blocks[q]
     here = lax.axis_index("domain")
     for j in range(fg.domains):
-        hartree_ref[j : j + 1, :] = phi[here, pl.ds(owner_ref[0, j], 1), :]
+        mine[j : j + 1, :] = phi[here, pl.ds(owner_ref[0, j], 1), :]
     for j in range(fg.domains):
-        column = column_of(hartree_ref[j : j + 1, :])
+        column = column_of(mine[j : j + 1, :])
         column_ref[j * fg.block : (j + 1) * fg.block, :] = column[0 : fg.block, :]
-    z_ref[...] = base_ref[...] + (column_ref[...] * scale) * y_ref[...]
-    add_halo(geo, scale, z_ref, up_ref, dn_ref, crosses, behinds, [], None)
-    write_sends(geo, z_ref, dn_out, up_out)
-
-
-def field_step(geo, fg, scale, dens, table, high, low, block_owner, base, halo, y, crosses, behinds):
-    columns = y.shape[1]
+    for row, lane, j, offset, count in pieces(fg.block, fg.domains):
+        hartree_ref[row : row + 1, lane : lane + count] = mine[j : j + 1, offset : offset + count]
+
+
+def field_step(fg, dens, table, matrix, block_owner):
     vmem = pl.BlockSpec(memory_space=pltpu.VMEM)
-    args = [dens, table, high, low, block_owner, base, halo[0], halo[1], y, *crosses, *behinds]
-    specs = [vmem] * len(args)
-    specs[4] = pl.BlockSpec(memory_space=pltpu.SMEM)
+    tile = (fg.domains, LANES)
     return vmem_call(
-        functools.partial(field_kernel, geo, fg, scale),
-        [sds(y.shape, F32), *send_shapes(geo, columns), sds((geo.own, LANES), F32), sds((fg.domains, LANES), F32)],
+        functools.partial(field_kernel, fg),
+        [sds((fg.own, LANES), F32), sds((fg.own // LANES, LANES), F32)],
         [
-            pltpu.VMEM((fg.at_owner, fg.domains, LANES), I32),
-            pltpu.VMEM((fg.cells * fg.domains, fg.rows * LANES), F32),
-            pltpu.VMEM((fg.domains, fg.domains, LANES), F32),
+            pltpu.VMEM((2 * fg.at_screen, *tile), I32),
+            pltpu.VMEM((fg.cells * fg.domains, fg.size), F32),
+            pltpu.VMEM((fg.domains, *tile), F32),
+            pltpu.VMEM(tile, F32),
+            pltpu.VMEM(matrix.shape, F32),
+            pltpu.VMEM(matrix.shape, BF),
+            pltpu.VMEM(matrix.shape, BF),
+            pltpu.SemaphoreType.DMA((1,)),
         ],
-        in_specs=specs,
-        cost=cost_of(5.0),
-    )(*args)
+        in_specs=[vmem] * 2
+        + [pl.BlockSpec(memory_space=pltpu.HBM)]
+        + [pl.BlockSpec(memory_space=pltpu.SMEM)],
+        cost=cost_of(4.0),
+    )(dens, table, *in_hbm(matrix), block_owner)
 
 
 def assembled(owned_rows, face_row, terms):
@@ -598,7 +709,7 @@
     return h_up, h_dn
 
 
-def per_device(
+def on_device(
     orbitals,
     potential,
     occupation,
@@ -618,26 +729,24 @@
     fg = FieldGeometry(domains, own, pois_face.shape[1], pois_nodes.shape[0], pois_nodes.shape[1])
     first, later = 1.0 / filter_half, 2.0 / filter_half
 
-    sends = pack(geo, orbitals)
+    *sends, y0 = pack(geo, orbitals, cell_nodes, face_order)
     halo = exchange(sends)
-    behind_nodes = from_behind(cell_nodes, "domain", 1)
-    behind_face = from_behind(face_order, "domain", 1)
     mats, crosses, pot = own_matrices(geo, cell_nodes, face_order, cell_matrix, potential)
+    base = owned_part(geo, first, y0, None, pot, None, mats, ())
+    behinds, uppers = behind_matrices(geo, halo[1], cell_matrix)
+    y1, *sends1 = finish(geo, first, base, halo, crosses, behinds, uppers, sends[1])
+
+    halo = exchange(sends1)
+    base = owned_part(geo, later, y1, y0, pot, None, mats, uppers)
     if fg.fits:
-        table, high, low = field_tables(fg, pois_nodes, pois_face, block_owner, screening, pois_matrix)
-        tables = lax.all_to_all(table, "domain", 0, 0, tiled=True)
-
-    base = owned_part(geo, first, orbitals, None, pot, None, mats, ())
-    behinds, uppers = behind_matrices(geo, behind_nodes, behind_face, cell_matrix)
-    y1, *sends1 = finish(geo, first, base, halo, crosses, behinds, uppers, sends[1])
-
-    halo = exchange(sends1)
-    base = owned_part(geo, later, y1, orbitals, pot, None, mats, uppers)
+        table = field_tables(fg, pois_nodes, pois_face, block_owner, screening, base)
     y2, *sends2 = finish(geo, later, base, halo, crosses, behinds)
 
     halo = exchange(sends2)
     base = owned_part(geo, later, y2, y1, pot, None, mats, uppers)
     if fg.fits:
+        table, base = lax.optimization_barrier((table, base))
+        tables = lax.all_to_all(table, "domain", 0, 0, tiled=True)
         parts = (domains * bands, domains, LANES)
         y3, dn, up, spread = finish(
             geo, later, base, halo, crosses, behinds, occ=occupation.reshape(1, columns), parts=parts
@@ -645,11 +754,9 @@
         dens = lax.all_to_all(spread, ("band", "domain"), 0, 0, tiled=True)
         halo = exchange((dn, up))
         base = owned_part(geo, first, y3, None, pot, None, mats, uppers)
-        z1, dn, up, column, packed = field_step(
-            geo, fg, first, dens, tables, high, low, block_owner, base, halo, y3, crosses, behinds
-        )
-        hartree = packed[:, : fg.block].reshape(own)
-        sends4 = (dn, up)
+        column, packed = field_step(fg, dens, tables, pois_matrix, block_owner)
+        hartree = packed.reshape(own)
+        z1, *sends4 = finish(geo, first, base, halo, crosses, behinds, field=(column, y3))
     else:
         y3, *sends3 = finish(geo, later, base, halo, crosses, behinds)
         halo = exchange(sends3)
@@ -668,7 +775,7 @@
 
 def solution(mesh):
     return jax.shard_map(
-        per_device,
+        on_device,
         mesh=mesh,
         in_specs=(
             P("domain", "band"),

time: 70.8 us -> 56.7 us (0.80)
  local copies, waits for them, and re-layouts: 13.5 us -> 0.02 us
  Pallas kernels: 14.8 us -> 18.1 us
  starting transfers between devices: 29.2 us -> 26 us
    unnamed x38 -> x6, local copies, waits for them, and re-layouts: 12.1 us -> 0.02 us
    ppermute x12 -> x10, waiting for transfers between devices: 11.9 us -> 7.18 us  [from_behind(): lax.ppermute(array, axis, [(i, (i + by) % length) for i in range(length)])]
    all_to_all x2, waiting for transfers between devices: 0.01 us -> 4.16 us  [the longest x1 4.16 us: on_device(): dens = lax.all_to_all(spread, ('band', 'domain'), 0, 0, tiled=True)]
    all_to_all x2, starting transfers between devices: 11 us -> 7.02 us  [the longest x1 3.78 us: on_device(): tables = lax.all_to_all(table, 'domain', 0, 0, tiled=True)]
    pallas_call x5, Pallas kernels: 9.36 us -> 12.4 us  [the longest x1 5.07 us: field_step(): vmem_call(functools.partial(field_kernel, fg), [sds((fg.own, LANES), F32)...]
    reshape x2 -> x0, local copies, waits for them, and re-layouts: 1.42 us -> none  [the longest x1 0.76 us: field_tables(): screening.reshape(fg.domains, fg.block)]
    ppermute x12 -> x10, starting transfers between devices: 18.2 us -> 19 us  [from_behind(): lax.ppermute(array, axis, [(i, (i + by) % length) for i in range(length)])]
    pallas_call x4 -> x5, Pallas kernels: 3.03 us -> 3.33 us  [finish(): vmem_call(functools.partial(finish_kernel, geo, scale, bool(uppers), mode...]
  transfers between devices with their start and end apart: 14 -> 12, of which waited for: 8 -> 6; matrix products, arithmetic and copies ran while one was open for 1% -> 0% of each run, Pallas kernels for 11% -> 26%
where the time goes in v3:
time: 56.7 us; the launch traced here: 56.3 us
  starting transfers between devices  26 us (46%)
  Pallas kernels  18.1 us (32%)
  waiting for transfers between devices  11.3 us (20%)
  between operations  0.82 us (1%)
    ppermute x10, starting transfers between devices, from_behind(): lax.ppermute(array, axis, [(i, (i + by) % length) for i in range(length)])  19 us
    ppermute x10, waiting for transfers between devices, from_behind(): lax.ppermute(array, axis, [(i, (i + by) % length) for i in range(length)])  7.18 us
    pallas_call x1, Pallas kernels, field_step(): vmem_call(functools.partial(field_kernel, fg), [sds((fg.own, LANES), F32)...  5.07 us
    all_to_all x1, waiting for transfers between devices, on_device(): dens = lax.all_to_all(spread, ('band', 'domain'), 0, 0, tiled=True)  4.16 us
    all_to_all x1, starting transfers between devices, on_device(): tables = lax.all_to_all(table, 'domain', 0, 0, tiled=True)  3.78 us
    pallas_call x5, Pallas kernels, finish(): vmem_call(functools.partial(finish_kernel, geo, scale, bool(uppers), mode...  3.33 us
    all_to_all x1, starting transfers between devices, on_device(): dens = lax.all_to_all(spread, ('band', 'domain'), 0, 0, tiled=True)  3.25 us
    pallas_call x1, Pallas kernels, own_matrices(): vmem_call(functools.partial(own_matrices_kernel, geo), shapes, [pltpu.VME...  3 us
  transfers between devices with their start and end apart: 12, of which 6 were waited for; matrix products, arithmetic and copies ran while one was open for 0% of the time, Pallas kernels for 26%

profile of v3, /device:TPU:0, one launch (start us, length us, event | category | flops | bytes accessed | tf_op | source)
XLA Modules:
  0.0 56.3 jit_solution(2052839718156129630)
XLA Ops:
  0.6 0.0 copy-start
  0.6 1.2 %shard_map.122 = (bf16[464,128]{1,0:T(8,128)(2,1)S(1)}, bf16[176,128]{1,0:T(8,128)(2,1)S(1)}, f32[768,128]{1,0:T(8,128)S(1)}) custom-call(f32[768,128]{1,0:T(8,128)} %y_hbm.1, s32[4,343]{1,0:T(4,128)} %refs_0_.2, s32[1,169]{1,0:T(1,128)} %refs_1_.3), custom_call_target="tpu_custom_call" | custom-call | bytes 3000000 | tf_op jit(solution)/shard_map/pallas_call | solution.py:264
  1.8 0.5 collective-permute-start.1
  2.4 4.1 %collective-permute-start = (bf16[176,128]{1,0:T(8,128)(2,1)S(1)}, bf16[176,128]{1,0:T(8,128)(2,1)S(1)}, u32[]{:S(2)}, u32[]{:S(2)}) collective-permute-start(bf16[176,128]{1,0:T(8,128)(2,1)S(1)} %get-tuple-element.39.refs_9_), channel_id=1, source_target_pairs={{0,7},{1,0},{2,1},{3,2},{4,3},{5,4},{6,5},{7,6},{8,15},{9,8},{10,9... | collective-permute-start | bytes 135176 | tf_op jit(solution)/shard_map/ppermute | solution.py:32
  6.4 3.0 %shard_map.123 = (bf16[352,352]{1,0:T(8,128)(2,1)S(1)}, bf16[368,368]{1,0:T(8,128)(2,1)S(1)}, bf16[304,304]{1,0:T(8,128)(2,1)S(1)}, bf16[192,192]{1,0:T(8,128)(2...) custom-call(s32[4,343]{1,0:T(4,128)} %refs_0_.2, s32[1,169]{1,0:T(1,128)} %refs_1_.3, ...), custom_call_target="tpu_custom_call" | custom-call | bytes 6000000 | tf_op jit(solution)/shard_map/pallas_call | solution.py:166
  9.5 0.4 shard_map.124.refs_0_
  9.9 0.0 collective-permute-done.1.refs_0_.refs_2_
  9.9 0.0 copy-done
  9.9 1.0 %shard_map.125 = (bf16[176,304]{1,0:T(8,128)(2,1)S(1)}, bf16[176,192]{1,0:T(8,128)(2,1)S(1)}, bf16[176,176]{1,0:T(8,128)(2,1)S(1)}, bf16[176,176]{1,0:T(8,128)(2,1)S(1)}) custom-call(bf16[464,128]{1,0:T(8,128)(2,1)S(1)} %collective-permute-done.1.refs_0_.refs_2_, bf16[343,343]{1,0:T(8,128)(2,1)S(1)} %copy-done), custom_call_target="tpu_custom_call" | custom-call | bytes 3000000 | tf_op jit(solution)/shard_map/pallas_call | solution.py:208
  11.0 0.0 collective-permute-done.refs_1_
  11.0 0.3 shard_map.126
  11.3 0.1 collective-permute-start.3
  11.4 3.5 %collective-permute-start.2 = (bf16[176,128]{1,0:T(8,128)(2,1)S(1)}, bf16[176,128]{1,0:T(8,128)(2,1)S(1)}, u32[]{:S(2)}, u32[]{:S(2)}) collective-permute-start(bf16[176,128]{1,0:T(8,128)(2,1)S(1)} %get-tuple-element.48), channel_id=1, source_target_pairs={{0,7},{1,0},{2,1},{3,2},{4,3},{5,4},{6,5},{7,6},{8,15},{9,8},{10,9... | collective-permute-start | bytes 135176 | tf_op jit(solution)/shard_map/ppermute | solution.py:32
  14.9 0.5 shard_map.127.refs_4_.refs_0_
  15.4 0.0 copy-start.2
  15.4 2.1 %shard_map.128 = f32[8,32,128]{2,1,0:T(8,128)} custom-call(s32[2,729]{1,0:T(2,128)} %refs_0_.3, s32[1,81]{1,0:T(1,128)} %refs_1_.5, s32[1,8]{1,0:T(1,128)} %owner_ref.1, f32[6,128]{1,0:T(8,128)} %bitcast.6, f32[768,128]{1,0:T(8,128)S(1)} %shard_map.127.refs_4_.refs_0_), custom_call_target="tpu_custom_call" | custom-call | bytes 4500000 | tf_op jit(solution)/shard_map/pallas_call | solution.py:505
  17.6 0.0 collective-permute-done.2.refs_1_
  17.6 0.1 collective-permute-done.3.refs_2_
  17.7 0.3 shard_map.129
  18.0 0.5 shard_map.130.refs_0_
  18.5 0.0 copy-start.1
  18.5 3.8 %all-to-all-start.1 = ((f32[8,32,128]{2,1,0:T(8,128)}), f32[8,32,128]{2,1,0:T(8,128)S(1)}, u32[]{:S(2)}, u32[]{:S(2)}) async-start(f32[8,32,128]{2,1,0:T(8,128)} %shard_map.128), calls=%async_computation.1 | async-start | bytes 262144 | tf_op jit(solution)/shard_map/all_to_all | solution.py:749
  22.3 0.5 collective-permute-start.5
  22.8 3.1 %collective-permute-start.4 = (bf16[176,128]{1,0:T(8,128)(2,1)S(1)}, bf16[176,128]{1,0:T(8,128)(2,1)S(1)}, u32[]{:S(2)}, u32[]{:S(2)}) collective-permute-start(bf16[176,128]{1,0:T(8,128)(2,1)S(1)} %get-tuple-element.52), channel_id=1, source_target_pairs={{0,7},{1,0},{2,1},{3,2},{4,3},{5,4},{6,5},{7,6},{8,15},{9,8},{10,9... | collective-permute-start | bytes 135176 | tf_op jit(solution)/shard_map/ppermute | solution.py:32
  25.9 1.7 %collective-permute-done.4.refs_1_ = bf16[176,128]{1,0:T(8,128)(2,1)S(1)} collective-permute-done((bf16[176,128]{1,0:T(8,128)(2,1)S(1)}, bf16[176,128]{1,0:T(8,128)(2,1)S(1)}, u32[]{:S(2)}, u32[]{:S(2)}) %collective-permute-start.4) | collective-permute-done | bytes 45088 | tf_op jit(solution)/shard_map/ppermute | solution.py:32
  27.6 3.4 %collective-permute-done.5.refs_2_ = bf16[416,128]{1,0:T(8,128)(2,1)S(1)} collective-permute-done((bf16[416,128]{1,0:T(8,128)(2,1)S(1)}, bf16[416,128]{1,0:T(8,128)(2,1)S(1)}, u32[]{:S(2)}, u32[]{:S(2)}) %collective-permute-start.5) | collective-permute-done | bytes 106528 | tf_op jit(solution)/shard_map/ppermute | solution.py:32
  31.0 0.0 copy-done.2
  31.0 1.3 %shard_map.131 = (f32[768,128]{1,0:T(8,128)S(1)}, bf16[416,128]{1,0:T(8,128)(2,1)S(1)}, bf16[176,128]{1,0:T(8,128)(2,1)S(1)}, f32[32,8,128]{2,1,0:T(8,128)}) custom-call(f32[768,128]{1,0:T(8,128)S(1)} %shard_map.130.refs_0_, bf16[176,128]{1,0:T(8,128)(2,1)S(1)} %collective-permute-done.4.refs_1_, bf16[416,128]{1,0:T(8,128)(2,1)S(1)} %collective-permute-done.5.refs_2_, ...), custom_call_target="tpu_custom_call" | custom-call | bytes 3000000 | tf_op jit(solution)/shard_map/pallas_call | solution.py:406
  32.3 0.0 all-to-all-done.1.table_ref
  32.4 3.2 %all-to-all-start = ((f32[32,8,128]{2,1,0:T(8,128)}), f32[32,8,128]{2,1,0:T(8,128)S(1)}, u32[]{:S(2)}, u32[]{:S(2)}) async-start(f32[32,8,128]{2,1,0:T(8,128)} %get-tuple-element.57), calls=%async_computation | async-start | bytes 262144 | tf_op jit(solution)/shard_map/all_to_all | solution.py:754
  35.6 0.3 collective-permute-start.7
  35.9 3.3 %collective-permute-start.6 = (bf16[176,128]{1,0:T(8,128)(2,1)S(1)}, bf16[176,128]{1,0:T(8,128)(2,1)S(1)}, u32[]{:S(2)}, u32[]{:S(2)}) collective-permute-start(bf16[176,128]{1,0:T(8,128)(2,1)S(1)} %get-tuple-element.55), channel_id=1, source_target_pairs={{0,7},{1,0},{2,1},{3,2},{4,3},{5,4},{6,5},{7,6},{8,15},{9,8},{10,9... | collective-permute-start | bytes 135176 | tf_op jit(solution)/shard_map/ppermute | solution.py:32
  39.2 0.5 shard_map.132.refs_0_
  39.7 4.2 %all-to-all-done.dens_ref = f32[32,8,128]{2,1,0:T(8,128)S(1)} async-done(((f32[32,8,128]{2,1,0:T(8,128)}), f32[32,8,128]{2,1,0:T(8,128)S(1)}, u32[]{:S(2)}, u32[]{:S(2)}) %all-to-all-start) | async-done | bytes 131104 | tf_op jit(solution)/shard_map/all_to_all | solution.py:754
  43.8 0.0 copy-done.1
  43.9 5.1 %shard_map.133 = (f32[768,128]{1,0:T(8,128)S(1)}, f32[6,128]{1,0:T(8,128)}) custom-call(f32[32,8,128]{2,1,0:T(8,128)S(1)} %all-to-all-done.dens_ref, f32[8,32,128]{2,1,0:T(8,128)S(1)} %all-to-all-done.1.table_ref, f32[729,729]{1,0:T(8,128)} %matrix_hbm.1, s32[1,8]{1,0:T(1,128)S(1)} %copy-done.1), custom_call_target="tpu_custom_call" | custom-call | bytes 12000000 | tf_op jit(solution)/shard_map/pallas_call | solution.py:625
  48.9 0.0 collective-permute-done.6.refs_1_
  48.9 0.0 collective-permute-done.7.refs_2_
  48.9 0.3 shard_map.134
  49.3 0.8 %collective-permute-start.9 = (bf16[416,128]{1,0:T(8,128)(2,1)S(1)}, bf16[416,128]{1,0:T(8,128)(2,1)S(1)}, u32[]{:S(2)}, u32[]{:S(2)}) collective-permute-start(bf16[416,128]{1,0:T(8,128)(2,1)S(1)} %get-tuple-element.62), channel_id=1, source_target_pairs={{0,1},{1,2},{2,3},{3,4},{4,5},{5,6},{6,7},{7,0},{8,9},{9,10},{10,1... | collective-permute-start | bytes 319496 | tf_op jit(solution)/shard_map/ppermute | solution.py:32
  50.1 2.8 %collective-permute-start.8 = (bf16[176,128]{1,0:T(8,128)(2,1)S(1)}, bf16[176,128]{1,0:T(8,128)(2,1)S(1)}, u32[]{:S(2)}, u32[]{:S(2)}) collective-permute-start(bf16[176,128]{1,0:T(8,128)(2,1)S(1)} %get-tuple-element.61), channel_id=1, source_target_pairs={{0,7},{1,0},{2,1},{3,2},{4,3},{5,4},{6,5},{7,6},{8,15},{9,8},{10,9... | collective-permute-start | bytes 135176 | tf_op jit(solution)/shard_map/ppermute | solution.py:32
  52.9 0.5 shard_map.135.refs_0_
  53.4 1.2 %collective-permute-done.8.refs_1_ = bf16[176,128]{1,0:T(8,128)(2,1)S(1)} collective-permute-done((bf16[176,128]{1,0:T(8,128)(2,1)S(1)}, bf16[176,128]{1,0:T(8,128)(2,1)S(1)}, u32[]{:S(2)}, u32[]{:S(2)}) %collective-permute-start.8) | collective-permute-done | bytes 45088 | tf_op jit(solution)/shard_map/ppermute | solution.py:32
  54.6 0.7 %collective-permute-done.9.refs_2_ = bf16[416,128]{1,0:T(8,128)(2,1)S(1)} collective-permute-done((bf16[416,128]{1,0:T(8,128)(2,1)S(1)}, bf16[416,128]{1,0:T(8,128)(2,1)S(1)}, u32[]{:S(2)}, u32[]{:S(2)}) %collective-permute-start.9) | collective-permute-done | bytes 106528 | tf_op jit(solution)/shard_map/ppermute | solution.py:32
  55.2 1.1 %shard_map.136 = f32[768,128]{1,0:T(8,128)} custom-call(f32[768,128]{1,0:T(8,128)S(1)} %shard_map.135.refs_0_, bf16[176,128]{1,0:T(8,128)(2,1)S(1)} %collective-permute-done.8.refs_1_, bf16[416,128]{1,0:T(8,128)(2,1)S(1)} %collective-permute-done.9.refs_2_, bf16[304,176]{1,0:T(8,128)(2,1)S(1)} %get-tuple-element.41.refs_3_, ...), custom_call_target="tpu_custom_call" | custom-call | bytes 3000000 | tf_op jit(solution)/shard_map/pallas_call | solution.py:406
Async XLA Ops:
  0.6 9.3 %copy-start = (bf16[343,343]{1,0:T(8,128)(2,1)S(1)}, bf16[343,343]{1,0:T(8,128)(2,1)}, u32[]{:S(2)}) copy-start(bf16[343,343]{1,0:T(8,128)(2,1)} %refs_1_.4) | copy-start | bytes 705898
  1.8 8.1 %collective-permute-start.1 = (bf16[464,128]{1,0:T(8,128)(2,1)S(1)}, bf16[464,128]{1,0:T(8,128)(2,1)S(1)}, u32[]{:S(2)}, u32[]{:S(2)}) collective-permute-start(bf16[464,128]{1,0:T(8,128)(2,1)S(1)} %get-tuple-element.40), channel_id=1, source_target_pairs={{0,1},{1,2},{2,3},{3,4},{4,5},{5,6},{6,7},{7,0},{8,9},{9,10},{10,1... | collective-permute-start | bytes 356360 | tf_op jit(solution)/shard_map/ppermute | solution.py:32
  2.4 8.6 %collective-permute-start = (bf16[176,128]{1,0:T(8,128)(2,1)S(1)}, bf16[176,128]{1,0:T(8,128)(2,1)S(1)}, u32[]{:S(2)}, u32[]{:S(2)}) collective-permute-start(bf16[176,128]{1,0:T(8,128)(2,1)S(1)} %get-tuple-element.39.refs_9_), channel_id=1, source_target_pairs={{0,7},{1,0},{2,1},{3,2},{4,3},{5,4},{6,5},{7,6},{8,15},{9,8},{10,9... | collective-permute-start | bytes 135176 | tf_op jit(solution)/shard_map/ppermute | solution.py:32
  11.3 6.4 %collective-permute-start.3 = (bf16[416,128]{1,0:T(8,128)(2,1)S(1)}, bf16[416,128]{1,0:T(8,128)(2,1)S(1)}, u32[]{:S(2)}, u32[]{:S(2)}) collective-permute-start(bf16[416,128]{1,0:T(8,128)(2,1)S(1)} %get-tuple-element.49), channel_id=1, source_target_pairs={{0,1},{1,2},{2,3},{3,4},{4,5},{5,6},{6,7},{7,0},{8,9},{9,10},{10,1... | collective-permute-start | bytes 319496 | tf_op jit(solution)/shard_map/ppermute | solution.py:32
  11.4 6.2 %collective-permute-start.2 = (bf16[176,128]{1,0:T(8,128)(2,1)S(1)}, bf16[176,128]{1,0:T(8,128)(2,1)S(1)}, u32[]{:S(2)}, u32[]{:S(2)}) collective-permute-start(bf16[176,128]{1,0:T(8,128)(2,1)S(1)} %get-tuple-element.48), channel_id=1, source_target_pairs={{0,7},{1,0},{2,1},{3,2},{4,3},{5,4},{6,5},{7,6},{8,15},{9,8},{10,9... | collective-permute-start | bytes 135176 | tf_op jit(solution)/shard_map/ppermute | solution.py:32
  15.4 15.6 %copy-start.2 = (f32[128]{0:T(128)S(1)}, f32[128]{0:T(128)}, u32[]{:S(2)}) copy-start(f32[128]{0:T(128)} %param.13) | copy-start | bytes 1540
  18.5 25.3 %copy-start.1 = (s32[1,8]{1,0:T(1,128)S(1)}, s32[1,8]{1,0:T(1,128)}, u32[]{:S(2)}) copy-start(s32[1,8]{1,0:T(1,128)} %owner_ref.1) | copy-start | bytes 100
  18.5 13.8 %all-to-all-start.1 = ((f32[8,32,128]{2,1,0:T(8,128)}), f32[8,32,128]{2,1,0:T(8,128)S(1)}, u32[]{:S(2)}, u32[]{:S(2)}) async-start(f32[8,32,128]{2,1,0:T(8,128)} %shard_map.128), calls=%async_computation.1 | async-start | bytes 262144 | tf_op jit(solution)/shard_map/all_to_all | solution.py:749
  22.3 8.7 %collective-permute-start.5 = (bf16[416,128]{1,0:T(8,128)(2,1)S(1)}, bf16[416,128]{1,0:T(8,128)(2,1)S(1)}, u32[]{:S(2)}, u32[]{:S(2)}) collective-permute-start(bf16[416,128]{1,0:T(8,128)(2,1)S(1)} %get-tuple-element.53), channel_id=1, source_target_pairs={{0,1},{1,2},{2,3},{3,4},{4,5},{5,6},{6,7},{7,0},{8,9},{9,10},{10,1... | collective-permute-start | bytes 319496 | tf_op jit(solution)/shard_map/ppermute | solution.py:32
  22.8 4.8 %collective-permute-start.4 = (bf16[176,128]{1,0:T(8,128)(2,1)S(1)}, bf16[176,128]{1,0:T(8,128)(2,1)S(1)}, u32[]{:S(2)}, u32[]{:S(2)}) collective-permute-start(bf16[176,128]{1,0:T(8,128)(2,1)S(1)} %get-tuple-element.52), channel_id=1, source_target_pairs={{0,7},{1,0},{2,1},{3,2},{4,3},{5,4},{6,5},{7,6},{8,15},{9,8},{10,9... | collective-permute-start | bytes 135176 | tf_op jit(solution)/shard_map/ppermute | solution.py:32
  32.4 11.5 %all-to-all-start = ((f32[32,8,128]{2,1,0:T(8,128)}), f32[32,8,128]{2,1,0:T(8,128)S(1)}, u32[]{:S(2)}, u32[]{:S(2)}) async-start(f32[32,8,128]{2,1,0:T(8,128)} %get-tuple-element.57), calls=%async_computation | async-start | bytes 262144 | tf_op jit(solution)/shard_map/all_to_all | solution.py:754
  35.6 13.3 %collective-permute-start.7 = (bf16[416,128]{1,0:T(8,128)(2,1)S(1)}, bf16[416,128]{1,0:T(8,128)(2,1)S(1)}, u32[]{:S(2)}, u32[]{:S(2)}) collective-permute-start(bf16[416,128]{1,0:T(8,128)(2,1)S(1)} %get-tuple-element.56), channel_id=1, source_target_pairs={{0,1},{1,2},{2,3},{3,4},{4,5},{5,6},{6,7},{7,0},{8,9},{9,10},{10,1... | collective-permute-start | bytes 319496 | tf_op jit(solution)/shard_map/ppermute | solution.py:32
  35.9 13.0 %collective-permute-start.6 = (bf16[176,128]{1,0:T(8,128)(2,1)S(1)}, bf16[176,128]{1,0:T(8,128)(2,1)S(1)}, u32[]{:S(2)}, u32[]{:S(2)}) collective-permute-start(bf16[176,128]{1,0:T(8,128)(2,1)S(1)} %get-tuple-element.55), channel_id=1, source_target_pairs={{0,7},{1,0},{2,1},{3,2},{4,3},{5,4},{6,5},{7,6},{8,15},{9,8},{10,9... | collective-permute-start | bytes 135176 | tf_op jit(solution)/shard_map/ppermute | solution.py:32
  49.3 6.0 %collective-permute-start.9 = (bf16[416,128]{1,0:T(8,128)(2,1)S(1)}, bf16[416,128]{1,0:T(8,128)(2,1)S(1)}, u32[]{:S(2)}, u32[]{:S(2)}) collective-permute-start(bf16[416,128]{1,0:T(8,128)(2,1)S(1)} %get-tuple-element.62), channel_id=1, source_target_pairs={{0,1},{1,2},{2,3},{3,4},{4,5},{5,6},{6,7},{7,0},{8,9},{9,10},{10,1... | collective-permute-start | bytes 319496 | tf_op jit(solution)/shard_map/ppermute | solution.py:32
  50.1 4.5 %collective-permute-start.8 = (bf16[176,128]{1,0:T(8,128)(2,1)S(1)}, bf16[176,128]{1,0:T(8,128)(2,1)S(1)}, u32[]{:S(2)}, u32[]{:S(2)}) collective-permute-start(bf16[176,128]{1,0:T(8,128)(2,1)S(1)} %get-tuple-element.61), channel_id=1, source_target_pairs={{0,7},{1,0},{2,1},{3,2},{4,3},{5,4},{6,5},{7,6},{8,15},{9,8},{10,9... | collective-permute-start | bytes 135176 | tf_op jit(solution)/shard_map/ppermute | solution.py:32

commit v4 on v3

--- a/solution.py
+++ b/solution.py
@@ -137,12 +137,8 @@
 
 
 def own_matrices_kernel(geo, *refs):
-    outs = refs[4:-7]
-    nodes_ref, face_ref, matrix_ref, pot_ref, table, matrix_pad, sems = refs[-7:]
-    copies = fetch(list(zip(refs[:4], (nodes_ref, face_ref, matrix_ref, pot_ref))), sems)
-    for copy in copies:
-        copy.wait()
-    place_table(geo, nodes_ref, face_ref, table)
+    table, matrix_ref, pot_ref = refs[:3]
+    outs, matrix_pad = refs[3:-1], refs[-1]
     matrix = place_matrix(geo, matrix_ref, matrix_pad)
     face = face_of(geo, table)
     for c in range(geo.cells):
@@ -159,25 +155,16 @@
         column[r * LANES : (r + 1) * LANES, :] = row.T
 
 
-def own_matrices(geo, cell_nodes, face_order, cell_matrix, potential):
+def own_matrices(geo, table, cell_matrix, lines):
     shapes = [sds((w.rows, w.rows), BF) for w in geo.windows]
     shapes += [sds((geo.windows[c].rows, geo.sp), BF) for c in geo.touching]
     shapes += [sds((geo.own, LANES), F32)]
     outs = vmem_call(
         functools.partial(own_matrices_kernel, geo),
         shapes,
-        [
-            pltpu.VMEM(cell_nodes.shape, I32),
-            pltpu.VMEM(face_order.shape, I32),
-            pltpu.VMEM(cell_matrix.shape, BF),
-            pltpu.VMEM((geo.own // LANES, LANES), F32),
-            table_scratch(geo),
-            matrix_scratch(geo),
-            pltpu.SemaphoreType.DMA((4,)),
-        ],
-        in_specs=[pl.BlockSpec(memory_space=pltpu.HBM)] * 4,
+        [matrix_scratch(geo)],
         cost=cost_of(2.0),
-    )(*in_hbm(cell_nodes, face_order, cell_matrix, potential.reshape(geo.own // LANES, LANES)))
+    )(table, cell_matrix, lines)
     n = geo.cells
     return outs[:n], outs[n:-1], outs[-1]
 
@@ -237,11 +224,15 @@
     return copies
 
 
-def pack_kernel(geo, y_hbm, nodes_hbm, face_hbm, dn_ref, up_ref, y, nodes, face, table, sems):
+def pack_kernel(geo, extra, y_hbm, nodes_hbm, face_hbm, *refs):
+    sources, refs = refs[:extra], refs[extra:]
+    dn_ref, up_ref, y, table = refs[:4]
+    kept, (nodes, face, sems) = refs[4 : 4 + extra], refs[4 + extra :]
     cuts = sorted({0, max(geo.sp, geo.low), geo.dn_lo, geo.own})
     spans = list(zip(cuts[:-1], cuts[1:]))
     pairs = [(nodes_hbm, nodes), (face_hbm, face)]
     pairs += [(y_hbm.at[pl.ds(a, b - a)], y.at[pl.ds(a, b - a)]) for a, b in spans]
+    pairs += list(zip(sources, kept))
     copies = fetch(pairs, sems)
     copies[0].wait()
     copies[1].wait()
@@ -258,21 +249,27 @@
     write_sends(geo, y, dn_ref, up_ref)
 
 
-def pack(geo, y, cell_nodes, face_order):
-    _, up = send_shapes(geo, y.shape[1])
+def pack(geo, y, cell_nodes, face_order, *others):
+    dn, up = send_shapes(geo, y.shape[1])
     rows = geo.dn_rows + 2 * geo.table_rows * geo.table_tiles
-    return vmem_call(
-        functools.partial(pack_kernel, geo),
-        [sds((rows, y.shape[1]), BF), up, sds(y.shape, F32)],
+    dn, up, y, table, *others = vmem_call(
+        functools.partial(pack_kernel, geo, len(others)),
+        [
+            sds((rows, y.shape[1]), BF),
+            up,
+            sds(y.shape, F32),
+            sds((geo.table_rows, geo.table_lanes), I32),
+            *[sds(a.shape, a.dtype) for a in others],
+        ],
         [
             pltpu.VMEM(cell_nodes.shape, I32),
             pltpu.VMEM(face_order.shape, I32),
-            table_scratch(geo),
-            pltpu.SemaphoreType.DMA((5,)),
+            pltpu.SemaphoreType.DMA((5 + len(others),)),
         ],
-        in_specs=[pl.BlockSpec(memory_space=pltpu.HBM)] * 3,
+        in_specs=[pl.BlockSpec(memory_space=pltpu.HBM)] * (3 + len(others)),
         cost=cost_of(1.0),
-    )(*in_hbm(y, cell_nodes, face_order))
+    )(*in_hbm(y, cell_nodes, face_order, *others))
+    return (dn, up), y, table, others
 
 
 def owned_part_kernel(geo, scale, has_prev, has_field, has_upper, *refs):
@@ -455,11 +452,8 @@
 
 
 def field_tables_kernel(fg, *refs):
-    sources, table_ref = refs[:4], refs[5]
-    nodes_ref, face_ref, owner_ref, screen_ref, pad, one, packed, sems = refs[6:]
-    copies = fetch(list(zip(sources, (nodes_ref, face_ref, owner_ref, screen_ref))), sems)
-    for copy in copies:
-        copy.wait()
+    nodes_ref, face_ref, owner_ref, screen_ref = refs[:4]
+    table_ref, pad, one, packed = refs[5:]
     one[...] = jnp.full(one.shape, -1.0, F32)
     pad[...] = jnp.full(pad.shape, -1, I32)
     pad[0 : fg.cells, 0 : fg.npc] = nodes_ref[...]
@@ -499,54 +493,81 @@
     table_ref[...] = jnp.broadcast_to(packed[...][None], table_ref.shape)
 
 
-def field_tables(fg, pois_nodes, pois_face, block_owner, screening, after):
-    specs = [pl.BlockSpec(memory_space=pltpu.HBM)] * 4 + [pl.BlockSpec(memory_space=pl.ANY)]
-    lines = screening.reshape(fg.own // LANES, LANES)
+def field_tables(fg, pois_nodes, pois_face, block_owner, lines, after):
+    specs = [pl.BlockSpec(memory_space=pltpu.VMEM)] * 4 + [pl.BlockSpec(memory_space=pl.ANY)]
     return vmem_call(
         functools.partial(field_tables_kernel, fg),
         sds((fg.domains, fg.table_rows, LANES), F32),
         [
-            pltpu.VMEM(pois_nodes.shape, I32),
-            pltpu.VMEM(pois_face.shape, I32),
-            pltpu.VMEM(block_owner.shape, I32),
-            pltpu.VMEM(lines.shape, F32),
             pltpu.VMEM((up_to(fg.cells, SUBLANES), fg.size), I32),
             pltpu.VMEM((up_to(2 * fg.at_screen, SUBLANES), LANES), F32),
             pltpu.VMEM((fg.table_rows, LANES), F32),
-            pltpu.SemaphoreType.DMA((4,)),
         ],
         in_specs=specs,
-        cost=cost_of(1.5),
-    )(*in_hbm(pois_nodes, pois_face, block_owner, lines), after)
+        cost=cost_of(1.0),
+    )(pois_nodes, pois_face, block_owner, lines, after)
 
 
 def lanes_of(values, index):
     return jnp.take_along_axis(values, index, axis=1, mode="promise_in_bounds")
 
 
-def field_solve(fg, dens_ref, table_ref, matrix_ref, high_ref, low_ref, codes, rows, copies):
+def field_codes_kernel(fg, table_ref, codes_ref, screen_ref, lines):
+    domains, half = fg.domains, fg.at_screen
+    for at in range(fg.table_rows):
+        for d in range(domains):
+            lines[at, d : d + 1, :] = table_ref[d, at : at + 1, :]
+    for at in range(half):
+        both = lines[at].astype(I32)
+        for here, code in ((at, jnp.bitwise_and(both, CODE_BASE - 1) - 1), (half + at, jnp.right_shift(both, CODE_BITS) - 1)):
+            if here == fg.at_face_inverse:
+                code = pltpu.roll(code, 1, 0)
+            if here < fg.at_owner:
+                codes_ref[here] = code
+            elif here == fg.at_owner:
+                owner = code.astype(F32)
+    part = lax.broadcasted_iota(I32, (domains, LANES), 0).astype(F32)
+    mine = jnp.zeros((domains, LANES), F32)
+    here = lax.axis_index("domain").astype(F32)
+    for q in range(domains):
+        column = column_of(owner[q : q + 1, :])[0:domains, :]
+        inverse = jnp.zeros((domains, LANES), F32)
+        for j in range(domains):
+            inverse = jnp.where(column[j : j + 1, :] == part, float(j), inverse)
+        codes_ref[fg.at_owner + q] = inverse.astype(I32)
+        mine = jnp.where(here == float(q), column, mine)
+    codes_ref[fg.at_owner + domains] = mine.astype(I32)
+    for q in range(domains):
+        screen_ref[q] = lines[fg.at_screen + q]
+
+
+def field_codes(fg, table):
+    return vmem_call(
+        functools.partial(field_codes_kernel, fg),
+        [
+            sds((fg.at_owner + fg.domains + 1, fg.domains, LANES), I32),
+            sds((fg.domains, fg.domains, LANES), F32),
+        ],
+        [pltpu.VMEM((fg.table_rows, fg.domains, LANES), F32)],
+        cost=cost_of(1.0),
+    )(table)
+
+
+def rows_of(values, index):
+    return jnp.take_along_axis(values, index, axis=0, mode="promise_in_bounds")
+
+
+def field_solve(fg, dens_ref, codes, screen_ref, matrix_ref, high_ref, low_ref, rows, copies):
     domains, cells = fg.domains, fg.cells
     bands = dens_ref.shape[0] // domains
     valid = lax.broadcasted_iota(I32, (domains, LANES), 1) < fg.block
-
-    half = fg.at_screen
-    for at in range(half):
-        both = table_ref[:, at, :].astype(I32)
-        codes[at] = jnp.bitwise_and(both, CODE_BASE - 1) - 1
-        codes[half + at] = jnp.right_shift(both, CODE_BITS) - 1
-    owner = codes[fg.at_owner].astype(F32)
-    part = lax.broadcasted_iota(I32, (domains, LANES), 0).astype(F32)
     source = []
     for q in range(domains):
         density = dens_ref[q]
         for b in range(1, bands):
             density = density + dens_ref[b * domains + q]
-        placed = jnp.zeros((domains, LANES), F32)
-        for j in range(domains):
-            who = jnp.broadcast_to(owner[q : q + 1, j : j + 1], (domains, LANES))
-            placed = placed + jnp.where(who == part, jnp.broadcast_to(density[j : j + 1, :], (domains, LANES)), 0.0)
-        source.append(placed)
-    screen = [table_ref[:, fg.at_screen + q, :] for q in range(domains)]
+        source.append(rows_of(density, codes[fg.at_owner + q]))
+    screen = [screen_ref[q] for q in range(domains)]
 
     def lookup(sources, code):
         lane = jnp.bitwise_and(code, LANES - 1)
@@ -558,8 +579,7 @@
 
     def operator(field):
         ahead = pltpu.roll(field[0], domains - 1, 0)
-        face = codes[fg.at_face]
-        upper = lookup([ahead], face)
+        upper = lookup([ahead], codes[fg.at_face])
         local = list(field) + [upper]
         for c in range(cells):
             for r in range(fg.rows):
@@ -588,8 +608,7 @@
                 total = term if total is None else total + term
             out.append(total)
         arriving = pltpu.roll(out[domains], 1, 0)
-        home = pltpu.roll(codes[fg.at_face_inverse], 1, 0)
-        out[0] = out[0] + lookup([arriving], home)
+        out[0] = out[0] + lookup([arriving], codes[fg.at_face_inverse])
         return [jnp.where(valid, screen[q] * field[q] + out[q], 0.0) for q in range(domains)]
 
     step_one = [s * (1.0 / solve_center) for s in source]
@@ -604,14 +623,13 @@
     return [(x + y) + z for x, y, z in zip(step_one, step_two, step_three)]
 
 
-def field_kernel(fg, dens_ref, table_ref, matrix_hbm, owner_ref, column_ref, hartree_ref, codes, rows, phi, mine, matrix_ref, high_ref, low_ref, sems):
+def field_kernel(fg, dens_ref, codes, screen_ref, matrix_hbm, column_ref, hartree_ref, rows, phi, mine, matrix_ref, high_ref, low_ref, sems):
     copies = fetch([(matrix_hbm, matrix_ref)], sems)
-    blocks = field_solve(fg, dens_ref, table_ref, matrix_ref, high_ref, low_ref, codes, rows, copies)
+    blocks = field_solve(fg, dens_ref, codes, screen_ref, matrix_ref, high_ref, low_ref, rows, copies)
     for q in range(fg.domains):
         phi[q] = blocks[q]
     here = lax.axis_index("domain")
-    for j in range(fg.domains):
-        mine[j : j + 1, :] = phi[here, pl.ds(owner_ref[0, j], 1), :]
+    mine[...] = rows_of(phi[here], codes[fg.at_owner + fg.domains])
     for j in range(fg.domains):
         column = column_of(mine[j : j + 1, :])
         column_ref[j * fg.block : (j + 1) * fg.block, :] = column[0 : fg.block, :]
@@ -619,14 +637,13 @@
         hartree_ref[row : row + 1, lane : lane + count] = mine[j : j + 1, offset : offset + count]
 
 
-def field_step(fg, dens, table, matrix, block_owner):
+def field_step(fg, dens, codes, screen, matrix):
     vmem = pl.BlockSpec(memory_space=pltpu.VMEM)
     tile = (fg.domains, LANES)
     return vmem_call(
         functools.partial(field_kernel, fg),
         [sds((fg.own, LANES), F32), sds((fg.own // LANES, LANES), F32)],
         [
-            pltpu.VMEM((2 * fg.at_screen, *tile), I32),
             pltpu.VMEM((fg.cells * fg.domains, fg.size), F32),
             pltpu.VMEM((fg.domains, *tile), F32),
             pltpu.VMEM(tile, F32),
@@ -635,11 +652,9 @@
             pltpu.VMEM(matrix.shape, BF),
             pltpu.SemaphoreType.DMA((1,)),
         ],
-        in_specs=[vmem] * 2
-        + [pl.BlockSpec(memory_space=pltpu.HBM)]
-        + [pl.BlockSpec(memory_space=pltpu.SMEM)],
+        in_specs=[vmem] * 3 + [pl.BlockSpec(memory_space=pltpu.HBM)],
         cost=cost_of(4.0),
-    )(dens, table, *in_hbm(matrix), block_owner)
+    )(dens, codes, screen, *in_hbm(matrix))
 
 
 def assembled(owned_rows, face_row, terms):
@@ -729,32 +744,37 @@
     fg = FieldGeometry(domains, own, pois_face.shape[1], pois_nodes.shape[0], pois_nodes.shape[1])
     first, later = 1.0 / filter_half, 2.0 / filter_half
 
-    *sends, y0 = pack(geo, orbitals, cell_nodes, face_order)
+    others = [cell_matrix, potential.reshape(own // LANES, LANES)]
+    if fg.fits:
+        others += [pois_nodes, pois_face, block_owner, screening.reshape(own // LANES, LANES)]
+        others.append(occupation.reshape(1, columns))
+    sends, y0, nodes, (matrix, lines, *others) = pack(geo, orbitals, cell_nodes, face_order, *others)
     halo = exchange(sends)
-    mats, crosses, pot = own_matrices(geo, cell_nodes, face_order, cell_matrix, potential)
+    mats, crosses, pot = own_matrices(geo, nodes, matrix, lines)
     base = owned_part(geo, first, y0, None, pot, None, mats, ())
-    behinds, uppers = behind_matrices(geo, halo[1], cell_matrix)
+    behinds, uppers = behind_matrices(geo, halo[1], matrix)
     y1, *sends1 = finish(geo, first, base, halo, crosses, behinds, uppers, sends[1])
 
     halo = exchange(sends1)
     base = owned_part(geo, later, y1, y0, pot, None, mats, uppers)
     if fg.fits:
-        table = field_tables(fg, pois_nodes, pois_face, block_owner, screening, base)
+        *others, weights = others
+        table = field_tables(fg, *others, base)
+        tables = lax.all_to_all(table, "domain", 0, 0, tiled=True)
     y2, *sends2 = finish(geo, later, base, halo, crosses, behinds)
 
     halo = exchange(sends2)
     base = owned_part(geo, later, y2, y1, pot, None, mats, uppers)
     if fg.fits:
-        table, base = lax.optimization_barrier((table, base))
-        tables = lax.all_to_all(table, "domain", 0, 0, tiled=True)
         parts = (domains * bands, domains, LANES)
         y3, dn, up, spread = finish(
-            geo, later, base, halo, crosses, behinds, occ=occupation.reshape(1, columns), parts=parts
+            geo, later, base, halo, crosses, behinds, occ=weights, parts=parts
         )
         dens = lax.all_to_all(spread, ("band", "domain"), 0, 0, tiled=True)
         halo = exchange((dn, up))
         base = owned_part(geo, first, y3, None, pot, None, mats, uppers)
-        column, packed = field_step(fg, dens, tables, pois_matrix, block_owner)
+        codes, screen = field_codes(fg, tables)
+        column, packed = field_step(fg, dens, codes, screen, pois_matrix)
         hartree = packed.reshape(own)
         z1, *sends4 = finish(geo, first, base, halo, crosses, behinds, field=(column, y3))
     else:

time: 56.7 us -> 58 us (1.023)
  Pallas kernels: 18.1 us -> 16 us
  starting transfers between devices: 26 us -> 27.9 us
  waiting for transfers between devices: 11.3 us -> 12.9 us
    all_to_all x1, starting transfers between devices: 3.25 us -> 5.47 us  [on_device(): dens = lax.all_to_all(spread, ('band', 'domain'), 0, 0, tiled=True)]
    ppermute x10, waiting for transfers between devices: 7.18 us -> 9.03 us  [from_behind(): lax.ppermute(array, axis, [(i, (i + by) % length) for i in range(length)])]
    pallas_call x1, Pallas kernels: 2.12 us -> 1.36 us  [field_tables(): vmem_call(functools.partial(field_tables_kernel, fg), sds((fg.domains, fg...]
    pallas_call x1, Pallas kernels: 5.07 us -> 4.35 us  [field_step(): vmem_call(functools.partial(field_kernel, fg), [sds((fg.own, LANES), F32)...]
    pallas_call x2 -> x3, Pallas kernels: 4.16 us -> 3.53 us  [the longest x1 1.98 us: own_matrices(): vmem_call(functools.partial(own_matrices_kernel, geo), shapes, [matrix_sc...]
  transfers between devices with their start and end apart: 12 -> 12, of which waited for: 6 -> 8; matrix products, arithmetic and copies ran while one was open for 0% -> 0% of each run, Pallas kernels for 26% -> 19%
where the time goes in v4:
time: 58 us; the launch traced here: 57.6 us
  starting transfers between devices  27.9 us (48%)
  Pallas kernels  16 us (28%)
  waiting for transfers between devices  12.9 us (22%)
  between operations  0.77 us (1%)
    ppermute x10, starting transfers between devices, from_behind(): lax.ppermute(array, axis, [(i, (i + by) % length) for i in range(length)])  19 us
    ppermute x10, waiting for transfers between devices, from_behind(): lax.ppermute(array, axis, [(i, (i + by) % length) for i in range(length)])  9.03 us
    all_to_all x1, starting transfers between devices, on_device(): dens = lax.all_to_all(spread, ('band', 'domain'), 0, 0, tiled=True)  5.47 us
    pallas_call x1, Pallas kernels, field_step(): vmem_call(functools.partial(field_kernel, fg), [sds((fg.own, LANES), F32)...  4.35 us
    all_to_all x1, waiting for transfers between devices, on_device(): dens = lax.all_to_all(spread, ('band', 'domain'), 0, 0, tiled=True)  3.91 us
    all_to_all x1, starting transfers between devices, on_device(): tables = lax.all_to_all(table, 'domain', 0, 0, tiled=True)  3.5 us
    pallas_call x5, Pallas kernels, finish(): vmem_call(functools.partial(finish_kernel, geo, scale, bool(uppers), mode...  3.31 us
    pallas_call x5, Pallas kernels, owned_part(): vmem_call(functools.partial(owned_part_kernel, geo, scale, prev is not No...  2.4 us
  transfers between devices with their start and end apart: 12, of which 8 were waited for; matrix products, arithmetic and copies ran while one was open for 0% of the time, Pallas kernels for 19%

profile of v4, /device:TPU:0, one launch (start us, length us, event | category | flops | bytes accessed | tf_op | source)
XLA Modules:
  0.0 57.6 jit_solution(14523123424994780619)
XLA Ops:
  0.6 1.3 %shard_map.122 = (bf16[464,128]{1,0:T(8,128)(2,1)S(1)}, bf16[176,128]{1,0:T(8,128)(2,1)S(1)}, f32[768,128]{1,0:T(8,128)S(1)}, s32[8,384]{1,0:T(8,128)S(1)}, bf16...) custom-call(f32[768,128]{1,0:T(8,128)} %y_hbm.1, ...), custom_call_target="tpu_custom_call" | custom-call | bytes 3000000 | tf_op jit(solution)/shard_map/pallas_call | solution.py:255
  1.9 0.5 collective-permute-start.1
  2.5 4.1 %collective-permute-start = (bf16[176,128]{1,0:T(8,128)(2,1)S(1)}, bf16[176,128]{1,0:T(8,128)(2,1)S(1)}, u32[]{:S(2)}, u32[]{:S(2)}) collective-permute-start(bf16[176,128]{1,0:T(8,128)(2,1)S(1)} %get-tuple-element.50.refs_9_), channel_id=1, source_target_pairs={{0,7},{1,0},{2,1},{3,2},{4,3},{5,4},{6,5},{7,6},{8,15},{9,8},{10,9... | collective-permute-start | bytes 135176 | tf_op jit(solution)/shard_map/ppermute | solution.py:32
  6.6 2.0 %shard_map.123 = (bf16[352,352]{1,0:T(8,128)(2,1)S(1)}, bf16[368,368]{1,0:T(8,128)(2,1)S(1)}, bf16[304,304]{1,0:T(8,128)(2,1)S(1)}, bf16[192,192]{1,0:T(8,128)(2...) custom-call(s32[8,384]{1,0:T(8,128)S(1)} %get-tuple-element.42.refs_0_, ...), custom_call_target="tpu_custom_call" | custom-call | bytes 6000000 | tf_op jit(solution)/shard_map/pallas_call | solution.py:162
  8.6 0.4 shard_map.124.refs_0_
  9.0 0.1 collective-permute-done.1.refs_0_.refs_2_
  9.1 1.0 %shard_map.125 = (bf16[176,304]{1,0:T(8,128)(2,1)S(1)}, bf16[176,192]{1,0:T(8,128)(2,1)S(1)}, bf16[176,176]{1,0:T(8,128)(2,1)S(1)}, bf16[176,176]{1,0:T(8,128)(2,1)S(1)}) custom-call(bf16[464,128]{1,0:T(8,128)(2,1)S(1)} %collective-permute-done.1.refs_0_.refs_2_, bf16[343,343]{1,0:T(8,128)(2,1)S(1)} %get-tuple-element.43.refs_1_), custom_call_target="tpu_custom_call" | custom-call | bytes 3000000 | tf_op jit(solution)/shard_map/pallas_call | solution.py:195
  10.2 0.0 collective-permute-done.refs_1_
  10.2 0.3 shard_map.126
  10.5 0.5 shard_map.127.refs_0_.refs_4_
  11.0 1.4 %shard_map.132 = f32[8,32,128]{2,1,0:T(8,128)} custom-call(s32[2,729]{1,0:T(2,128)S(1)} %get-tuple-element.69.refs_0_, s32[1,81]{1,0:T(1,128)S(1)} %get-tuple-element.70.refs_1_, s32[1,8]{1,0:T(1,128)S(1)} %get-tuple-element.71.refs_2_, f32[6,128]{1,0:T(8,128)S(1)} %get-tuple-element.72.refs_3_, f32[768,128]{1,0:T(8,128)S(1)} %shard_map.127.refs_0_.refs_4_), custom_call_target="tpu_custom_call" | custom-call | bytes 3000000 | tf_op jit(solution)/shard_map/pallas_call | solution.py:498
  12.4 3.5 %all-to-all-start.1 = ((f32[8,32,128]{2,1,0:T(8,128)}), f32[8,32,128]{2,1,0:T(8,128)S(1)}, u32[]{:S(2)}, u32[]{:S(2)}) async-start(f32[8,32,128]{2,1,0:T(8,128)} %shard_map.132), calls=%async_computation.1 | async-start | bytes 262144 | tf_op jit(solution)/shard_map/all_to_all | solution.py:763
  15.9 0.5 collective-permute-start.3
  16.4 3.1 %collective-permute-start.2 = (bf16[176,128]{1,0:T(8,128)(2,1)S(1)}, bf16[176,128]{1,0:T(8,128)(2,1)S(1)}, u32[]{:S(2)}, u32[]{:S(2)}) collective-permute-start(bf16[176,128]{1,0:T(8,128)(2,1)S(1)} %get-tuple-element.59), channel_id=1, source_target_pairs={{0,7},{1,0},{2,1},{3,2},{4,3},{5,4},{6,5},{7,6},{8,15},{9,8},{10,9... | collective-permute-start | bytes 135176 | tf_op jit(solution)/shard_map/ppermute | solution.py:32
  19.4 1.7 %collective-permute-done.2.refs_1_ = bf16[176,128]{1,0:T(8,128)(2,1)S(1)} collective-permute-done((bf16[176,128]{1,0:T(8,128)(2,1)S(1)}, bf16[176,128]{1,0:T(8,128)(2,1)S(1)}, u32[]{:S(2)}, u32[]{:S(2)}) %collective-permute-start.2) | collective-permute-done | bytes 45088 | tf_op jit(solution)/shard_map/ppermute | solution.py:32
  21.1 3.4 %collective-permute-done.3.refs_2_ = bf16[416,128]{1,0:T(8,128)(2,1)S(1)} collective-permute-done((bf16[416,128]{1,0:T(8,128)(2,1)S(1)}, bf16[416,128]{1,0:T(8,128)(2,1)S(1)}, u32[]{:S(2)}, u32[]{:S(2)}) %collective-permute-start.3) | collective-permute-done | bytes 106528 | tf_op jit(solution)/shard_map/ppermute | solution.py:32
  24.6 0.3 shard_map.128
  24.9 0.1 collective-permute-start.5
  25.0 3.5 %collective-permute-start.4 = (bf16[176,128]{1,0:T(8,128)(2,1)S(1)}, bf16[176,128]{1,0:T(8,128)(2,1)S(1)}, u32[]{:S(2)}, u32[]{:S(2)}) collective-permute-start(bf16[176,128]{1,0:T(8,128)(2,1)S(1)} %get-tuple-element.62), channel_id=1, source_target_pairs={{0,7},{1,0},{2,1},{3,2},{4,3},{5,4},{6,5},{7,6},{8,15},{9,8},{10,9... | collective-permute-start | bytes 135176 | tf_op jit(solution)/shard_map/ppermute | solution.py:32
  28.5 0.5 shard_map.129.refs_0_
  29.0 1.2 %collective-permute-done.4.refs_1_ = bf16[176,128]{1,0:T(8,128)(2,1)S(1)} collective-permute-done((bf16[176,128]{1,0:T(8,128)(2,1)S(1)}, bf16[176,128]{1,0:T(8,128)(2,1)S(1)}, u32[]{:S(2)}, u32[]{:S(2)}) %collective-permute-start.4) | collective-permute-done | bytes 45088 | tf_op jit(solution)/shard_map/ppermute | solution.py:32
  30.2 0.7 %collective-permute-done.5.refs_2_ = bf16[416,128]{1,0:T(8,128)(2,1)S(1)} collective-permute-done((bf16[416,128]{1,0:T(8,128)(2,1)S(1)}, bf16[416,128]{1,0:T(8,128)(2,1)S(1)}, u32[]{:S(2)}, u32[]{:S(2)}) %collective-permute-start.5) | collective-permute-done | bytes 106528 | tf_op jit(solution)/shard_map/ppermute | solution.py:32
  30.9 1.3 %shard_map.130 = (f32[768,128]{1,0:T(8,128)S(1)}, bf16[416,128]{1,0:T(8,128)(2,1)S(1)}, bf16[176,128]{1,0:T(8,128)(2,1)S(1)}, f32[32,8,128]{2,1,0:T(8,128)}) custom-call(f32[768,128]{1,0:T(8,128)S(1)} %shard_map.129.refs_0_, bf16[176,128]{1,0:T(8,128)(2,1)S(1)} %collective-permute-done.4.refs_1_, bf16[416,128]{1,0:T(8,128)(2,1)S(1)} %collective-permute-done.5.refs_2_, ...), custom_call_target="tpu_custom_call" | custom-call | bytes 3000000 | tf_op jit(solution)/shard_map/pallas_call | solution.py:403
  32.2 0.0 all-to-all-done.1.table_ref
  32.2 5.5 %all-to-all-start = ((f32[32,8,128]{2,1,0:T(8,128)}), f32[32,8,128]{2,1,0:T(8,128)S(1)}, u32[]{:S(2)}, u32[]{:S(2)}) async-start(f32[32,8,128]{2,1,0:T(8,128)} %get-tuple-element.68), calls=%async_computation | async-start | bytes 262144 | tf_op jit(solution)/shard_map/all_to_all | solution.py:773
  37.7 0.3 collective-permute-start.7
  38.0 3.3 %collective-permute-start.6 = (bf16[176,128]{1,0:T(8,128)(2,1)S(1)}, bf16[176,128]{1,0:T(8,128)(2,1)S(1)}, u32[]{:S(2)}, u32[]{:S(2)}) collective-permute-start(bf16[176,128]{1,0:T(8,128)(2,1)S(1)} %get-tuple-element.66), channel_id=1, source_target_pairs={{0,7},{1,0},{2,1},{3,2},{4,3},{5,4},{6,5},{7,6},{8,15},{9,8},{10,9... | collective-permute-start | bytes 135176 | tf_op jit(solution)/shard_map/ppermute | solution.py:32
  41.3 0.5 shard_map.131.refs_0_
  41.8 0.2 shard_map.133
  42.0 3.9 %all-to-all-done.dens_ref = f32[32,8,128]{2,1,0:T(8,128)S(1)} async-done(((f32[32,8,128]{2,1,0:T(8,128)}), f32[32,8,128]{2,1,0:T(8,128)S(1)}, u32[]{:S(2)}, u32[]{:S(2)}) %all-to-all-start) | async-done | bytes 131104 | tf_op jit(solution)/shard_map/all_to_all | solution.py:773
  45.9 4.3 %shard_map.134 = (f32[768,128]{1,0:T(8,128)S(1)}, f32[6,128]{1,0:T(8,128)}) custom-call(f32[32,8,128]{2,1,0:T(8,128)S(1)} %all-to-all-done.dens_ref, s32[41,8,128]{2,1,0:T(8,128)S(1)} %get-tuple-element.73.codes, f32[8,8,128]{2,1,0:T(8,128)S(1)} %get-tuple-element.74.screen_ref, f32[729,729]{1,0:T(8,128)} %matrix_hbm.1), custom_call_target="tpu_custom_call" | custom-call | bytes 12000000 | tf_op jit(solution)/shard_map/pallas_call | solution.py:643
  50.3 0.0 collective-permute-done.6.refs_1_
  50.3 0.0 collective-permute-done.7.refs_2_
  50.3 0.3 shard_map.135
  50.6 0.8 %collective-permute-start.9 = (bf16[416,128]{1,0:T(8,128)(2,1)S(1)}, bf16[416,128]{1,0:T(8,128)(2,1)S(1)}, u32[]{:S(2)}, u32[]{:S(2)}) collective-permute-start(bf16[416,128]{1,0:T(8,128)(2,1)S(1)} %get-tuple-element.78), channel_id=1, source_target_pairs={{0,1},{1,2},{2,3},{3,4},{4,5},{5,6},{6,7},{7,0},{8,9},{9,10},{10,1... | collective-permute-start | bytes 319496 | tf_op jit(solution)/shard_map/ppermute | solution.py:32
  51.5 2.8 %collective-permute-start.8 = (bf16[176,128]{1,0:T(8,128)(2,1)S(1)}, bf16[176,128]{1,0:T(8,128)(2,1)S(1)}, u32[]{:S(2)}, u32[]{:S(2)}) collective-permute-start(bf16[176,128]{1,0:T(8,128)(2,1)S(1)} %get-tuple-element.77), channel_id=1, source_target_pairs={{0,7},{1,0},{2,1},{3,2},{4,3},{5,4},{6,5},{7,6},{8,15},{9,8},{10,9... | collective-permute-start | bytes 135176 | tf_op jit(solution)/shard_map/ppermute | solution.py:32
  54.2 0.5 shard_map.136.refs_0_
  54.7 1.2 %collective-permute-done.8.refs_1_ = bf16[176,128]{1,0:T(8,128)(2,1)S(1)} collective-permute-done((bf16[176,128]{1,0:T(8,128)(2,1)S(1)}, bf16[176,128]{1,0:T(8,128)(2,1)S(1)}, u32[]{:S(2)}, u32[]{:S(2)}) %collective-permute-start.8) | collective-permute-done | bytes 45088 | tf_op jit(solution)/shard_map/ppermute | solution.py:32
  55.9 0.7 %collective-permute-done.9.refs_2_ = bf16[416,128]{1,0:T(8,128)(2,1)S(1)} collective-permute-done((bf16[416,128]{1,0:T(8,128)(2,1)S(1)}, bf16[416,128]{1,0:T(8,128)(2,1)S(1)}, u32[]{:S(2)}, u32[]{:S(2)}) %collective-permute-start.9) | collective-permute-done | bytes 106528 | tf_op jit(solution)/shard_map/ppermute | solution.py:32
  56.6 1.1 %shard_map.137 = f32[768,128]{1,0:T(8,128)} custom-call(f32[768,128]{1,0:T(8,128)S(1)} %shard_map.136.refs_0_, bf16[176,128]{1,0:T(8,128)(2,1)S(1)} %collective-permute-done.8.refs_1_, bf16[416,128]{1,0:T(8,128)(2,1)S(1)} %collective-permute-done.9.refs_2_, bf16[304,176]{1,0:T(8,128)(2,1)S(1)} %get-tuple-element.52.refs_3_, ...), custom_call_target="tpu_custom_call" | custom-call | bytes 3000000 | tf_op jit(solution)/shard_map/pallas_call | solution.py:403
Async XLA Ops:
  1.9 7.2 %collective-permute-start.1 = (bf16[464,128]{1,0:T(8,128)(2,1)S(1)}, bf16[464,128]{1,0:T(8,128)(2,1)S(1)}, u32[]{:S(2)}, u32[]{:S(2)}) collective-permute-start(bf16[464,128]{1,0:T(8,128)(2,1)S(1)} %get-tuple-element.51), channel_id=1, source_target_pairs={{0,1},{1,2},{2,3},{3,4},{4,5},{5,6},{6,7},{7,0},{8,9},{9,10},{10,1... | collective-permute-start | bytes 356360 | tf_op jit(solution)/shard_map/ppermute | solution.py:32
  2.5 7.7 %collective-permute-start = (bf16[176,128]{1,0:T(8,128)(2,1)S(1)}, bf16[176,128]{1,0:T(8,128)(2,1)S(1)}, u32[]{:S(2)}, u32[]{:S(2)}) collective-permute-start(bf16[176,128]{1,0:T(8,128)(2,1)S(1)} %get-tuple-element.50.refs_9_), channel_id=1, source_target_pairs={{0,7},{1,0},{2,1},{3,2},{4,3},{5,4},{6,5},{7,6},{8,15},{9,8},{10,9... | collective-permute-start | bytes 135176 | tf_op jit(solution)/shard_map/ppermute | solution.py:32
  12.4 19.8 %all-to-all-start.1 = ((f32[8,32,128]{2,1,0:T(8,128)}), f32[8,32,128]{2,1,0:T(8,128)S(1)}, u32[]{:S(2)}, u32[]{:S(2)}) async-start(f32[8,32,128]{2,1,0:T(8,128)} %shard_map.132), calls=%async_computation.1 | async-start | bytes 262144 | tf_op jit(solution)/shard_map/all_to_all | solution.py:763
  15.9 8.7 %collective-permute-start.3 = (bf16[416,128]{1,0:T(8,128)(2,1)S(1)}, bf16[416,128]{1,0:T(8,128)(2,1)S(1)}, u32[]{:S(2)}, u32[]{:S(2)}) collective-permute-start(bf16[416,128]{1,0:T(8,128)(2,1)S(1)} %get-tuple-element.60), channel_id=1, source_target_pairs={{0,1},{1,2},{2,3},{3,4},{4,5},{5,6},{6,7},{7,0},{8,9},{9,10},{10,1... | collective-permute-start | bytes 319496 | tf_op jit(solution)/shard_map/ppermute | solution.py:32
  16.4 4.8 %collective-permute-start.2 = (bf16[176,128]{1,0:T(8,128)(2,1)S(1)}, bf16[176,128]{1,0:T(8,128)(2,1)S(1)}, u32[]{:S(2)}, u32[]{:S(2)}) collective-permute-start(bf16[176,128]{1,0:T(8,128)(2,1)S(1)} %get-tuple-element.59), channel_id=1, source_target_pairs={{0,7},{1,0},{2,1},{3,2},{4,3},{5,4},{6,5},{7,6},{8,15},{9,8},{10,9... | collective-permute-start | bytes 135176 | tf_op jit(solution)/shard_map/ppermute | solution.py:32
  24.9 6.0 %collective-permute-start.5 = (bf16[416,128]{1,0:T(8,128)(2,1)S(1)}, bf16[416,128]{1,0:T(8,128)(2,1)S(1)}, u32[]{:S(2)}, u32[]{:S(2)}) collective-permute-start(bf16[416,128]{1,0:T(8,128)(2,1)S(1)} %get-tuple-element.63), channel_id=1, source_target_pairs={{0,1},{1,2},{2,3},{3,4},{4,5},{5,6},{6,7},{7,0},{8,9},{9,10},{10,1... | collective-permute-start | bytes 319496 | tf_op jit(solution)/shard_map/ppermute | solution.py:32
  25.0 5.2 %collective-permute-start.4 = (bf16[176,128]{1,0:T(8,128)(2,1)S(1)}, bf16[176,128]{1,0:T(8,128)(2,1)S(1)}, u32[]{:S(2)}, u32[]{:S(2)}) collective-permute-start(bf16[176,128]{1,0:T(8,128)(2,1)S(1)} %get-tuple-element.62), channel_id=1, source_target_pairs={{0,7},{1,0},{2,1},{3,2},{4,3},{5,4},{6,5},{7,6},{8,15},{9,8},{10,9... | collective-permute-start | bytes 135176 | tf_op jit(solution)/shard_map/ppermute | solution.py:32
  32.2 13.7 %all-to-all-start = ((f32[32,8,128]{2,1,0:T(8,128)}), f32[32,8,128]{2,1,0:T(8,128)S(1)}, u32[]{:S(2)}, u32[]{:S(2)}) async-start(f32[32,8,128]{2,1,0:T(8,128)} %get-tuple-element.68), calls=%async_computation | async-start | bytes 262144 | tf_op jit(solution)/shard_map/all_to_all | solution.py:773
  37.7 12.6 %collective-permute-start.7 = (bf16[416,128]{1,0:T(8,128)(2,1)S(1)}, bf16[416,128]{1,0:T(8,128)(2,1)S(1)}, u32[]{:S(2)}, u32[]{:S(2)}) collective-permute-start(bf16[416,128]{1,0:T(8,128)(2,1)S(1)} %get-tuple-element.67), channel_id=1, source_target_pairs={{0,1},{1,2},{2,3},{3,4},{4,5},{5,6},{6,7},{7,0},{8,9},{9,10},{10,1... | collective-permute-start | bytes 319496 | tf_op jit(solution)/shard_map/ppermute | solution.py:32
  38.0 12.3 %collective-permute-start.6 = (bf16[176,128]{1,0:T(8,128)(2,1)S(1)}, bf16[176,128]{1,0:T(8,128)(2,1)S(1)}, u32[]{:S(2)}, u32[]{:S(2)}) collective-permute-start(bf16[176,128]{1,0:T(8,128)(2,1)S(1)} %get-tuple-element.66), channel_id=1, source_target_pairs={{0,7},{1,0},{2,1},{3,2},{4,3},{5,4},{6,5},{7,6},{8,15},{9,8},{10,9... | collective-permute-start | bytes 135176 | tf_op jit(solution)/shard_map/ppermute | solution.py:32
  50.6 6.0 %collective-permute-start.9 = (bf16[416,128]{1,0:T(8,128)(2,1)S(1)}, bf16[416,128]{1,0:T(8,128)(2,1)S(1)}, u32[]{:S(2)}, u32[]{:S(2)}) collective-permute-start(bf16[416,128]{1,0:T(8,128)(2,1)S(1)} %get-tuple-element.78), channel_id=1, source_target_pairs={{0,1},{1,2},{2,3},{3,4},{4,5},{5,6},{6,7},{7,0},{8,9},{9,10},{10,1... | collective-permute-start | bytes 319496 | tf_op jit(solution)/shard_map/ppermute | solution.py:32
  51.5 4.5 %collective-permute-start.8 = (bf16[176,128]{1,0:T(8,128)(2,1)S(1)}, bf16[176,128]{1,0:T(8,128)(2,1)S(1)}, u32[]{:S(2)}, u32[]{:S(2)}) collective-permute-start(bf16[176,128]{1,0:T(8,128)(2,1)S(1)} %get-tuple-element.77), channel_id=1, source_target_pairs={{0,7},{1,0},{2,1},{3,2},{4,3},{5,4},{6,5},{7,6},{8,15},{9,8},{10,9... | collective-permute-start | bytes 135176 | tf_op jit(solution)/shard_map/ppermute | solution.py:32

commit v5 on v4

--- a/solution.py
+++ b/solution.py
@@ -338,23 +338,23 @@
     y_ref[0 : geo.sp, :] += total * scale
 
 
-def write_density(y_ref, occ_ref, dens_ref, row_pad):
-    _, blocks, _ = dens_ref.shape
+def write_density(y_ref, occ_ref, table_ref, part_rows, dens_ref):
+    parts = dens_ref.shape[0]
     own = y_ref.shape[0]
-    length = own // blocks
     y = y_ref[...]
     terms = y * y * occ_ref[...]
     high = terms.astype(BF)
     low = (terms - high.astype(F32)).astype(BF)
     ones = jnp.ones((SUBLANES, terms.shape[1]), BF)
     summed = dot_t(ones, high) + dot_t(ones, low)
-    row_pad[...] = jnp.zeros(row_pad.shape, F32)
-    for j in range(blocks):
-        row_pad[j : j + 1, 0:length] = summed[0:1, j * length : (j + 1) * length]
-    dens_ref[...] = jnp.broadcast_to(row_pad[...][None], dens_ref.shape)
-
-
-def finish_kernel(geo, scale, has_upper, mode, *refs):
+    dens_ref[:, 0, 0:own] = jnp.broadcast_to(summed[0:1, :], (parts, own))
+    band = lax.axis_index("band")
+    for r in range(part_rows):
+        row = table_ref[band, r : r + 1, :]
+        dens_ref[:, 0, own + r * LANES : own + (r + 1) * LANES] = jnp.broadcast_to(row, (parts, LANES))
+
+
+def finish_kernel(geo, scale, has_upper, mode, part_rows, *refs):
     refs = list(refs)
     n = len(geo.touching)
     base_ref, up_ref, dn_ref = refs[:3]
@@ -365,7 +365,8 @@
     if has_upper:
         uppers, refs = refs[:n], refs[n:]
         own_up = refs.pop(0)
-    occ_ref = refs.pop(0) if mode == "density" else None
+    if mode == "density":
+        occ_ref, table_ref = refs.pop(0), refs.pop(0)
     if mode == "field":
         column_ref, before_ref = refs.pop(0), refs.pop(0)
     y_ref = refs.pop(0)
@@ -377,17 +378,16 @@
     if mode != "last":
         write_sends(geo, y_ref, refs[0], refs[1])
     if mode == "density":
-        write_density(y_ref, occ_ref, refs[2], refs[3])
-
-
-def finish(geo, scale, base, halo, crosses, behinds, uppers=(), own_up=None, occ=None, parts=None, field=None, last=False):
+        write_density(y_ref, occ_ref, table_ref, part_rows, refs[2])
+
+
+def finish(geo, scale, base, halo, crosses, behinds, uppers=(), own_up=None, density=None, field=None, last=False):
     columns = base.shape[1]
     args = [base, halo[0], halo[1], *crosses, *behinds, *uppers]
     if uppers:
         args.append(own_up)
     shapes = [sds(base.shape, F32)]
-    scratch = []
-    mode = "plain"
+    mode, part_rows = "plain", 0
     if last:
         mode = "last"
     else:
@@ -395,21 +395,21 @@
     if field is not None:
         mode = "field"
         args += list(field)
-    if occ is not None:
+    if density is not None:
         mode = "density"
-        args.append(occ)
-        shapes.append(sds(parts, F32))
-        scratch.append(pltpu.VMEM(parts[1:], F32))
+        fg, weights, table = density
+        part_rows = fg.part_rows
+        args += [weights, table]
+        shapes.append(sds((fg.bands * fg.domains, 1, fg.width), F32))
     return vmem_call(
-        functools.partial(finish_kernel, geo, scale, bool(uppers), mode),
+        functools.partial(finish_kernel, geo, scale, bool(uppers), mode, part_rows),
         shapes,
-        scratch,
         cost=cost_of(1.0),
     )(*args)
 
 
 class FieldGeometry:
-    def __init__(self, domains, own, share, cells, npc):
+    def __init__(self, bands, domains, own, share, cells, npc):
         self.domains, self.own, self.share, self.cells, self.npc = domains, own, share, cells, npc
         self.block = own // domains
         self.rows = up_to(npc, LANES) // LANES
@@ -418,9 +418,14 @@
         self.at_face = self.at_inverse + cells * self.blocks
         self.at_face_inverse = self.at_face + 1
         self.at_owner = self.at_face + 2
-        self.codes = self.at_face + 3
+        self.at_owner_inverse = self.at_face + 3
+        self.codes = self.at_face + 4
         self.at_screen = up_to(self.codes, 2) // 2
-        self.table_rows = up_to(self.at_screen + domains, SUBLANES)
+        self.lines = own // LANES
+        self.part_rows = -(-(self.at_screen + self.lines) // bands)
+        self.table_rows = up_to(self.part_rows * bands, SUBLANES)
+        self.bands = bands
+        self.width = own + self.part_rows * LANES
         self.size = self.rows * LANES
         self.fits = (
             domains == SUBLANES
@@ -484,20 +489,23 @@
     hits = jnp.where(column == wide_lane.astype(F32), (sub + 1).astype(F32), 0.0)
     one[fg.at_face_inverse : fg.at_face_inverse + 1, :] = jnp.sum(hits, axis=0, keepdims=True) - 1.0
     one[fg.at_owner : fg.at_owner + 1, 0 : fg.domains] = owner_ref[...].astype(F32)
+    column = column_of(one[fg.at_owner : fg.at_owner + 1, :])
+    hits = jnp.where(column == wide_lane.astype(F32), (sub + 1).astype(F32), 0.0)
+    hits = jnp.where(sub < fg.domains, hits, 0.0)
+    one[fg.at_owner_inverse : fg.at_owner_inverse + 1, :] = jnp.sum(hits, axis=0, keepdims=True) - 1.0
     packed[...] = jnp.zeros(packed.shape, F32)
     half = fg.at_screen
     packed[0:half, :] = (one[0:half, :] + 1.0) + (one[half : 2 * half, :] + 1.0) * CODE_BASE
-    for row, lane, j, offset, count in pieces(fg.block, fg.domains):
-        at = fg.at_screen + j
-        packed[at : at + 1, offset : offset + count] = screen_ref[row : row + 1, lane : lane + count]
-    table_ref[...] = jnp.broadcast_to(packed[...][None], table_ref.shape)
+    packed[half : half + fg.lines, :] = screen_ref[...]
+    for b in range(fg.bands):
+        table_ref[b, 0 : fg.part_rows, :] = packed[b * fg.part_rows : (b + 1) * fg.part_rows, :]
 
 
 def field_tables(fg, pois_nodes, pois_face, block_owner, lines, after):
     specs = [pl.BlockSpec(memory_space=pltpu.VMEM)] * 4 + [pl.BlockSpec(memory_space=pl.ANY)]
     return vmem_call(
         functools.partial(field_tables_kernel, fg),
-        sds((fg.domains, fg.table_rows, LANES), F32),
+        sds((fg.bands, up_to(fg.part_rows, SUBLANES), LANES), F32),
         [
             pltpu.VMEM((up_to(fg.cells, SUBLANES), fg.size), I32),
             pltpu.VMEM((up_to(2 * fg.at_screen, SUBLANES), LANES), F32),
@@ -512,62 +520,49 @@
     return jnp.take_along_axis(values, index, axis=1, mode="promise_in_bounds")
 
 
-def field_codes_kernel(fg, table_ref, codes_ref, screen_ref, lines):
-    domains, half = fg.domains, fg.at_screen
-    for at in range(fg.table_rows):
-        for d in range(domains):
-            lines[at, d : d + 1, :] = table_ref[d, at : at + 1, :]
+def decode(fg, got_ref, codes):
+    domains, half, own = fg.domains, fg.at_screen, fg.own
+
+    def tile(at):
+        band, row = at // fg.part_rows, at % fg.part_rows
+        first = own + row * LANES
+        return got_ref[band * domains : (band + 1) * domains, 0, first : first + LANES]
+
     for at in range(half):
-        both = lines[at].astype(I32)
-        for here, code in ((at, jnp.bitwise_and(both, CODE_BASE - 1) - 1), (half + at, jnp.right_shift(both, CODE_BITS) - 1)):
-            if here == fg.at_face_inverse:
-                code = pltpu.roll(code, 1, 0)
-            if here < fg.at_owner:
-                codes_ref[here] = code
-            elif here == fg.at_owner:
-                owner = code.astype(F32)
-    part = lax.broadcasted_iota(I32, (domains, LANES), 0).astype(F32)
-    mine = jnp.zeros((domains, LANES), F32)
-    here = lax.axis_index("domain").astype(F32)
+        both = tile(at).astype(I32)
+        low = jnp.bitwise_and(both, CODE_BASE - 1) - 1
+        codes[at] = low
+        codes[half + at] = jnp.right_shift(both, CODE_BITS) - 1
+    codes[fg.at_face_inverse] = pltpu.roll(codes[fg.at_face_inverse], 1, 0)
+    lines = [tile(half + g) for g in range(fg.lines)]
+    lane = lax.broadcasted_iota(I32, (domains, LANES), 1)
+    screens = []
     for q in range(domains):
-        column = column_of(owner[q : q + 1, :])[0:domains, :]
-        inverse = jnp.zeros((domains, LANES), F32)
-        for j in range(domains):
-            inverse = jnp.where(column[j : j + 1, :] == part, float(j), inverse)
-        codes_ref[fg.at_owner + q] = inverse.astype(I32)
-        mine = jnp.where(here == float(q), column, mine)
-    codes_ref[fg.at_owner + domains] = mine.astype(I32)
+        screen = jnp.zeros((domains, LANES), F32)
+        for row, start, j, offset, count in pieces(fg.block, domains):
+            if j == q:
+                moved = pltpu.roll(lines[row], (offset - start) % LANES, 1)
+                screen = jnp.where((lane >= offset) & (lane < offset + count), moved, screen)
+        screens.append(screen)
+    inverse = codes[fg.at_owner_inverse].astype(F32).T[0:domains, :]
+    places = []
     for q in range(domains):
-        screen_ref[q] = lines[fg.at_screen + q]
-
-
-def field_codes(fg, table):
-    return vmem_call(
-        functools.partial(field_codes_kernel, fg),
-        [
-            sds((fg.at_owner + fg.domains + 1, fg.domains, LANES), I32),
-            sds((fg.domains, fg.domains, LANES), F32),
-        ],
-        [pltpu.VMEM((fg.table_rows, fg.domains, LANES), F32)],
-        cost=cost_of(1.0),
-    )(table)
+        block = jnp.broadcast_to(inverse[:, q : q + 1], (domains, LANES)).astype(I32)
+        places.append(block * fg.block + lane)
+    owners = codes[fg.at_owner].astype(F32).T[0:domains, :]
+    here = lax.axis_index("domain")
+    narrow = lax.broadcasted_iota(I32, (domains, domains), 1)
+    mine = jnp.sum(jnp.where(narrow == here, owners, 0.0), axis=1, keepdims=True)
+    return places, jnp.broadcast_to(mine, (domains, LANES)).astype(I32), screens
 
 
 def rows_of(values, index):
     return jnp.take_along_axis(values, index, axis=0, mode="promise_in_bounds")
 
 
-def field_solve(fg, dens_ref, codes, screen_ref, matrix_ref, high_ref, low_ref, rows, copies):
+def field_solve(fg, got_ref, codes, places, screen, matrix_ref, high_ref, low_ref, rows, copies):
     domains, cells = fg.domains, fg.cells
-    bands = dens_ref.shape[0] // domains
     valid = lax.broadcasted_iota(I32, (domains, LANES), 1) < fg.block
-    source = []
-    for q in range(domains):
-        density = dens_ref[q]
-        for b in range(1, bands):
-            density = density + dens_ref[b * domains + q]
-        source.append(rows_of(density, codes[fg.at_owner + q]))
-    screen = [screen_ref[q] for q in range(domains)]
 
     def lookup(sources, code):
         lane = jnp.bitwise_and(code, LANES - 1)
@@ -611,6 +606,17 @@
         out[0] = out[0] + lookup([arriving], codes[fg.at_face_inverse])
         return [jnp.where(valid, screen[q] * field[q] + out[q], 0.0) for q in range(domains)]
 
+    density = []
+    for g in range(fg.lines):
+        at = slice(g * LANES, (g + 1) * LANES)
+        total = got_ref[0:domains, 0, at]
+        for b in range(1, fg.bands):
+            total = total + got_ref[b * domains : (b + 1) * domains, 0, at]
+        density.append(total)
+    source = []
+    for q in range(domains):
+        spread = [jnp.broadcast_to(d[q : q + 1, :], (domains, LANES)) for d in density]
+        source.append(jnp.where(valid, lookup(spread, places[q]), 0.0))
     step_one = [s * (1.0 / solve_center) for s in source]
     applied = operator(step_one)
     residual = [s - a for s, a in zip(source, applied)]
@@ -623,13 +629,13 @@
     return [(x + y) + z for x, y, z in zip(step_one, step_two, step_three)]
 
 
-def field_kernel(fg, dens_ref, codes, screen_ref, matrix_hbm, column_ref, hartree_ref, rows, phi, mine, matrix_ref, high_ref, low_ref, sems):
+def field_kernel(fg, got_ref, matrix_hbm, column_ref, hartree_ref, codes, rows, phi, mine, matrix_ref, high_ref, low_ref, sems):
     copies = fetch([(matrix_hbm, matrix_ref)], sems)
-    blocks = field_solve(fg, dens_ref, codes, screen_ref, matrix_ref, high_ref, low_ref, rows, copies)
+    places, owner, screens = decode(fg, got_ref, codes)
+    blocks = field_solve(fg, got_ref, codes, places, screens, matrix_ref, high_ref, low_ref, rows, copies)
     for q in range(fg.domains):
         phi[q] = blocks[q]
-    here = lax.axis_index("domain")
-    mine[...] = rows_of(phi[here], codes[fg.at_owner + fg.domains])
+    mine[...] = rows_of(phi[lax.axis_index("domain")], owner)
     for j in range(fg.domains):
         column = column_of(mine[j : j + 1, :])
         column_ref[j * fg.block : (j + 1) * fg.block, :] = column[0 : fg.block, :]
@@ -637,13 +643,13 @@
         hartree_ref[row : row + 1, lane : lane + count] = mine[j : j + 1, offset : offset + count]
 
 
-def field_step(fg, dens, codes, screen, matrix):
-    vmem = pl.BlockSpec(memory_space=pltpu.VMEM)
+def field_step(fg, got, matrix):
     tile = (fg.domains, LANES)
     return vmem_call(
         functools.partial(field_kernel, fg),
-        [sds((fg.own, LANES), F32), sds((fg.own // LANES, LANES), F32)],
+        [sds((fg.own, LANES), F32), sds((fg.lines, LANES), F32)],
         [
+            pltpu.VMEM((2 * fg.at_screen, *tile), I32),
             pltpu.VMEM((fg.cells * fg.domains, fg.size), F32),
             pltpu.VMEM((fg.domains, *tile), F32),
             pltpu.VMEM(tile, F32),
@@ -652,9 +658,9 @@
             pltpu.VMEM(matrix.shape, BF),
             pltpu.SemaphoreType.DMA((1,)),
         ],
-        in_specs=[vmem] * 3 + [pl.BlockSpec(memory_space=pltpu.HBM)],
+        in_specs=[pl.BlockSpec(memory_space=pltpu.VMEM), pl.BlockSpec(memory_space=pltpu.HBM)],
         cost=cost_of(4.0),
-    )(dens, codes, screen, *in_hbm(matrix))
+    )(got, *in_hbm(matrix))
 
 
 def assembled(owned_rows, face_row, terms):
@@ -741,7 +747,7 @@
     bands = lax.axis_size("band")
     own, columns = orbitals.shape
     geo = Geometry(own, face_order.shape[1], cell_nodes.shape[0], cell_nodes.shape[1])
-    fg = FieldGeometry(domains, own, pois_face.shape[1], pois_nodes.shape[0], pois_nodes.shape[1])
+    fg = FieldGeometry(bands, domains, own, pois_face.shape[1], pois_nodes.shape[0], pois_nodes.shape[1])
     first, later = 1.0 / filter_half, 2.0 / filter_half
 
     others = [cell_matrix, potential.reshape(own // LANES, LANES)]
@@ -760,21 +766,18 @@
     if fg.fits:
         *others, weights = others
         table = field_tables(fg, *others, base)
-        tables = lax.all_to_all(table, "domain", 0, 0, tiled=True)
     y2, *sends2 = finish(geo, later, base, halo, crosses, behinds)
 
     halo = exchange(sends2)
     base = owned_part(geo, later, y2, y1, pot, None, mats, uppers)
     if fg.fits:
-        parts = (domains * bands, domains, LANES)
         y3, dn, up, spread = finish(
-            geo, later, base, halo, crosses, behinds, occ=weights, parts=parts
+            geo, later, base, halo, crosses, behinds, density=(fg, weights, table)
         )
         dens = lax.all_to_all(spread, ("band", "domain"), 0, 0, tiled=True)
         halo = exchange((dn, up))
         base = owned_part(geo, first, y3, None, pot, None, mats, uppers)
-        codes, screen = field_codes(fg, tables)
-        column, packed = field_step(fg, dens, codes, screen, pois_matrix)
+        column, packed = field_step(fg, dens, pois_matrix)
         hartree = packed.reshape(own)
         z1, *sends4 = finish(geo, first, base, halo, crosses, behinds, field=(column, y3))
     else:

time: 58 us -> 51.1 us (0.88)
  starting transfers between devices: 27.9 us -> 24.6 us
  waiting for transfers between devices: 12.9 us -> 10.4 us
  Pallas kernels: 16 us -> 15.1 us
    all_to_all x1 -> x0, starting transfers between devices: 3.5 us -> none  [on_device(): tables = lax.all_to_all(table, 'domain', 0, 0, tiled=True)]
    ppermute x10, waiting for transfers between devices: 9.03 us -> 5.66 us  [from_behind(): lax.ppermute(array, axis, [(i, (i + by) % length) for i in range(length)])]
    pallas_call x2 -> x1, Pallas kernels: 1.6 us -> 0.71 us  [field_tables(): vmem_call(functools.partial(field_tables_kernel, fg), sds((fg.bands, up_t...]
    all_to_all x1, waiting for transfers between devices: 3.91 us -> 4.73 us  [on_device(): dens = lax.all_to_all(spread, ('band', 'domain'), 0, 0, tiled=True)]
  transfers between devices with their start and end apart: 12 -> 11, of which waited for: 8 -> 8; matrix products, arithmetic and copies ran while one was open for 0% -> 0% of each run, Pallas kernels for 19% -> 21%
where the time goes in v5:
time: 51.1 us; the launch traced here: 50.9 us
  starting transfers between devices  24.6 us (48%)
  Pallas kernels  15.1 us (30%)
  waiting for transfers between devices  10.4 us (20%)
  between operations  0.77 us (2%)
    ppermute x10, starting transfers between devices, from_behind(): lax.ppermute(array, axis, [(i, (i + by) % length) for i in range(length)])  19 us
    ppermute x10, waiting for transfers between devices, from_behind(): lax.ppermute(array, axis, [(i, (i + by) % length) for i in range(length)])  5.66 us
    all_to_all x1, starting transfers between devices, on_device(): dens = lax.all_to_all(spread, ('band', 'domain'), 0, 0, tiled=True)  5.62 us
    all_to_all x1, waiting for transfers between devices, on_device(): dens = lax.all_to_all(spread, ('band', 'domain'), 0, 0, tiled=True)  4.73 us
    pallas_call x1, Pallas kernels, field_step(): vmem_call(functools.partial(field_kernel, fg), [sds((fg.own, LANES), F32)...  4.37 us
    pallas_call x5, Pallas kernels, finish(): vmem_call(functools.partial(finish_kernel, geo, scale, bool(uppers), mode...  3.27 us
    pallas_call x5, Pallas kernels, owned_part(): vmem_call(functools.partial(owned_part_kernel, geo, scale, prev is not No...  2.41 us
    pallas_call x1, Pallas kernels, own_matrices(): vmem_call(functools.partial(own_matrices_kernel, geo), shapes, [matrix_sc...  1.98 us
  transfers between devices with their start and end apart: 11, of which 8 were waited for; matrix products, arithmetic and copies ran while one was open for 0% of the time, Pallas kernels for 21%

profile of v5, /device:TPU:0, one launch (start us, length us, event | category | flops | bytes accessed | tf_op | source)
XLA Modules:
  0.0 50.9 jit_solution(2160353593587638148)
XLA Ops:
  0.6 1.3 %shard_map.122 = (bf16[464,128]{1,0:T(8,128)(2,1)S(1)}, bf16[176,128]{1,0:T(8,128)(2,1)S(1)}, f32[768,128]{1,0:T(8,128)S(1)}, s32[8,384]{1,0:T(8,128)S(1)}, bf16...) custom-call(f32[768,128]{1,0:T(8,128)} %y_hbm.1, ...), custom_call_target="tpu_custom_call" | custom-call | bytes 3000000 | tf_op jit(solution)/shard_map/pallas_call | solution.py:255
  1.9 0.5 %collective-permute-start.1 = (bf16[464,128]{1,0:T(8,128)(2,1)S(1)}, bf16[464,128]{1,0:T(8,128)(2,1)S(1)}, u32[]{:S(2)}, u32[]{:S(2)}) collective-permute-start(bf16[464,128]{1,0:T(8,128)(2,1)S(1)} %get-tuple-element.49), channel_id=1, source_target_pairs={{0,1},{1,2},{2,3},{3,4},{4,5},{5,6},{6,7},{7,0},{8,9},{9,10},{10,1... | collective-permute-start | bytes 356360 | tf_op jit(solution)/shard_map/ppermute | solution.py:32
  2.5 4.1 %collective-permute-start = (bf16[176,128]{1,0:T(8,128)(2,1)S(1)}, bf16[176,128]{1,0:T(8,128)(2,1)S(1)}, u32[]{:S(2)}, u32[]{:S(2)}) collective-permute-start(bf16[176,128]{1,0:T(8,128)(2,1)S(1)} %get-tuple-element.48.refs_9_), channel_id=1, source_target_pairs={{0,7},{1,0},{2,1},{3,2},{4,3},{5,4},{6,5},{7,6},{8,15},{9,8},{10,9... | collective-permute-start | bytes 135176 | tf_op jit(solution)/shard_map/ppermute | solution.py:32
  6.6 2.0 %shard_map.123 = (bf16[352,352]{1,0:T(8,128)(2,1)S(1)}, bf16[368,368]{1,0:T(8,128)(2,1)S(1)}, bf16[304,304]{1,0:T(8,128)(2,1)S(1)}, bf16[192,192]{1,0:T(8,128)(2...) custom-call(s32[8,384]{1,0:T(8,128)S(1)} %get-tuple-element.40.refs_0_, ...), custom_call_target="tpu_custom_call" | custom-call | bytes 6000000 | tf_op jit(solution)/shard_map/pallas_call | solution.py:162
  8.6 0.4 shard_map.124.refs_0_
  9.0 0.1 collective-permute-done.1.refs_0_.refs_2_
  9.1 1.0 %shard_map.125 = (bf16[176,304]{1,0:T(8,128)(2,1)S(1)}, bf16[176,192]{1,0:T(8,128)(2,1)S(1)}, bf16[176,176]{1,0:T(8,128)(2,1)S(1)}, bf16[176,176]{1,0:T(8,128)(2,1)S(1)}) custom-call(bf16[464,128]{1,0:T(8,128)(2,1)S(1)} %collective-permute-done.1.refs_0_.refs_2_, bf16[343,343]{1,0:T(8,128)(2,1)S(1)} %get-tuple-element.41.refs_1_), custom_call_target="tpu_custom_call" | custom-call | bytes 3000000 | tf_op jit(solution)/shard_map/pallas_call | solution.py:195
  10.2 0.0 collective-permute-done.refs_1_
  10.2 0.3 shard_map.126
  10.5 0.1 collective-permute-start.3
  10.6 3.5 %collective-permute-start.2 = (bf16[176,128]{1,0:T(8,128)(2,1)S(1)}, bf16[176,128]{1,0:T(8,128)(2,1)S(1)}, u32[]{:S(2)}, u32[]{:S(2)}) collective-permute-start(bf16[176,128]{1,0:T(8,128)(2,1)S(1)} %get-tuple-element.57), channel_id=1, source_target_pairs={{0,7},{1,0},{2,1},{3,2},{4,3},{5,4},{6,5},{7,6},{8,15},{9,8},{10,9... | collective-permute-start | bytes 135176 | tf_op jit(solution)/shard_map/ppermute | solution.py:32
  14.1 0.5 shard_map.127.refs_0_.refs_4_
  14.6 1.2 %collective-permute-done.2.refs_1_ = bf16[176,128]{1,0:T(8,128)(2,1)S(1)} collective-permute-done((bf16[176,128]{1,0:T(8,128)(2,1)S(1)}, bf16[176,128]{1,0:T(8,128)(2,1)S(1)}, u32[]{:S(2)}, u32[]{:S(2)}) %collective-permute-start.2) | collective-permute-done | bytes 45088 | tf_op jit(solution)/shard_map/ppermute | solution.py:32
  15.8 1.1 %collective-permute-done.3.refs_2_ = bf16[416,128]{1,0:T(8,128)(2,1)S(1)} collective-permute-done((bf16[416,128]{1,0:T(8,128)(2,1)S(1)}, bf16[416,128]{1,0:T(8,128)(2,1)S(1)}, u32[]{:S(2)}, u32[]{:S(2)}) %collective-permute-start.3) | collective-permute-done | bytes 106528 | tf_op jit(solution)/shard_map/ppermute | solution.py:32
  16.9 0.3 shard_map.128
  17.2 0.1 collective-permute-start.5
  17.3 3.5 %collective-permute-start.4 = (bf16[176,128]{1,0:T(8,128)(2,1)S(1)}, bf16[176,128]{1,0:T(8,128)(2,1)S(1)}, u32[]{:S(2)}, u32[]{:S(2)}) collective-permute-start(bf16[176,128]{1,0:T(8,128)(2,1)S(1)} %get-tuple-element.60), channel_id=1, source_target_pairs={{0,7},{1,0},{2,1},{3,2},{4,3},{5,4},{6,5},{7,6},{8,15},{9,8},{10,9... | collective-permute-start | bytes 135176 | tf_op jit(solution)/shard_map/ppermute | solution.py:32
  20.8 0.7 %shard_map.130.refs_8_ = f32[4,8,128]{2,1,0:T(8,128)S(1)} custom-call(s32[2,729]{1,0:T(2,128)S(1)} %get-tuple-element.63.refs_0_, s32[1,81]{1,0:T(1,128)S(1)} %get-tuple-element.64.refs_1_, s32[1,8]{1,0:T(1,128)S(1)} %get-tuple-element.65.refs_2_, f32[6,128]{1,0:T(8,128)S(1)} %get-tuple-element.66.refs_3_, f32[768,128]{1,0:T(8,128)S(1)} %shard_map.127.refs_0_.refs_4_), custom_call_target="tpu_custom_call" | custom-call | bytes 3000000 | tf_op jit(solution)/shard_map/pallas_call | solution.py:506
  21.5 0.5 shard_map.129.refs_0_
  22.0 0.5 collective-permute-done.4.refs_1_
  22.5 0.8 %collective-permute-done.5.refs_2_ = bf16[416,128]{1,0:T(8,128)(2,1)S(1)} collective-permute-done((bf16[416,128]{1,0:T(8,128)(2,1)S(1)}, bf16[416,128]{1,0:T(8,128)(2,1)S(1)}, u32[]{:S(2)}, u32[]{:S(2)}) %collective-permute-start.5) | collective-permute-done | bytes 106528 | tf_op jit(solution)/shard_map/ppermute | solution.py:32
  23.3 1.3 %shard_map.131 = (f32[768,128]{1,0:T(8,128)S(1)}, bf16[416,128]{1,0:T(8,128)(2,1)S(1)}, bf16[176,128]{1,0:T(8,128)(2,1)S(1)}, f32[32,1,1536]{2,1,0:T(1,128)}) custom-call(f32[768,128]{1,0:T(8,128)S(1)} %shard_map.129.refs_0_, bf16[176,128]{1,0:T(8,128)(2,1)S(1)} %collective-permute-done.4.refs_1_, bf16[416,128]{1,0:T(8,128)(2,1)S(1)} %collective-permute-done.5.refs_2_, ...), custom_call_target="tpu_custom_call" | custom-call | bytes 3000000 | tf_op jit(solution)/shard_map/pallas_call | solution.py:404
  24.6 5.6 %all-to-all-start = ((f32[32,1,1536]{2,1,0:T(1,128)}), f32[32,1,1536]{2,1,0:T(1,128)S(1)}, u32[]{:S(2)}, u32[]{:S(2)}) async-start(f32[32,1,1536]{2,1,0:T(1,128)} %get-tuple-element.70), calls=%async_computation | async-start | bytes 393216 | tf_op jit(solution)/shard_map/all_to_all | solution.py:777
  30.2 0.3 collective-permute-start.7
  30.5 3.3 %collective-permute-start.6 = (bf16[176,128]{1,0:T(8,128)(2,1)S(1)}, bf16[176,128]{1,0:T(8,128)(2,1)S(1)}, u32[]{:S(2)}, u32[]{:S(2)}) collective-permute-start(bf16[176,128]{1,0:T(8,128)(2,1)S(1)} %get-tuple-element.68), channel_id=1, source_target_pairs={{0,7},{1,0},{2,1},{3,2},{4,3},{5,4},{6,5},{7,6},{8,15},{9,8},{10,9... | collective-permute-start | bytes 135176 | tf_op jit(solution)/shard_map/ppermute | solution.py:32
  33.8 0.5 shard_map.132.refs_0_
  34.3 4.7 %all-to-all-done.got_ref = f32[32,1,1536]{2,1,0:T(1,128)S(1)} async-done(((f32[32,1,1536]{2,1,0:T(1,128)}), f32[32,1,1536]{2,1,0:T(1,128)S(1)}, u32[]{:S(2)}, u32[]{:S(2)}) %all-to-all-start) | async-done | bytes 196640 | tf_op jit(solution)/shard_map/all_to_all | solution.py:777
  39.0 4.4 %shard_map.133 = (f32[768,128]{1,0:T(8,128)S(1)}, f32[6,128]{1,0:T(8,128)}) custom-call(f32[32,1,1536]{2,1,0:T(1,128)S(1)} %all-to-all-done.got_ref, f32[729,729]{1,0:T(8,128)} %matrix_hbm.1), custom_call_target="tpu_custom_call" | custom-call | bytes 12000000 | tf_op jit(solution)/shard_map/pallas_call | solution.py:648
  43.4 0.0 collective-permute-done.6.refs_1_
  43.4 0.0 collective-permute-done.7.refs_2_
  43.4 0.3 shard_map.134
  43.7 1.3 %collective-permute-start.9 = (bf16[416,128]{1,0:T(8,128)(2,1)S(1)}, bf16[416,128]{1,0:T(8,128)(2,1)S(1)}, u32[]{:S(2)}, u32[]{:S(2)}) collective-permute-start(bf16[416,128]{1,0:T(8,128)(2,1)S(1)} %get-tuple-element.74), channel_id=1, source_target_pairs={{0,1},{1,2},{2,3},{3,4},{4,5},{5,6},{6,7},{7,0},{8,9},{9,10},{10,1... | collective-permute-start | bytes 319496 | tf_op jit(solution)/shard_map/ppermute | solution.py:32
  45.1 2.3 %collective-permute-start.8 = (bf16[176,128]{1,0:T(8,128)(2,1)S(1)}, bf16[176,128]{1,0:T(8,128)(2,1)S(1)}, u32[]{:S(2)}, u32[]{:S(2)}) collective-permute-start(bf16[176,128]{1,0:T(8,128)(2,1)S(1)} %get-tuple-element.73), channel_id=1, source_target_pairs={{0,7},{1,0},{2,1},{3,2},{4,3},{5,4},{6,5},{7,6},{8,15},{9,8},{10,9... | collective-permute-start | bytes 135176 | tf_op jit(solution)/shard_map/ppermute | solution.py:32
  47.3 0.5 shard_map.135.refs_0_
  47.8 1.2 %collective-permute-done.8.refs_1_ = bf16[176,128]{1,0:T(8,128)(2,1)S(1)} collective-permute-done((bf16[176,128]{1,0:T(8,128)(2,1)S(1)}, bf16[176,128]{1,0:T(8,128)(2,1)S(1)}, u32[]{:S(2)}, u32[]{:S(2)}) %collective-permute-start.8) | collective-permute-done | bytes 45088 | tf_op jit(solution)/shard_map/ppermute | solution.py:32
  49.0 0.8 %collective-permute-done.9.refs_2_ = bf16[416,128]{1,0:T(8,128)(2,1)S(1)} collective-permute-done((bf16[416,128]{1,0:T(8,128)(2,1)S(1)}, bf16[416,128]{1,0:T(8,128)(2,1)S(1)}, u32[]{:S(2)}, u32[]{:S(2)}) %collective-permute-start.9) | collective-permute-done | bytes 106528 | tf_op jit(solution)/shard_map/ppermute | solution.py:32
  49.8 1.1 %shard_map.136 = f32[768,128]{1,0:T(8,128)} custom-call(f32[768,128]{1,0:T(8,128)S(1)} %shard_map.135.refs_0_, bf16[176,128]{1,0:T(8,128)(2,1)S(1)} %collective-permute-done.8.refs_1_, bf16[416,128]{1,0:T(8,128)(2,1)S(1)} %collective-permute-done.9.refs_2_, bf16[304,176]{1,0:T(8,128)(2,1)S(1)} %get-tuple-element.50.refs_3_, ...), custom_call_target="tpu_custom_call" | custom-call | bytes 3000000 | tf_op jit(solution)/shard_map/pallas_call | solution.py:404
Async XLA Ops:
  1.9 7.2 %collective-permute-start.1 = (bf16[464,128]{1,0:T(8,128)(2,1)S(1)}, bf16[464,128]{1,0:T(8,128)(2,1)S(1)}, u32[]{:S(2)}, u32[]{:S(2)}) collective-permute-start(bf16[464,128]{1,0:T(8,128)(2,1)S(1)} %get-tuple-element.49), channel_id=1, source_target_pairs={{0,1},{1,2},{2,3},{3,4},{4,5},{5,6},{6,7},{7,0},{8,9},{9,10},{10,1... | collective-permute-start | bytes 356360 | tf_op jit(solution)/shard_map/ppermute | solution.py:32
  2.5 7.7 %collective-permute-start = (bf16[176,128]{1,0:T(8,128)(2,1)S(1)}, bf16[176,128]{1,0:T(8,128)(2,1)S(1)}, u32[]{:S(2)}, u32[]{:S(2)}) collective-permute-start(bf16[176,128]{1,0:T(8,128)(2,1)S(1)} %get-tuple-element.48.refs_9_), channel_id=1, source_target_pairs={{0,7},{1,0},{2,1},{3,2},{4,3},{5,4},{6,5},{7,6},{8,15},{9,8},{10,9... | collective-permute-start | bytes 135176 | tf_op jit(solution)/shard_map/ppermute | solution.py:32
  10.5 6.4 %collective-permute-start.3 = (bf16[416,128]{1,0:T(8,128)(2,1)S(1)}, bf16[416,128]{1,0:T(8,128)(2,1)S(1)}, u32[]{:S(2)}, u32[]{:S(2)}) collective-permute-start(bf16[416,128]{1,0:T(8,128)(2,1)S(1)} %get-tuple-element.58), channel_id=1, source_target_pairs={{0,1},{1,2},{2,3},{3,4},{4,5},{5,6},{6,7},{7,0},{8,9},{9,10},{10,1... | collective-permute-start | bytes 319496 | tf_op jit(solution)/shard_map/ppermute | solution.py:32
  10.6 5.2 %collective-permute-start.2 = (bf16[176,128]{1,0:T(8,128)(2,1)S(1)}, bf16[176,128]{1,0:T(8,128)(2,1)S(1)}, u32[]{:S(2)}, u32[]{:S(2)}) collective-permute-start(bf16[176,128]{1,0:T(8,128)(2,1)S(1)} %get-tuple-element.57), channel_id=1, source_target_pairs={{0,7},{1,0},{2,1},{3,2},{4,3},{5,4},{6,5},{7,6},{8,15},{9,8},{10,9... | collective-permute-start | bytes 135176 | tf_op jit(solution)/shard_map/ppermute | solution.py:32
  17.2 6.1 %collective-permute-start.5 = (bf16[416,128]{1,0:T(8,128)(2,1)S(1)}, bf16[416,128]{1,0:T(8,128)(2,1)S(1)}, u32[]{:S(2)}, u32[]{:S(2)}) collective-permute-start(bf16[416,128]{1,0:T(8,128)(2,1)S(1)} %get-tuple-element.61), channel_id=1, source_target_pairs={{0,1},{1,2},{2,3},{3,4},{4,5},{5,6},{6,7},{7,0},{8,9},{9,10},{10,1... | collective-permute-start | bytes 319496 | tf_op jit(solution)/shard_map/ppermute | solution.py:32
  17.3 5.2 %collective-permute-start.4 = (bf16[176,128]{1,0:T(8,128)(2,1)S(1)}, bf16[176,128]{1,0:T(8,128)(2,1)S(1)}, u32[]{:S(2)}, u32[]{:S(2)}) collective-permute-start(bf16[176,128]{1,0:T(8,128)(2,1)S(1)} %get-tuple-element.60), channel_id=1, source_target_pairs={{0,7},{1,0},{2,1},{3,2},{4,3},{5,4},{6,5},{7,6},{8,15},{9,8},{10,9... | collective-permute-start | bytes 135176 | tf_op jit(solution)/shard_map/ppermute | solution.py:32
  24.6 14.4 %all-to-all-start = ((f32[32,1,1536]{2,1,0:T(1,128)}), f32[32,1,1536]{2,1,0:T(1,128)S(1)}, u32[]{:S(2)}, u32[]{:S(2)}) async-start(f32[32,1,1536]{2,1,0:T(1,128)} %get-tuple-element.70), calls=%async_computation | async-start | bytes 393216 | tf_op jit(solution)/shard_map/all_to_all | solution.py:777
  30.2 13.2 %collective-permute-start.7 = (bf16[416,128]{1,0:T(8,128)(2,1)S(1)}, bf16[416,128]{1,0:T(8,128)(2,1)S(1)}, u32[]{:S(2)}, u32[]{:S(2)}) collective-permute-start(bf16[416,128]{1,0:T(8,128)(2,1)S(1)} %get-tuple-element.69), channel_id=1, source_target_pairs={{0,1},{1,2},{2,3},{3,4},{4,5},{5,6},{6,7},{7,0},{8,9},{9,10},{10,1... | collective-permute-start | bytes 319496 | tf_op jit(solution)/shard_map/ppermute | solution.py:32
  30.5 12.9 %collective-permute-start.6 = (bf16[176,128]{1,0:T(8,128)(2,1)S(1)}, bf16[176,128]{1,0:T(8,128)(2,1)S(1)}, u32[]{:S(2)}, u32[]{:S(2)}) collective-permute-start(bf16[176,128]{1,0:T(8,128)(2,1)S(1)} %get-tuple-element.68), channel_id=1, source_target_pairs={{0,7},{1,0},{2,1},{3,2},{4,3},{5,4},{6,5},{7,6},{8,15},{9,8},{10,9... | collective-permute-start | bytes 135176 | tf_op jit(solution)/shard_map/ppermute | solution.py:32
  43.7 6.1 %collective-permute-start.9 = (bf16[416,128]{1,0:T(8,128)(2,1)S(1)}, bf16[416,128]{1,0:T(8,128)(2,1)S(1)}, u32[]{:S(2)}, u32[]{:S(2)}) collective-permute-start(bf16[416,128]{1,0:T(8,128)(2,1)S(1)} %get-tuple-element.74), channel_id=1, source_target_pairs={{0,1},{1,2},{2,3},{3,4},{4,5},{5,6},{6,7},{7,0},{8,9},{9,10},{10,1... | collective-permute-start | bytes 319496 | tf_op jit(solution)/shard_map/ppermute | solution.py:32
  45.1 4.0 %collective-permute-start.8 = (bf16[176,128]{1,0:T(8,128)(2,1)S(1)}, bf16[176,128]{1,0:T(8,128)(2,1)S(1)}, u32[]{:S(2)}, u32[]{:S(2)}) collective-permute-start(bf16[176,128]{1,0:T(8,128)(2,1)S(1)} %get-tuple-element.73), channel_id=1, source_target_pairs={{0,7},{1,0},{2,1},{3,2},{4,3},{5,4},{6,5},{7,6},{8,15},{9,8},{10,9... | collective-permute-start | bytes 135176 | tf_op jit(solution)/shard_map/ppermute | solution.py:32

commit v6 on v5

--- a/solution.py
+++ b/solution.py
@@ -67,10 +67,12 @@
     return lax.dot_general(a, b, (((1,), (1,)), ((), ())), preferred_element_type=F32)
 
 
-def vmem_call(kernel, out_shape, scratch=(), in_specs=None, cost=None):
+def vmem_call(kernel, out_shape, scratch=(), in_specs=None, out_specs=None, cost=None):
     kwargs = {}
     if in_specs is not None:
         kwargs["in_specs"] = in_specs
+    if out_specs is not None:
+        kwargs["out_specs"] = out_specs
     return pl.pallas_call(
         kernel,
         out_shape=out_shape,
@@ -365,6 +367,10 @@
     if has_upper:
         uppers, refs = refs[:n], refs[n:]
         own_up = refs.pop(0)
+    halo = (up_ref, dn_ref, crosses, behinds, uppers, own_up)
+    if mode == "last":
+        finish_last(geo, scale, base_ref, halo, *refs)
+        return
     if mode == "density":
         occ_ref, table_ref = refs.pop(0), refs.pop(0)
     if mode == "field":
@@ -374,22 +380,53 @@
         y_ref[...] = base_ref[...] + (column_ref[...] * scale) * before_ref[...]
     else:
         y_ref[...] = base_ref[...]
-    add_halo(geo, scale, y_ref, up_ref, dn_ref, crosses, behinds, uppers, own_up)
-    if mode != "last":
-        write_sends(geo, y_ref, refs[0], refs[1])
+    add_halo(geo, scale, y_ref, *halo)
     if mode == "density":
-        write_density(y_ref, occ_ref, table_ref, part_rows, refs[2])
-
-
-def finish(geo, scale, base, halo, crosses, behinds, uppers=(), own_up=None, density=None, field=None, last=False):
+        _, _, out_hbm, dens, sem = refs
+        write_density(y_ref, occ_ref, table_ref, part_rows, dens)
+        copy = pltpu.make_async_copy(dens, out_hbm, sem)
+        copy.start()
+    write_sends(geo, y_ref, refs[0], refs[1])
+    if mode == "density":
+        copy.wait()
+
+
+def finish_last(geo, scale, base_ref, halo, *refs):
+    extras = (len(refs) - 3) // 2
+    sources, out_hbm, targets = refs[:extras], refs[extras], refs[extras + 1 : -2]
+    y_ref, sems = refs[-2:]
+    top = max(geo.sp, geo.low)
+    inner = pl.ds(top, geo.dn_lo - top)
+    copies = fetch([(base_ref.at[inner], out_hbm.at[inner]), *zip(sources, targets)], sems)
+    edges = [(0, top), (geo.dn_lo, geo.own)]
+    for a, b in edges:
+        y_ref[a:b, :] = base_ref[a:b, :]
+    add_halo(geo, scale, y_ref, *halo)
+    for i, (a, b) in enumerate(edges):
+        edge = pl.ds(a, b - a)
+        copy = pltpu.make_async_copy(y_ref.at[edge], out_hbm.at[edge], sems.at[1 + extras + i])
+        copy.start()
+        copies.append(copy)
+    for copy in copies:
+        copy.wait()
+
+
+def finish(geo, scale, base, halo, crosses, behinds, uppers=(), own_up=None, density=None, field=None, last=None):
     columns = base.shape[1]
     args = [base, halo[0], halo[1], *crosses, *behinds, *uppers]
     if uppers:
         args.append(own_up)
+    mode, part_rows = "plain", 0
     shapes = [sds(base.shape, F32)]
-    mode, part_rows = "plain", 0
-    if last:
+    scratch = []
+    vmem, hbm = pl.BlockSpec(memory_space=pltpu.VMEM), pl.BlockSpec(memory_space=pltpu.HBM)
+    out_specs = [vmem, vmem, vmem]
+    if last is not None:
         mode = "last"
+        args += last
+        shapes += [sds(a.shape, a.dtype) for a in last]
+        out_specs = [hbm] * len(shapes)
+        scratch = [pltpu.VMEM(base.shape, F32), pltpu.SemaphoreType.DMA((3 + len(last),))]
     else:
         shapes += send_shapes(geo, columns)
     if field is not None:
@@ -400,10 +437,15 @@
         fg, weights, table = density
         part_rows = fg.part_rows
         args += [weights, table]
-        shapes.append(sds((fg.bands * fg.domains, 1, fg.width), F32))
+        spread = (fg.bands * fg.domains, 1, fg.width)
+        shapes.append(sds(spread, F32))
+        out_specs.append(hbm)
+        scratch = [pltpu.VMEM(spread, F32), pltpu.SemaphoreType.DMA(())]
     return vmem_call(
         functools.partial(finish_kernel, geo, scale, bool(uppers), mode, part_rows),
         shapes,
+        scratch,
+        out_specs=out_specs,
         cost=cost_of(1.0),
     )(*args)
 
@@ -576,15 +618,16 @@
         ahead = pltpu.roll(field[0], domains - 1, 0)
         upper = lookup([ahead], codes[fg.at_face])
         local = list(field) + [upper]
-        for c in range(cells):
-            for r in range(fg.rows):
+        for r in range(fg.rows):
+            for c in range(cells):
                 rows[c * domains : (c + 1) * domains, r * LANES : (r + 1) * LANES] = lookup(local, codes[c * fg.rows + r])
-        if copies:
-            copies.pop().wait()
-            full = matrix_ref[...]
-            top = full.astype(BF)
-            high_ref[...] = top
-            low_ref[...] = (full - top.astype(F32)).astype(BF)
+            if copies:
+                copies.pop(0).wait()
+                span = slice(r * LANES, min((r + 1) * LANES, fg.npc))
+                full = matrix_ref[span, :]
+                top = full.astype(BF)
+                high_ref[span, :] = top
+                low_ref[span, :] = (full - top.astype(F32)).astype(BF)
         picked = rows[:, 0 : fg.npc]
         high = picked.astype(BF)
         low = (picked - high.astype(F32)).astype(BF)
@@ -630,7 +673,8 @@
 
 
 def field_kernel(fg, got_ref, matrix_hbm, column_ref, hartree_ref, codes, rows, phi, mine, matrix_ref, high_ref, low_ref, sems):
-    copies = fetch([(matrix_hbm, matrix_ref)], sems)
+    spans = [pl.ds(r * LANES, min(LANES, fg.npc - r * LANES)) for r in range(fg.rows)]
+    copies = fetch([(matrix_hbm.at[span], matrix_ref.at[span]) for span in spans], sems)
     places, owner, screens = decode(fg, got_ref, codes)
     blocks = field_solve(fg, got_ref, codes, places, screens, matrix_ref, high_ref, low_ref, rows, copies)
     for q in range(fg.domains):
@@ -656,7 +700,7 @@
             pltpu.VMEM(matrix.shape, F32),
             pltpu.VMEM(matrix.shape, BF),
             pltpu.VMEM(matrix.shape, BF),
-            pltpu.SemaphoreType.DMA((1,)),
+            pltpu.SemaphoreType.DMA((fg.rows,)),
         ],
         in_specs=[pl.BlockSpec(memory_space=pltpu.VMEM), pl.BlockSpec(memory_space=pltpu.HBM)],
         cost=cost_of(4.0),
@@ -778,7 +822,6 @@
         halo = exchange((dn, up))
         base = owned_part(geo, first, y3, None, pot, None, mats, uppers)
         column, packed = field_step(fg, dens, pois_matrix)
-        hartree = packed.reshape(own)
         z1, *sends4 = finish(geo, first, base, halo, crosses, behinds, field=(column, y3))
     else:
         y3, *sends3 = finish(geo, later, base, halo, crosses, behinds)
@@ -792,7 +835,10 @@
 
     halo = exchange(sends4)
     base = owned_part(geo, later, z1, y3, pot, column, mats, uppers)
-    (filtered,) = finish(geo, later, base, halo, crosses, behinds, last=True)
+    last = [packed] if fg.fits else []
+    filtered, *rest = finish(geo, later, base, halo, crosses, behinds, last=last)
+    if fg.fits:
+        hartree = rest[0].reshape(own)
     return filtered, hartree
 
 

time: 51.1 us -> 50.4 us (0.986)
  Pallas kernels: 15.1 us -> 14.3 us
    pallas_call x1, Pallas kernels: 4.37 us -> 3.65 us  [field_step(): vmem_call(functools.partial(field_kernel, fg), [sds((fg.own, LANES), F32)...]
  transfers between devices with their start and end apart: 11 -> 11, of which waited for: 8 -> 8; matrix products, arithmetic and copies ran while one was open for 0% -> 0% of each run, Pallas kernels for 21% -> 20%
where the time goes in v6:
time: 50.4 us; the launch traced here: 50.1 us
  starting transfers between devices  24.6 us (49%)
  Pallas kernels  14.3 us (28%)
  waiting for transfers between devices  10.4 us (21%)
  between operations  0.78 us (2%)
    ppermute x10, starting transfers between devices, from_behind(): lax.ppermute(array, axis, [(i, (i + by) % length) for i in range(length)])  19 us
    ppermute x10, waiting for transfers between devices, from_behind(): lax.ppermute(array, axis, [(i, (i + by) % length) for i in range(length)])  5.67 us
    all_to_all x1, starting transfers between devices, on_device(): dens = lax.all_to_all(spread, ('band', 'domain'), 0, 0, tiled=True)  5.63 us
    all_to_all x1, waiting for transfers between devices, on_device(): dens = lax.all_to_all(spread, ('band', 'domain'), 0, 0, tiled=True)  4.73 us
    pallas_call x1, Pallas kernels, field_step(): vmem_call(functools.partial(field_kernel, fg), [sds((fg.own, LANES), F32)...  3.65 us
    pallas_call x5, Pallas kernels, finish(): vmem_call(functools.partial(finish_kernel, geo, scale, bool(uppers), mode...  3.25 us
    pallas_call x5, Pallas kernels, owned_part(): vmem_call(functools.partial(owned_part_kernel, geo, scale, prev is not No...  2.4 us
    pallas_call x1, Pallas kernels, own_matrices(): vmem_call(functools.partial(own_matrices_kernel, geo), shapes, [matrix_sc...  1.98 us
  transfers between devices with their start and end apart: 11, of which 8 were waited for; matrix products, arithmetic and copies ran while one was open for 0% of the time, Pallas kernels for 20%

profile of v6, /device:TPU:0, one launch (start us, length us, event | category | flops | bytes accessed | tf_op | source)
XLA Modules:
  0.0 50.1 jit_solution(6046019658888760171)
XLA Ops:
  0.6 1.3 %shard_map.122 = (bf16[464,128]{1,0:T(8,128)(2,1)S(1)}, bf16[176,128]{1,0:T(8,128)(2,1)S(1)}, f32[768,128]{1,0:T(8,128)S(1)}, s32[8,384]{1,0:T(8,128)S(1)}, bf16...) custom-call(f32[768,128]{1,0:T(8,128)} %y_hbm.1, ...), custom_call_target="tpu_custom_call" | custom-call | bytes 3000000 | tf_op jit(solution)/shard_map/pallas_call | solution.py:257
  1.9 0.5 %collective-permute-start.1 = (bf16[464,128]{1,0:T(8,128)(2,1)S(1)}, bf16[464,128]{1,0:T(8,128)(2,1)S(1)}, u32[]{:S(2)}, u32[]{:S(2)}) collective-permute-start(bf16[464,128]{1,0:T(8,128)(2,1)S(1)} %get-tuple-element.51), channel_id=1, source_target_pairs={{0,1},{1,2},{2,3},{3,4},{4,5},{5,6},{6,7},{7,0},{8,9},{9,10},{10,1... | collective-permute-start | bytes 356360 | tf_op jit(solution)/shard_map/ppermute | solution.py:32
  2.5 4.1 %collective-permute-start = (bf16[176,128]{1,0:T(8,128)(2,1)S(1)}, bf16[176,128]{1,0:T(8,128)(2,1)S(1)}, u32[]{:S(2)}, u32[]{:S(2)}) collective-permute-start(bf16[176,128]{1,0:T(8,128)(2,1)S(1)} %get-tuple-element.50.refs_9_), channel_id=1, source_target_pairs={{0,7},{1,0},{2,1},{3,2},{4,3},{5,4},{6,5},{7,6},{8,15},{9,8},{10,9... | collective-permute-start | bytes 135176 | tf_op jit(solution)/shard_map/ppermute | solution.py:32
  6.6 2.0 %shard_map.123 = (bf16[352,352]{1,0:T(8,128)(2,1)S(1)}, bf16[368,368]{1,0:T(8,128)(2,1)S(1)}, bf16[304,304]{1,0:T(8,128)(2,1)S(1)}, bf16[192,192]{1,0:T(8,128)(2...) custom-call(s32[8,384]{1,0:T(8,128)S(1)} %get-tuple-element.42.refs_0_, ...), custom_call_target="tpu_custom_call" | custom-call | bytes 6000000 | tf_op jit(solution)/shard_map/pallas_call | solution.py:164
  8.6 0.4 shard_map.124.refs_0_
  9.0 0.1 collective-permute-done.1.refs_0_.refs_2_
  9.1 1.0 %shard_map.125 = (bf16[176,304]{1,0:T(8,128)(2,1)S(1)}, bf16[176,192]{1,0:T(8,128)(2,1)S(1)}, bf16[176,176]{1,0:T(8,128)(2,1)S(1)}, bf16[176,176]{1,0:T(8,128)(2,1)S(1)}) custom-call(bf16[464,128]{1,0:T(8,128)(2,1)S(1)} %collective-permute-done.1.refs_0_.refs_2_, bf16[343,343]{1,0:T(8,128)(2,1)S(1)} %get-tuple-element.43.refs_1_), custom_call_target="tpu_custom_call" | custom-call | bytes 3000000 | tf_op jit(solution)/shard_map/pallas_call | solution.py:197
  10.2 0.0 collective-permute-done.refs_1_
  10.2 0.3 shard_map.126
  10.5 0.1 collective-permute-start.3
  10.6 3.5 %collective-permute-start.2 = (bf16[176,128]{1,0:T(8,128)(2,1)S(1)}, bf16[176,128]{1,0:T(8,128)(2,1)S(1)}, u32[]{:S(2)}, u32[]{:S(2)}) collective-permute-start(bf16[176,128]{1,0:T(8,128)(2,1)S(1)} %get-tuple-element.59), channel_id=1, source_target_pairs={{0,7},{1,0},{2,1},{3,2},{4,3},{5,4},{6,5},{7,6},{8,15},{9,8},{10,9... | collective-permute-start | bytes 135176 | tf_op jit(solution)/shard_map/ppermute | solution.py:32
  14.1 0.5 shard_map.127.refs_0_.refs_4_
  14.6 1.2 %collective-permute-done.2.refs_1_ = bf16[176,128]{1,0:T(8,128)(2,1)S(1)} collective-permute-done((bf16[176,128]{1,0:T(8,128)(2,1)S(1)}, bf16[176,128]{1,0:T(8,128)(2,1)S(1)}, u32[]{:S(2)}, u32[]{:S(2)}) %collective-permute-start.2) | collective-permute-done | bytes 45088 | tf_op jit(solution)/shard_map/ppermute | solution.py:32
  15.8 1.1 %collective-permute-done.3.refs_2_ = bf16[416,128]{1,0:T(8,128)(2,1)S(1)} collective-permute-done((bf16[416,128]{1,0:T(8,128)(2,1)S(1)}, bf16[416,128]{1,0:T(8,128)(2,1)S(1)}, u32[]{:S(2)}, u32[]{:S(2)}) %collective-permute-start.3) | collective-permute-done | bytes 106528 | tf_op jit(solution)/shard_map/ppermute | solution.py:32
  16.9 0.3 shard_map.128
  17.2 0.1 collective-permute-start.5
  17.3 3.5 %collective-permute-start.4 = (bf16[176,128]{1,0:T(8,128)(2,1)S(1)}, bf16[176,128]{1,0:T(8,128)(2,1)S(1)}, u32[]{:S(2)}, u32[]{:S(2)}) collective-permute-start(bf16[176,128]{1,0:T(8,128)(2,1)S(1)} %get-tuple-element.62), channel_id=1, source_target_pairs={{0,7},{1,0},{2,1},{3,2},{4,3},{5,4},{6,5},{7,6},{8,15},{9,8},{10,9... | collective-permute-start | bytes 135176 | tf_op jit(solution)/shard_map/ppermute | solution.py:32
  20.8 0.7 %shard_map.130.refs_8_ = f32[4,8,128]{2,1,0:T(8,128)S(1)} custom-call(s32[2,729]{1,0:T(2,128)S(1)} %get-tuple-element.65.refs_0_, s32[1,81]{1,0:T(1,128)S(1)} %get-tuple-element.66.refs_1_, s32[1,8]{1,0:T(1,128)S(1)} %get-tuple-element.67.refs_2_, f32[6,128]{1,0:T(8,128)S(1)} %get-tuple-element.68.refs_3_, f32[768,128]{1,0:T(8,128)S(1)} %shard_map.127.refs_0_.refs_4_), custom_call_target="tpu_custom_call" | custom-call | bytes 3000000 | tf_op jit(solution)/shard_map/pallas_call | solution.py:548
  21.5 0.5 shard_map.129.refs_0_
  22.0 0.5 %collective-permute-done.4.refs_1_ = bf16[176,128]{1,0:T(8,128)(2,1)S(1)} collective-permute-done((bf16[176,128]{1,0:T(8,128)(2,1)S(1)}, bf16[176,128]{1,0:T(8,128)(2,1)S(1)}, u32[]{:S(2)}, u32[]{:S(2)}) %collective-permute-start.4) | collective-permute-done | bytes 45088 | tf_op jit(solution)/shard_map/ppermute | solution.py:32
  22.5 0.8 %collective-permute-done.5.refs_2_ = bf16[416,128]{1,0:T(8,128)(2,1)S(1)} collective-permute-done((bf16[416,128]{1,0:T(8,128)(2,1)S(1)}, bf16[416,128]{1,0:T(8,128)(2,1)S(1)}, u32[]{:S(2)}, u32[]{:S(2)}) %collective-permute-start.5) | collective-permute-done | bytes 106528 | tf_op jit(solution)/shard_map/ppermute | solution.py:32
  23.3 1.3 %shard_map.131 = (f32[768,128]{1,0:T(8,128)S(1)}, bf16[416,128]{1,0:T(8,128)(2,1)S(1)}, bf16[176,128]{1,0:T(8,128)(2,1)S(1)}, f32[32,1,1536]{2,1,0:T(1,128)}) custom-call(f32[768,128]{1,0:T(8,128)S(1)} %shard_map.129.refs_0_, bf16[176,128]{1,0:T(8,128)(2,1)S(1)} %collective-permute-done.4.refs_1_, bf16[416,128]{1,0:T(8,128)(2,1)S(1)} %collective-permute-done.5.refs_2_, ...), custom_call_target="tpu_custom_call" | custom-call | bytes 3000000 | tf_op jit(solution)/shard_map/pallas_call | solution.py:444
  24.6 5.6 %all-to-all-start = ((f32[32,1,1536]{2,1,0:T(1,128)}), f32[32,1,1536]{2,1,0:T(1,128)S(1)}, u32[]{:S(2)}, u32[]{:S(2)}) async-start(f32[32,1,1536]{2,1,0:T(1,128)} %get-tuple-element.72), calls=%async_computation | async-start | bytes 393216 | tf_op jit(solution)/shard_map/all_to_all | solution.py:821
  30.2 0.3 collective-permute-start.7
  30.5 3.3 %collective-permute-start.6 = (bf16[176,128]{1,0:T(8,128)(2,1)S(1)}, bf16[176,128]{1,0:T(8,128)(2,1)S(1)}, u32[]{:S(2)}, u32[]{:S(2)}) collective-permute-start(bf16[176,128]{1,0:T(8,128)(2,1)S(1)} %get-tuple-element.70), channel_id=1, source_target_pairs={{0,7},{1,0},{2,1},{3,2},{4,3},{5,4},{6,5},{7,6},{8,15},{9,8},{10,9... | collective-permute-start | bytes 135176 | tf_op jit(solution)/shard_map/ppermute | solution.py:32
  33.8 0.5 shard_map.132.refs_0_
  34.3 4.7 %all-to-all-done.got_ref = f32[32,1,1536]{2,1,0:T(1,128)S(1)} async-done(((f32[32,1,1536]{2,1,0:T(1,128)}), f32[32,1,1536]{2,1,0:T(1,128)S(1)}, u32[]{:S(2)}, u32[]{:S(2)}) %all-to-all-start) | async-done | bytes 196640 | tf_op jit(solution)/shard_map/all_to_all | solution.py:821
  39.0 3.7 %shard_map.133 = (f32[768,128]{1,0:T(8,128)S(1)}, f32[6,128]{1,0:T(8,128)S(1)}) custom-call(f32[32,1,1536]{2,1,0:T(1,128)S(1)} %all-to-all-done.got_ref, f32[729,729]{1,0:T(8,128)} %matrix_hbm.1), custom_call_target="tpu_custom_call" | custom-call | bytes 12000000 | tf_op jit(solution)/shard_map/pallas_call | solution.py:692
  42.7 0.0 collective-permute-done.6.refs_1_
  42.7 0.0 collective-permute-done.7.refs_2_
  42.7 0.3 shard_map.134
  43.0 1.3 %collective-permute-start.9 = (bf16[416,128]{1,0:T(8,128)(2,1)S(1)}, bf16[416,128]{1,0:T(8,128)(2,1)S(1)}, u32[]{:S(2)}, u32[]{:S(2)}) collective-permute-start(bf16[416,128]{1,0:T(8,128)(2,1)S(1)} %get-tuple-element.76), channel_id=1, source_target_pairs={{0,1},{1,2},{2,3},{3,4},{4,5},{5,6},{6,7},{7,0},{8,9},{9,10},{10,1... | collective-permute-start | bytes 319496 | tf_op jit(solution)/shard_map/ppermute | solution.py:32
  44.3 2.3 %collective-permute-start.8 = (bf16[176,128]{1,0:T(8,128)(2,1)S(1)}, bf16[176,128]{1,0:T(8,128)(2,1)S(1)}, u32[]{:S(2)}, u32[]{:S(2)}) collective-permute-start(bf16[176,128]{1,0:T(8,128)(2,1)S(1)} %get-tuple-element.75), channel_id=1, source_target_pairs={{0,7},{1,0},{2,1},{3,2},{4,3},{5,4},{6,5},{7,6},{8,15},{9,8},{10,9... | collective-permute-start | bytes 135176 | tf_op jit(solution)/shard_map/ppermute | solution.py:32
  46.6 0.5 %shard_map.135.refs_0_ = f32[768,128]{1,0:T(8,128)S(1)} custom-call(f32[768,128]{1,0:T(8,128)S(1)} %get-tuple-element.74.refs_0_, f32[768,128]{1,0:T(8,128)S(1)} %get-tuple-element.69.refs_0_.refs_8_.refs_1_, f32[768,128]{1,0:T(8,128)S(1)} %get-tuple-element.45.refs_1_.refs_2_, f32[768,128]{1,0:T(8,128)S(1)} %get-tuple-element.73.refs_7_.refs_3_, ...), custom_call_target="tpu_custom_call" | custom-call | bytes 6000000 | tf_op jit(solution)/shard_map/pallas_call | solution.py:313
  47.1 1.2 %collective-permute-done.8.refs_1_ = bf16[176,128]{1,0:T(8,128)(2,1)S(1)} collective-permute-done((bf16[176,128]{1,0:T(8,128)(2,1)S(1)}, bf16[176,128]{1,0:T(8,128)(2,1)S(1)}, u32[]{:S(2)}, u32[]{:S(2)}) %collective-permute-start.8) | collective-permute-done | bytes 45088 | tf_op jit(solution)/shard_map/ppermute | solution.py:32
  48.3 0.8 %collective-permute-done.9.refs_2_ = bf16[416,128]{1,0:T(8,128)(2,1)S(1)} collective-permute-done((bf16[416,128]{1,0:T(8,128)(2,1)S(1)}, bf16[416,128]{1,0:T(8,128)(2,1)S(1)}, u32[]{:S(2)}, u32[]{:S(2)}) %collective-permute-start.9) | collective-permute-done | bytes 106528 | tf_op jit(solution)/shard_map/ppermute | solution.py:32
  49.1 1.0 %shard_map.136 = (f32[768,128]{1,0:T(8,128)}, f32[6,128]{1,0:T(8,128)}) custom-call(f32[768,128]{1,0:T(8,128)S(1)} %shard_map.135.refs_0_, bf16[176,128]{1,0:T(8,128)(2,1)S(1)} %collective-permute-done.8.refs_1_, bf16[416,128]{1,0:T(8,128)(2,1)S(1)} %collective-permute-done.9.refs_2_, bf16[304,176]{1,0:T(8,128)(2,1)S(1)} %get-tuple-element.52.refs_3_, ...), custom_call_target="tpu_custom_call" | custom-call | bytes 3000000 | tf_op jit(solution)/shard_map/pallas_call | solution.py:444
Async XLA Ops:
  1.9 7.2 %collective-permute-start.1 = (bf16[464,128]{1,0:T(8,128)(2,1)S(1)}, bf16[464,128]{1,0:T(8,128)(2,1)S(1)}, u32[]{:S(2)}, u32[]{:S(2)}) collective-permute-start(bf16[464,128]{1,0:T(8,128)(2,1)S(1)} %get-tuple-element.51), channel_id=1, source_target_pairs={{0,1},{1,2},{2,3},{3,4},{4,5},{5,6},{6,7},{7,0},{8,9},{9,10},{10,1... | collective-permute-start | bytes 356360 | tf_op jit(solution)/shard_map/ppermute | solution.py:32
  2.5 7.7 %collective-permute-start = (bf16[176,128]{1,0:T(8,128)(2,1)S(1)}, bf16[176,128]{1,0:T(8,128)(2,1)S(1)}, u32[]{:S(2)}, u32[]{:S(2)}) collective-permute-start(bf16[176,128]{1,0:T(8,128)(2,1)S(1)} %get-tuple-element.50.refs_9_), channel_id=1, source_target_pairs={{0,7},{1,0},{2,1},{3,2},{4,3},{5,4},{6,5},{7,6},{8,15},{9,8},{10,9... | collective-permute-start | bytes 135176 | tf_op jit(solution)/shard_map/ppermute | solution.py:32
  10.5 6.4 %collective-permute-start.3 = (bf16[416,128]{1,0:T(8,128)(2,1)S(1)}, bf16[416,128]{1,0:T(8,128)(2,1)S(1)}, u32[]{:S(2)}, u32[]{:S(2)}) collective-permute-start(bf16[416,128]{1,0:T(8,128)(2,1)S(1)} %get-tuple-element.60), channel_id=1, source_target_pairs={{0,1},{1,2},{2,3},{3,4},{4,5},{5,6},{6,7},{7,0},{8,9},{9,10},{10,1... | collective-permute-start | bytes 319496 | tf_op jit(solution)/shard_map/ppermute | solution.py:32
  10.6 5.2 %collective-permute-start.2 = (bf16[176,128]{1,0:T(8,128)(2,1)S(1)}, bf16[176,128]{1,0:T(8,128)(2,1)S(1)}, u32[]{:S(2)}, u32[]{:S(2)}) collective-permute-start(bf16[176,128]{1,0:T(8,128)(2,1)S(1)} %get-tuple-element.59), channel_id=1, source_target_pairs={{0,7},{1,0},{2,1},{3,2},{4,3},{5,4},{6,5},{7,6},{8,15},{9,8},{10,9... | collective-permute-start | bytes 135176 | tf_op jit(solution)/shard_map/ppermute | solution.py:32
  17.2 6.1 %collective-permute-start.5 = (bf16[416,128]{1,0:T(8,128)(2,1)S(1)}, bf16[416,128]{1,0:T(8,128)(2,1)S(1)}, u32[]{:S(2)}, u32[]{:S(2)}) collective-permute-start(bf16[416,128]{1,0:T(8,128)(2,1)S(1)} %get-tuple-element.63), channel_id=1, source_target_pairs={{0,1},{1,2},{2,3},{3,4},{4,5},{5,6},{6,7},{7,0},{8,9},{9,10},{10,1... | collective-permute-start | bytes 319496 | tf_op jit(solution)/shard_map/ppermute | solution.py:32
  17.3 5.2 %collective-permute-start.4 = (bf16[176,128]{1,0:T(8,128)(2,1)S(1)}, bf16[176,128]{1,0:T(8,128)(2,1)S(1)}, u32[]{:S(2)}, u32[]{:S(2)}) collective-permute-start(bf16[176,128]{1,0:T(8,128)(2,1)S(1)} %get-tuple-element.62), channel_id=1, source_target_pairs={{0,7},{1,0},{2,1},{3,2},{4,3},{5,4},{6,5},{7,6},{8,15},{9,8},{10,9... | collective-permute-start | bytes 135176 | tf_op jit(solution)/shard_map/ppermute | solution.py:32
  24.6 14.5 %all-to-all-start = ((f32[32,1,1536]{2,1,0:T(1,128)}), f32[32,1,1536]{2,1,0:T(1,128)S(1)}, u32[]{:S(2)}, u32[]{:S(2)}) async-start(f32[32,1,1536]{2,1,0:T(1,128)} %get-tuple-element.72), calls=%async_computation | async-start | bytes 393216 | tf_op jit(solution)/shard_map/all_to_all | solution.py:821
  30.2 12.5 %collective-permute-start.7 = (bf16[416,128]{1,0:T(8,128)(2,1)S(1)}, bf16[416,128]{1,0:T(8,128)(2,1)S(1)}, u32[]{:S(2)}, u32[]{:S(2)}) collective-permute-start(bf16[416,128]{1,0:T(8,128)(2,1)S(1)} %get-tuple-element.71), channel_id=1, source_target_pairs={{0,1},{1,2},{2,3},{3,4},{4,5},{5,6},{6,7},{7,0},{8,9},{9,10},{10,1... | collective-permute-start | bytes 319496 | tf_op jit(solution)/shard_map/ppermute | solution.py:32
  30.5 12.2 %collective-permute-start.6 = (bf16[176,128]{1,0:T(8,128)(2,1)S(1)}, bf16[176,128]{1,0:T(8,128)(2,1)S(1)}, u32[]{:S(2)}, u32[]{:S(2)}) collective-permute-start(bf16[176,128]{1,0:T(8,128)(2,1)S(1)} %get-tuple-element.70), channel_id=1, source_target_pairs={{0,7},{1,0},{2,1},{3,2},{4,3},{5,4},{6,5},{7,6},{8,15},{9,8},{10,9... | collective-permute-start | bytes 135176 | tf_op jit(solution)/shard_map/ppermute | solution.py:32
  43.0 6.1 %collective-permute-start.9 = (bf16[416,128]{1,0:T(8,128)(2,1)S(1)}, bf16[416,128]{1,0:T(8,128)(2,1)S(1)}, u32[]{:S(2)}, u32[]{:S(2)}) collective-permute-start(bf16[416,128]{1,0:T(8,128)(2,1)S(1)} %get-tuple-element.76), channel_id=1, source_target_pairs={{0,1},{1,2},{2,3},{3,4},{4,5},{5,6},{6,7},{7,0},{8,9},{9,10},{10,1... | collective-permute-start | bytes 319496 | tf_op jit(solution)/shard_map/ppermute | solution.py:32
  44.3 4.0 %collective-permute-start.8 = (bf16[176,128]{1,0:T(8,128)(2,1)S(1)}, bf16[176,128]{1,0:T(8,128)(2,1)S(1)}, u32[]{:S(2)}, u32[]{:S(2)}) collective-permute-start(bf16[176,128]{1,0:T(8,128)(2,1)S(1)} %get-tuple-element.75), channel_id=1, source_target_pairs={{0,7},{1,0},{2,1},{3,2},{4,3},{5,4},{6,5},{7,6},{8,15},{9,8},{10,9... | collective-permute-start | bytes 135176 | tf_op jit(solution)/shard_map/ppermute | solution.py:32

commit v7 on v6

--- a/solution.py
+++ b/solution.py
@@ -54,8 +54,8 @@
         self.dn_lo = min(self.windows[c].lo for c in self.touching)
         self.low = max(w.low for w in self.windows)
         self.dn_rows = own - self.dn_lo + self.low
-        self.table_rows = up_to(cells + 1, SUBLANES)
-        self.table_lanes = up_to(max(npc, share), LANES)
+        self.table_rows = up_to(cells, SUBLANES)
+        self.table_lanes = up_to(npc, LANES)
         self.table_tiles = self.table_lanes // LANES
 
 
@@ -96,10 +96,21 @@
     return jnp.where(ids == nodes, 1.0, 0.0).astype(BF)
 
 
-def place_table(geo, nodes_ref, face_ref, table):
+def place_table(geo, nodes_ref, face_ref, table, faces):
     table[...] = jnp.full(table.shape, -1, I32)
     table[0 : geo.cells, 0 : geo.npc] = nodes_ref[...]
-    table[geo.cells : geo.cells + 1, 0 : geo.share] = face_ref[...]
+    faces[...] = jnp.zeros(faces.shape, I32)
+    faces[0:1, 0 : geo.share] = face_ref[...]
+    for t in range(geo.table_tiles):
+        lanes = slice(t * LANES, (t + 1) * LANES)
+        nodes = table[:, lanes]
+        beyond = nodes - geo.own
+        at = jnp.bitwise_and(beyond, LANES - 1)
+        which = jnp.right_shift(beyond, 7)
+        for f in range(faces.shape[1] // LANES):
+            row = jnp.broadcast_to(faces[0:1, f * LANES : (f + 1) * LANES], nodes.shape)
+            nodes = jnp.where(which == f, lanes_of(row, at) + geo.own, nodes)
+        table[:, lanes] = nodes
 
 
 def place_matrix(geo, matrix_ref, matrix_pad):
@@ -118,10 +129,6 @@
 
 def nodes_of(geo, table, c):
     return table[c : c + 1, 0 : geo.npl]
-
-
-def face_of(geo, table):
-    return table[geo.cells : geo.cells + 1, 0 : up_to(geo.share, LANES)]
 
 
 def owned_picks(geo, c, nodes):
@@ -132,17 +139,14 @@
     return picks
 
 
-def upper_picks(geo, nodes, face):
-    by_local = one_hot_rows(face.shape[1], geo.own, nodes)
-    by_owner = one_hot_rows(geo.sp, 0, face)
-    return dot(by_owner, by_local).astype(BF)
+def upper_picks(geo, nodes):
+    return one_hot_rows(geo.sp, geo.own, nodes)
 
 
 def own_matrices_kernel(geo, *refs):
     table, matrix_ref, pot_ref = refs[:3]
     outs, matrix_pad = refs[3:-1], refs[-1]
     matrix = place_matrix(geo, matrix_ref, matrix_pad)
-    face = face_of(geo, table)
     for c in range(geo.cells):
         nodes = nodes_of(geo, table, c)
         own = owned_picks(geo, c, nodes)
@@ -150,7 +154,7 @@
         outs[c][...] = dot_t(left, own).astype(BF)
         if c in geo.touching:
             at = geo.cells + geo.touching.index(c)
-            outs[at][...] = dot_t(left, upper_picks(geo, nodes, face)).astype(BF)
+            outs[at][...] = dot_t(left, upper_picks(geo, nodes)).astype(BF)
     column = outs[-1]
     for r in range(geo.own // LANES):
         row = jnp.broadcast_to(pot_ref[r : r + 1, :], (LANES, LANES))
@@ -171,37 +175,25 @@
     return outs[:n], outs[n:-1], outs[-1]
 
 
-def behind_matrices_kernel(geo, *refs):
-    sent_ref, matrix_ref = refs[:2]
-    outs = refs[2:-2]
-    table, matrix_pad = refs[-2:]
+def build_behind(geo, sent_ref, matrix_ref, table, matrix_pad, outs):
     for t in range(geo.table_tiles):
         at = geo.dn_rows + 2 * t * geo.table_rows
         digits = sent_ref[at : at + 2 * geo.table_rows, :].astype(F32)
         value = digits[: geo.table_rows] * LANES + digits[geo.table_rows :] - 1.0
         table[:, t * LANES : (t + 1) * LANES] = value.astype(I32)
     matrix = place_matrix(geo, matrix_ref, matrix_pad)
-    face = face_of(geo, table)
     count = len(geo.touching)
     for at, c in enumerate(geo.touching):
         nodes = nodes_of(geo, table, c)
-        upper = upper_picks(geo, nodes, face)
+        upper = upper_picks(geo, nodes)
         left = dot(upper, matrix).astype(BF)
         outs[at][...] = dot_t(left, owned_picks(geo, c, nodes)).astype(BF)
         outs[count + at][...] = dot_t(left, upper).astype(BF)
 
 
-def behind_matrices(geo, sent, cell_matrix):
+def behind_shapes(geo):
     shapes = [sds((geo.sp, geo.windows[c].rows), BF) for c in geo.touching]
-    shapes += [sds((geo.sp, geo.sp), BF) for _ in geo.touching]
-    outs = vmem_call(
-        functools.partial(behind_matrices_kernel, geo),
-        shapes,
-        [table_scratch(geo), matrix_scratch(geo)],
-        cost=cost_of(1.0),
-    )(sent, cell_matrix)
-    n = len(geo.touching)
-    return outs[:n], outs[n:]
+    return shapes + [sds((geo.sp, geo.sp), BF) for _ in geo.touching]
 
 
 def cost_of(us):
@@ -229,7 +221,7 @@
 def pack_kernel(geo, extra, y_hbm, nodes_hbm, face_hbm, *refs):
     sources, refs = refs[:extra], refs[extra:]
     dn_ref, up_ref, y, table = refs[:4]
-    kept, (nodes, face, sems) = refs[4 : 4 + extra], refs[4 + extra :]
+    kept, (nodes, face, faces, sems) = refs[4 : 4 + extra], refs[4 + extra :]
     cuts = sorted({0, max(geo.sp, geo.low), geo.dn_lo, geo.own})
     spans = list(zip(cuts[:-1], cuts[1:]))
     pairs = [(nodes_hbm, nodes), (face_hbm, face)]
@@ -238,7 +230,7 @@
     copies = fetch(pairs, sems)
     copies[0].wait()
     copies[1].wait()
-    place_table(geo, nodes, face, table)
+    place_table(geo, nodes, face, table, faces)
     for t in range(geo.table_tiles):
         at = geo.dn_rows + 2 * t * geo.table_rows
         value = table[:, t * LANES : (t + 1) * LANES] + 1
@@ -266,6 +258,7 @@
         [
             pltpu.VMEM(cell_nodes.shape, I32),
             pltpu.VMEM(face_order.shape, I32),
+            pltpu.VMEM((1, up_to(geo.share, LANES)), I32),
             pltpu.SemaphoreType.DMA((5 + len(others),)),
         ],
         in_specs=[pl.BlockSpec(memory_space=pltpu.HBM)] * (3 + len(others)),
@@ -356,18 +349,37 @@
         dens_ref[:, 0, own + r * LANES : own + (r + 1) * LANES] = jnp.broadcast_to(row, (parts, LANES))
 
 
-def finish_kernel(geo, scale, has_upper, mode, part_rows, *refs):
+def first_finish_kernel(geo, scale, *refs):
+    n = len(geo.touching)
+    base_ref, up_ref, dn_ref, own_up_ref, matrix_ref = refs[:5]
+    crosses, (y_ref, dn_out, up_out) = refs[5 : 5 + n], refs[5 + n : 8 + n]
+    outs = refs[8 + n : 8 + 3 * n]
+    build_behind(geo, dn_ref, matrix_ref, *refs[-2:], outs)
+    y_ref[...] = base_ref[...]
+    add_halo(geo, scale, y_ref, up_ref, dn_ref, crosses, outs[:n], outs[n:], own_up_ref)
+    write_sends(geo, y_ref, dn_out, up_out)
+
+
+def first_finish(geo, scale, base, halo, own_up, matrix, crosses):
+    shapes = [sds(base.shape, F32), *send_shapes(geo, base.shape[1]), *behind_shapes(geo)]
+    y, dn, up, *outs = vmem_call(
+        functools.partial(first_finish_kernel, geo, scale),
+        shapes,
+        [table_scratch(geo), matrix_scratch(geo)],
+        cost=cost_of(1.5),
+    )(base, halo[0], halo[1], own_up, matrix, *crosses)
+    n = len(geo.touching)
+    return y, (dn, up), outs[:n], outs[n:]
+
+
+def finish_kernel(geo, scale, mode, part_rows, *refs):
     refs = list(refs)
     n = len(geo.touching)
     base_ref, up_ref, dn_ref = refs[:3]
     refs = refs[3:]
     crosses, refs = refs[:n], refs[n:]
     behinds, refs = refs[:n], refs[n:]
-    uppers, own_up = [], None
-    if has_upper:
-        uppers, refs = refs[:n], refs[n:]
-        own_up = refs.pop(0)
-    halo = (up_ref, dn_ref, crosses, behinds, uppers, own_up)
+    halo = (up_ref, dn_ref, crosses, behinds, (), None)
     if mode == "last":
         finish_last(geo, scale, base_ref, halo, *refs)
         return
@@ -411,11 +423,9 @@
         copy.wait()
 
 
-def finish(geo, scale, base, halo, crosses, behinds, uppers=(), own_up=None, density=None, field=None, last=None):
+def finish(geo, scale, base, halo, crosses, behinds, density=None, field=None, last=None):
     columns = base.shape[1]
-    args = [base, halo[0], halo[1], *crosses, *behinds, *uppers]
-    if uppers:
-        args.append(own_up)
+    args = [base, halo[0], halo[1], *crosses, *behinds]
     mode, part_rows = "plain", 0
     shapes = [sds(base.shape, F32)]
     scratch = []
@@ -442,7 +452,7 @@
         out_specs.append(hbm)
         scratch = [pltpu.VMEM(spread, F32), pltpu.SemaphoreType.DMA(())]
     return vmem_call(
-        functools.partial(finish_kernel, geo, scale, bool(uppers), mode, part_rows),
+        functools.partial(finish_kernel, geo, scale, mode, part_rows),
         shapes,
         scratch,
         out_specs=out_specs,
@@ -452,29 +462,32 @@
 
 class FieldGeometry:
     def __init__(self, bands, domains, own, share, cells, npc):
-        self.domains, self.own, self.share, self.cells, self.npc = domains, own, share, cells, npc
+        self.bands, self.domains, self.own, self.share = bands, domains, own, share
+        self.cells, self.npc = cells, npc
         self.block = own // domains
         self.rows = up_to(npc, LANES) // LANES
-        self.blocks = domains + 1
+        self.lines = own // LANES
+        self.tiles = self.lines + 1
+        nloc = own + share
+        self.touched = []
+        for c in range(cells):
+            nodes = [(c * (nloc // cells) + k) % nloc for k in range(npc)]
+            self.touched.append(sorted({node // LANES for node in nodes}))
         self.at_inverse = cells * self.rows
-        self.at_face = self.at_inverse + cells * self.blocks
-        self.at_face_inverse = self.at_face + 1
-        self.at_owner = self.at_face + 2
-        self.at_owner_inverse = self.at_face + 3
-        self.codes = self.at_face + 4
-        self.at_screen = up_to(self.codes, 2) // 2
-        self.lines = own // LANES
+        self.at_face = self.at_inverse + cells * self.tiles
+        self.at_screen = up_to(self.at_face + 2, 2) // 2
         self.part_rows = -(-(self.at_screen + self.lines) // bands)
         self.table_rows = up_to(self.part_rows * bands, SUBLANES)
-        self.bands = bands
         self.width = own + self.part_rows * LANES
         self.size = self.rows * LANES
+        self.at_owner_lane = LANES - domains
         self.fits = (
             domains == SUBLANES
             and own % (domains * SUBLANES) == 0
             and own % LANES == 0
-            and share <= self.block <= LANES
-            and max(npc, self.blocks * LANES) < CODE_BASE - 1
+            and self.block <= LANES
+            and share <= self.at_owner_lane
+            and max(npc, nloc) < CODE_BASE - 1
         )
 
 
@@ -498,43 +511,41 @@
     return jnp.broadcast_to(row, (LANES, LANES)).T
 
 
+def inverse_row(columns, first):
+    sub = lax.broadcasted_iota(I32, (LANES, LANES), 0)
+    target = (lax.broadcasted_iota(I32, (LANES, LANES), 1) + first).astype(F32)
+    found = jnp.zeros((LANES, LANES), F32)
+    for r, column in enumerate(columns):
+        found = jnp.where(column == target, (sub + (r * LANES + 1)).astype(F32), found)
+    return jnp.sum(found, axis=0, keepdims=True) - 1.0
+
+
 def field_tables_kernel(fg, *refs):
     nodes_ref, face_ref, owner_ref, screen_ref = refs[:4]
-    table_ref, pad, one, packed = refs[5:]
+    table_ref, pad, one, spare, packed = refs[5:]
     one[...] = jnp.full(one.shape, -1.0, F32)
+    spare[...] = jnp.full(spare.shape, -1.0, F32)
     pad[...] = jnp.full(pad.shape, -1, I32)
     pad[0 : fg.cells, 0 : fg.npc] = nodes_ref[...]
-    sub = lax.broadcasted_iota(I32, (LANES, LANES), 0)
-    wide_lane = lax.broadcasted_iota(I32, (LANES, LANES), 1)
     for c in range(fg.cells):
         columns = []
         for r in range(fg.rows):
-            nodes = pad[c : c + 1, r * LANES : (r + 1) * LANES]
-            block = jnp.zeros((1, LANES), I32)
-            for b in range(1, fg.blocks):
-                block = block + jnp.where(nodes >= b * fg.block, 1, 0)
-            code = jnp.where(nodes < 0, -1, nodes + block * (LANES - fg.block))
-            code = code.astype(F32)
-            at = c * fg.rows + r
-            one[at : at + 1, :] = code
+            code = pad[c : c + 1, r * LANES : (r + 1) * LANES].astype(F32)
+            one[c * fg.rows + r : c * fg.rows + r + 1, :] = code
             columns.append(column_of(code))
-        for b in range(fg.blocks):
-            target = (wide_lane + b * LANES).astype(F32)
-            found = jnp.zeros((LANES, LANES), F32)
-            for r in range(fg.rows):
-                position = (sub + (r * LANES + 1)).astype(F32)
-                found = jnp.where(columns[r] == target, position, found)
-            at = fg.at_inverse + c * fg.blocks + b
-            one[at : at + 1, :] = jnp.sum(found, axis=0, keepdims=True) - 1.0
-    one[fg.at_face : fg.at_face + 1, 0 : fg.share] = face_ref[...].astype(F32)
-    column = column_of(one[fg.at_face : fg.at_face + 1, :])
-    hits = jnp.where(column == wide_lane.astype(F32), (sub + 1).astype(F32), 0.0)
-    one[fg.at_face_inverse : fg.at_face_inverse + 1, :] = jnp.sum(hits, axis=0, keepdims=True) - 1.0
-    one[fg.at_owner : fg.at_owner + 1, 0 : fg.domains] = owner_ref[...].astype(F32)
-    column = column_of(one[fg.at_owner : fg.at_owner + 1, :])
-    hits = jnp.where(column == wide_lane.astype(F32), (sub + 1).astype(F32), 0.0)
-    hits = jnp.where(sub < fg.domains, hits, 0.0)
-    one[fg.at_owner_inverse : fg.at_owner_inverse + 1, :] = jnp.sum(hits, axis=0, keepdims=True) - 1.0
+        for t in fg.touched[c]:
+            at = fg.at_inverse + c * fg.tiles + t
+            one[at : at + 1, :] = inverse_row(columns, t * LANES)
+    lane = fg.at_owner_lane
+    spare[0:1, 0 : fg.share] = face_ref[...].astype(F32)
+    spare[1:2, 0 : fg.domains] = owner_ref[...].astype(F32)
+    at = fg.at_face
+    one[at : at + 1, :] = spare[0:1, :]
+    one[at : at + 1, lane:LANES] = owner_ref[...].astype(F32)
+    back = inverse_row([column_of(spare[0:1, :])], 0)
+    home = inverse_row([column_of(spare[1:2, :])], -lane)
+    lanes = lax.broadcasted_iota(I32, (1, LANES), 1)
+    one[at + 1 : at + 2, :] = jnp.where(lanes < lane, back, home)
     packed[...] = jnp.zeros(packed.shape, F32)
     half = fg.at_screen
     packed[0:half, :] = (one[0:half, :] + 1.0) + (one[half : 2 * half, :] + 1.0) * CODE_BASE
@@ -551,6 +562,7 @@
         [
             pltpu.VMEM((up_to(fg.cells, SUBLANES), fg.size), I32),
             pltpu.VMEM((up_to(2 * fg.at_screen, SUBLANES), LANES), F32),
+            pltpu.VMEM((SUBLANES, LANES), F32),
             pltpu.VMEM((fg.table_rows, LANES), F32),
         ],
         in_specs=specs,
@@ -572,26 +584,19 @@
 
     for at in range(half):
         both = tile(at).astype(I32)
-        low = jnp.bitwise_and(both, CODE_BASE - 1) - 1
-        codes[at] = low
+        codes[at] = jnp.bitwise_and(both, CODE_BASE - 1) - 1
         codes[half + at] = jnp.right_shift(both, CODE_BITS) - 1
-    codes[fg.at_face_inverse] = pltpu.roll(codes[fg.at_face_inverse], 1, 0)
-    lines = [tile(half + g) for g in range(fg.lines)]
+    screens = [tile(half + g) for g in range(fg.lines)]
     lane = lax.broadcasted_iota(I32, (domains, LANES), 1)
-    screens = []
-    for q in range(domains):
-        screen = jnp.zeros((domains, LANES), F32)
-        for row, start, j, offset, count in pieces(fg.block, domains):
-            if j == q:
-                moved = pltpu.roll(lines[row], (offset - start) % LANES, 1)
-                screen = jnp.where((lane >= offset) & (lane < offset + count), moved, screen)
-        screens.append(screen)
-    inverse = codes[fg.at_owner_inverse].astype(F32).T[0:domains, :]
+    first, last = fg.at_owner_lane, LANES
+    owners = codes[fg.at_face].astype(F32).T[first:last, :]
+    inverse = codes[fg.at_face + 1].astype(F32).T[first:last, :]
+    back = jnp.where(lane < fg.share, codes[fg.at_face + 1], -1)
+    codes[fg.at_face + 1] = pltpu.roll(back, 1, 0)
     places = []
     for q in range(domains):
         block = jnp.broadcast_to(inverse[:, q : q + 1], (domains, LANES)).astype(I32)
         places.append(block * fg.block + lane)
-    owners = codes[fg.at_owner].astype(F32).T[0:domains, :]
     here = lax.axis_index("domain")
     narrow = lax.broadcasted_iota(I32, (domains, domains), 1)
     mine = jnp.sum(jnp.where(narrow == here, owners, 0.0), axis=1, keepdims=True)
@@ -602,25 +607,48 @@
     return jnp.take_along_axis(values, index, axis=0, mode="promise_in_bounds")
 
 
-def field_solve(fg, got_ref, codes, places, screen, matrix_ref, high_ref, low_ref, rows, copies):
+def lookup(sources, code):
+    lane = jnp.bitwise_and(code, LANES - 1)
+    which = jnp.right_shift(code, 7)
+    total = jnp.zeros(code.shape, F32)
+    for b, values in sources:
+        total = jnp.where(which == b, lanes_of(values, lane), total)
+    return total
+
+
+def field_source(fg, got_ref, places):
+    domains = fg.domains
+    density = []
+    for g in range(fg.lines):
+        at = slice(g * LANES, (g + 1) * LANES)
+        total = got_ref[0:domains, 0, at]
+        for b in range(1, fg.bands):
+            total = total + got_ref[b * domains : (b + 1) * domains, 0, at]
+        density.append(total)
+    lane = lax.broadcasted_iota(I32, (domains, LANES), 1)
+    source = [None] * fg.lines
+    for q in range(domains):
+        spread = [jnp.broadcast_to(d[q : q + 1, :], (domains, LANES)) for d in density]
+        block = lookup(list(enumerate(spread)), places[q])
+        for row, start, j, offset, count in pieces(fg.block, domains):
+            if j == q:
+                moved = pltpu.roll(block, (start - offset) % LANES, 1)
+                inside = (lane >= start) & (lane < start + count)
+                before = 0.0 if source[row] is None else source[row]
+                source[row] = jnp.where(inside, moved, before)
+    return source
+
+
+def field_solve(fg, source, codes, screen, matrix_ref, high_ref, low_ref, rows, copies):
     domains, cells = fg.domains, fg.cells
-    valid = lax.broadcasted_iota(I32, (domains, LANES), 1) < fg.block
-
-    def lookup(sources, code):
-        lane = jnp.bitwise_and(code, LANES - 1)
-        which = jnp.right_shift(code, 7)
-        total = jnp.zeros((domains, LANES), F32)
-        for b, values in enumerate(sources):
-            total = jnp.where(which == b, lanes_of(values, lane), total)
-        return total
 
     def operator(field):
         ahead = pltpu.roll(field[0], domains - 1, 0)
-        upper = lookup([ahead], codes[fg.at_face])
-        local = list(field) + [upper]
+        local = list(field) + [lookup([(0, ahead)], codes[fg.at_face])]
         for r in range(fg.rows):
             for c in range(cells):
-                rows[c * domains : (c + 1) * domains, r * LANES : (r + 1) * LANES] = lookup(local, codes[c * fg.rows + r])
+                sources = [(t, local[t]) for t in fg.touched[c]]
+                rows[c * domains : (c + 1) * domains, r * LANES : (r + 1) * LANES] = lookup(sources, codes[c * fg.rows + r])
             if copies:
                 copies.pop(0).wait()
                 span = slice(r * LANES, min((r + 1) * LANES, fg.npc))
@@ -634,32 +662,19 @@
         both = dot(jnp.concatenate([high, low], axis=0), high_ref[...])
         half_rows = cells * domains
         rows[:, 0 : fg.npc] = both[:half_rows] + (both[half_rows:] + dot(high, low_ref[...]))
-        out = []
-        for b in range(fg.blocks):
-            total = None
-            for c in range(cells):
-                sources = [
-                    rows[c * domains : (c + 1) * domains, r * LANES : (r + 1) * LANES]
-                    for r in range(fg.rows)
-                ]
-                term = lookup(sources, codes[fg.at_inverse + c * fg.blocks + b])
-                total = term if total is None else total + term
-            out.append(total)
-        arriving = pltpu.roll(out[domains], 1, 0)
-        out[0] = out[0] + lookup([arriving], codes[fg.at_face_inverse])
-        return [jnp.where(valid, screen[q] * field[q] + out[q], 0.0) for q in range(domains)]
-
-    density = []
-    for g in range(fg.lines):
-        at = slice(g * LANES, (g + 1) * LANES)
-        total = got_ref[0:domains, 0, at]
-        for b in range(1, fg.bands):
-            total = total + got_ref[b * domains : (b + 1) * domains, 0, at]
-        density.append(total)
-    source = []
-    for q in range(domains):
-        spread = [jnp.broadcast_to(d[q : q + 1, :], (domains, LANES)) for d in density]
-        source.append(jnp.where(valid, lookup(spread, places[q]), 0.0))
+        out = [None] * fg.tiles
+        for c in range(cells):
+            sources = [
+                (r, rows[c * domains : (c + 1) * domains, r * LANES : (r + 1) * LANES])
+                for r in range(fg.rows)
+            ]
+            for t in fg.touched[c]:
+                term = lookup(sources, codes[fg.at_inverse + c * fg.tiles + t])
+                out[t] = term if out[t] is None else out[t] + term
+        arriving = pltpu.roll(out[fg.lines], 1, 0)
+        out[0] = out[0] + lookup([(0, arriving)], codes[fg.at_face + 1])
+        return [screen[g] * field[g] + out[g] for g in range(fg.lines)]
+
     step_one = [s * (1.0 / solve_center) for s in source]
     applied = operator(step_one)
     residual = [s - a for s, a in zip(source, applied)]
@@ -672,19 +687,20 @@
     return [(x + y) + z for x, y, z in zip(step_one, step_two, step_three)]
 
 
-def field_kernel(fg, got_ref, matrix_hbm, column_ref, hartree_ref, codes, rows, phi, mine, matrix_ref, high_ref, low_ref, sems):
+def field_kernel(fg, got_ref, matrix_hbm, column_ref, hartree_ref, codes, rows, mine, matrix_ref, high_ref, low_ref, sems):
     spans = [pl.ds(r * LANES, min(LANES, fg.npc - r * LANES)) for r in range(fg.rows)]
     copies = fetch([(matrix_hbm.at[span], matrix_ref.at[span]) for span in spans], sems)
     places, owner, screens = decode(fg, got_ref, codes)
-    blocks = field_solve(fg, got_ref, codes, places, screens, matrix_ref, high_ref, low_ref, rows, copies)
-    for q in range(fg.domains):
-        phi[q] = blocks[q]
-    mine[...] = rows_of(phi[lax.axis_index("domain")], owner)
+    source = field_source(fg, got_ref, places)
+    solved = field_solve(fg, source, codes, screens, matrix_ref, high_ref, low_ref, rows, copies)
+    lane = lax.broadcasted_iota(I32, (fg.domains, LANES), 1)
+    block = lookup(list(enumerate(solved)), lane + lax.axis_index("domain") * fg.block)
+    mine[...] = rows_of(block, owner)
     for j in range(fg.domains):
         column = column_of(mine[j : j + 1, :])
         column_ref[j * fg.block : (j + 1) * fg.block, :] = column[0 : fg.block, :]
-    for row, lane, j, offset, count in pieces(fg.block, fg.domains):
-        hartree_ref[row : row + 1, lane : lane + count] = mine[j : j + 1, offset : offset + count]
+    for row, start, j, offset, count in pieces(fg.block, fg.domains):
+        hartree_ref[row : row + 1, start : start + count] = mine[j : j + 1, offset : offset + count]
 
 
 def field_step(fg, got, matrix):
@@ -695,7 +711,6 @@
         [
             pltpu.VMEM((2 * fg.at_screen, *tile), I32),
             pltpu.VMEM((fg.cells * fg.domains, fg.size), F32),
-            pltpu.VMEM((fg.domains, *tile), F32),
             pltpu.VMEM(tile, F32),
             pltpu.VMEM(matrix.shape, F32),
             pltpu.VMEM(matrix.shape, BF),
@@ -802,8 +817,7 @@
     halo = exchange(sends)
     mats, crosses, pot = own_matrices(geo, nodes, matrix, lines)
     base = owned_part(geo, first, y0, None, pot, None, mats, ())
-    behinds, uppers = behind_matrices(geo, halo[1], matrix)
-    y1, *sends1 = finish(geo, first, base, halo, crosses, behinds, uppers, sends[1])
+    y1, sends1, behinds, uppers = first_finish(geo, first, base, halo, sends[1], matrix, crosses)
 
     halo = exchange(sends1)
     base = owned_part(geo, later, y1, y0, pot, None, mats, uppers)

time: 50.4 us -> 49.7 us (0.986)
  Pallas kernels: 14.3 us -> 13.4 us
    pallas_call x6 -> x5, Pallas kernels: 4.28 us -> 3.86 us  [the longest x4 2.9 us: finish(): vmem_call(functools.partial(finish_kernel, geo, scale, mode, part_rows),...]
  transfers between devices with their start and end apart: 11 -> 11, of which waited for: 8 -> 8; matrix products, arithmetic and copies ran while one was open for 0% -> 0% of each run, Pallas kernels for 20% -> 17%
where the time goes in v7:
time: 49.7 us; the launch traced here: 49.4 us
  starting transfers between devices  24.6 us (49%)
  Pallas kernels  13.4 us (27%)
  waiting for transfers between devices  10.7 us (22%)
  between operations  0.76 us (2%)
    ppermute x10, starting transfers between devices, from_behind(): lax.ppermute(array, axis, [(i, (i + by) % length) for i in range(length)])  19 us
    ppermute x10, waiting for transfers between devices, from_behind(): lax.ppermute(array, axis, [(i, (i + by) % length) for i in range(length)])  6.08 us
    all_to_all x1, starting transfers between devices, on_device(): dens = lax.all_to_all(spread, ('band', 'domain'), 0, 0, tiled=True)  5.63 us
    all_to_all x1, waiting for transfers between devices, on_device(): dens = lax.all_to_all(spread, ('band', 'domain'), 0, 0, tiled=True)  4.59 us
    pallas_call x1, Pallas kernels, field_step(): vmem_call(functools.partial(field_kernel, fg), [sds((fg.own, LANES), F32)...  3.56 us
    pallas_call x4, Pallas kernels, finish(): vmem_call(functools.partial(finish_kernel, geo, scale, mode, part_rows),...  2.9 us
    pallas_call x5, Pallas kernels, owned_part(): vmem_call(functools.partial(owned_part_kernel, geo, scale, prev is not No...  2.41 us
    pallas_call x1, Pallas kernels, own_matrices(): vmem_call(functools.partial(own_matrices_kernel, geo), shapes, [matrix_sc...  1.72 us
  transfers between devices with their start and end apart: 11, of which 8 were waited for; matrix products, arithmetic and copies ran while one was open for 0% of the time, Pallas kernels for 17%

profile of v7, /device:TPU:0, one launch (start us, length us, event | category | flops | bytes accessed | tf_op | source)
XLA Modules:
  0.0 49.4 jit_solution(7106574485400833790)
XLA Ops:
  0.6 1.3 %shard_map.122 = (bf16[464,128]{1,0:T(8,128)(2,1)S(1)}, bf16[176,128]{1,0:T(8,128)(2,1)S(1)}, f32[768,128]{1,0:T(8,128)S(1)}, s32[8,384]{1,0:T(8,128)S(1)}, bf16...) custom-call(f32[768,128]{1,0:T(8,128)} %y_hbm.1, ...), custom_call_target="tpu_custom_call" | custom-call | bytes 3000000 | tf_op jit(solution)/shard_map/pallas_call | solution.py:249
  1.9 0.5 %collective-permute-start.1 = (bf16[464,128]{1,0:T(8,128)(2,1)S(1)}, bf16[464,128]{1,0:T(8,128)(2,1)S(1)}, u32[]{:S(2)}, u32[]{:S(2)}) collective-permute-start(bf16[464,128]{1,0:T(8,128)(2,1)S(1)} %get-tuple-element.51), channel_id=1, source_target_pairs={{0,1},{1,2},{2,3},{3,4},{4,5},{5,6},{6,7},{7,0},{8,9},{9,10},{10,1... | collective-permute-start | bytes 356360 | tf_op jit(solution)/shard_map/ppermute | solution.py:32
  2.5 4.1 %collective-permute-start = (bf16[176,128]{1,0:T(8,128)(2,1)S(1)}, bf16[176,128]{1,0:T(8,128)(2,1)S(1)}, u32[]{:S(2)}, u32[]{:S(2)}) collective-permute-start(bf16[176,128]{1,0:T(8,128)(2,1)S(1)} %get-tuple-element.50.refs_3_), channel_id=1, source_target_pairs={{0,7},{1,0},{2,1},{3,2},{4,3},{5,4},{6,5},{7,6},{8,15},{9,8},{10,9... | collective-permute-start | bytes 135176 | tf_op jit(solution)/shard_map/ppermute | solution.py:32
  6.6 1.7 %shard_map.123 = (bf16[352,352]{1,0:T(8,128)(2,1)S(1)}, bf16[368,368]{1,0:T(8,128)(2,1)S(1)}, bf16[304,304]{1,0:T(8,128)(2,1)S(1)}, bf16[192,192]{1,0:T(8,128)(2...) custom-call(s32[8,384]{1,0:T(8,128)S(1)} %get-tuple-element.42.refs_0_, ...), custom_call_target="tpu_custom_call" | custom-call | bytes 6000000 | tf_op jit(solution)/shard_map/pallas_call | solution.py:168
  8.3 0.4 shard_map.124.refs_0_
  8.8 0.0 collective-permute-done.refs_1_
  8.8 0.3 collective-permute-done.1.refs_2_
  9.1 1.0 %shard_map.125 = (f32[768,128]{1,0:T(8,128)S(1)}, bf16[416,128]{1,0:T(8,128)(2,1)S(1)}, bf16[176,128]{1,0:T(8,128)(2,1)S(1)}, bf16[176,304]{1,0:T(8,128)(2,1)S(1...) custom-call(f32[768,128]{1,0:T(8,128)S(1)} %shard_map.124.refs_0_, ...), custom_call_target="tpu_custom_call" | custom-call | bytes 4500000 | tf_op jit(solution)/shard_map/pallas_call | solution.py:365
  10.1 0.3 collective-permute-start.3
  10.4 3.3 %collective-permute-start.2 = (bf16[176,128]{1,0:T(8,128)(2,1)S(1)}, bf16[176,128]{1,0:T(8,128)(2,1)S(1)}, u32[]{:S(2)}, u32[]{:S(2)}) collective-permute-start(bf16[176,128]{1,0:T(8,128)(2,1)S(1)} %get-tuple-element.57), channel_id=1, source_target_pairs={{0,7},{1,0},{2,1},{3,2},{4,3},{5,4},{6,5},{7,6},{8,15},{9,8},{10,9... | collective-permute-start | bytes 135176 | tf_op jit(solution)/shard_map/ppermute | solution.py:32
  13.7 0.5 shard_map.126.refs_0_.refs_4_
  14.2 1.2 %collective-permute-done.2.refs_1_ = bf16[176,128]{1,0:T(8,128)(2,1)S(1)} collective-permute-done((bf16[176,128]{1,0:T(8,128)(2,1)S(1)}, bf16[176,128]{1,0:T(8,128)(2,1)S(1)}, u32[]{:S(2)}, u32[]{:S(2)}) %collective-permute-start.2) | collective-permute-done | bytes 45088 | tf_op jit(solution)/shard_map/ppermute | solution.py:32
  15.4 1.1 %collective-permute-done.3.refs_2_ = bf16[416,128]{1,0:T(8,128)(2,1)S(1)} collective-permute-done((bf16[416,128]{1,0:T(8,128)(2,1)S(1)}, bf16[416,128]{1,0:T(8,128)(2,1)S(1)}, u32[]{:S(2)}, u32[]{:S(2)}) %collective-permute-start.3) | collective-permute-done | bytes 106528 | tf_op jit(solution)/shard_map/ppermute | solution.py:32
  16.5 0.3 shard_map.127
  16.8 0.1 collective-permute-start.5
  16.8 3.5 %collective-permute-start.4 = (bf16[176,128]{1,0:T(8,128)(2,1)S(1)}, bf16[176,128]{1,0:T(8,128)(2,1)S(1)}, u32[]{:S(2)}, u32[]{:S(2)}) collective-permute-start(bf16[176,128]{1,0:T(8,128)(2,1)S(1)} %get-tuple-element.62), channel_id=1, source_target_pairs={{0,7},{1,0},{2,1},{3,2},{4,3},{5,4},{6,5},{7,6},{8,15},{9,8},{10,9... | collective-permute-start | bytes 135176 | tf_op jit(solution)/shard_map/ppermute | solution.py:32
  20.4 0.5 %shard_map.129.refs_8_ = f32[4,8,128]{2,1,0:T(8,128)S(1)} custom-call(s32[2,729]{1,0:T(2,128)S(1)} %get-tuple-element.65.refs_0_, s32[1,81]{1,0:T(1,128)S(1)} %get-tuple-element.66.refs_1_, s32[1,8]{1,0:T(1,128)S(1)} %get-tuple-element.67.refs_2_, f32[6,128]{1,0:T(8,128)S(1)} %get-tuple-element.68.refs_3_, f32[768,128]{1,0:T(8,128)S(1)} %shard_map.126.refs_0_.refs_4_), custom_call_target="tpu_custom_call" | custom-call | bytes 3000000 | tf_op jit(solution)/shard_map/pallas_call | solution.py:559
  20.9 0.5 shard_map.128.refs_0_
  21.4 0.7 %collective-permute-done.4.refs_1_ = bf16[176,128]{1,0:T(8,128)(2,1)S(1)} collective-permute-done((bf16[176,128]{1,0:T(8,128)(2,1)S(1)}, bf16[176,128]{1,0:T(8,128)(2,1)S(1)}, u32[]{:S(2)}, u32[]{:S(2)}) %collective-permute-start.4) | collective-permute-done | bytes 45088 | tf_op jit(solution)/shard_map/ppermute | solution.py:32
  22.1 0.8 %collective-permute-done.5.refs_2_ = bf16[416,128]{1,0:T(8,128)(2,1)S(1)} collective-permute-done((bf16[416,128]{1,0:T(8,128)(2,1)S(1)}, bf16[416,128]{1,0:T(8,128)(2,1)S(1)}, u32[]{:S(2)}, u32[]{:S(2)}) %collective-permute-start.5) | collective-permute-done | bytes 106528 | tf_op jit(solution)/shard_map/ppermute | solution.py:32
  22.9 1.3 %shard_map.130 = (f32[768,128]{1,0:T(8,128)S(1)}, bf16[416,128]{1,0:T(8,128)(2,1)S(1)}, bf16[176,128]{1,0:T(8,128)(2,1)S(1)}, f32[32,1,1408]{2,1,0:T(1,128)}) custom-call(f32[768,128]{1,0:T(8,128)S(1)} %shard_map.128.refs_0_, bf16[176,128]{1,0:T(8,128)(2,1)S(1)} %collective-permute-done.4.refs_1_, bf16[416,128]{1,0:T(8,128)(2,1)S(1)} %collective-permute-done.5.refs_2_, ...), custom_call_target="tpu_custom_call" | custom-call | bytes 3000000 | tf_op jit(solution)/shard_map/pallas_call | solution.py:454
  24.2 5.6 %all-to-all-start = ((f32[32,1,1408]{2,1,0:T(1,128)}), f32[32,1,1408]{2,1,0:T(1,128)S(1)}, u32[]{:S(2)}, u32[]{:S(2)}) async-start(f32[32,1,1408]{2,1,0:T(1,128)} %get-tuple-element.72), calls=%async_computation | async-start | bytes 360448 | tf_op jit(solution)/shard_map/all_to_all | solution.py:835
  29.8 0.3 collective-permute-start.7
  30.1 3.3 %collective-permute-start.6 = (bf16[176,128]{1,0:T(8,128)(2,1)S(1)}, bf16[176,128]{1,0:T(8,128)(2,1)S(1)}, u32[]{:S(2)}, u32[]{:S(2)}) collective-permute-start(bf16[176,128]{1,0:T(8,128)(2,1)S(1)} %get-tuple-element.70), channel_id=1, source_target_pairs={{0,7},{1,0},{2,1},{3,2},{4,3},{5,4},{6,5},{7,6},{8,15},{9,8},{10,9... | collective-permute-start | bytes 135176 | tf_op jit(solution)/shard_map/ppermute | solution.py:32
  33.4 0.5 shard_map.131.refs_0_
  33.9 4.6 %all-to-all-done.got_ref = f32[32,1,1408]{2,1,0:T(1,128)S(1)} async-done(((f32[32,1,1408]{2,1,0:T(1,128)}), f32[32,1,1408]{2,1,0:T(1,128)S(1)}, u32[]{:S(2)}, u32[]{:S(2)}) %all-to-all-start) | async-done | bytes 180256 | tf_op jit(solution)/shard_map/all_to_all | solution.py:835
  38.5 3.6 %shard_map.132 = (f32[768,128]{1,0:T(8,128)S(1)}, f32[6,128]{1,0:T(8,128)S(1)}) custom-call(f32[32,1,1408]{2,1,0:T(1,128)S(1)} %all-to-all-done.got_ref, f32[729,729]{1,0:T(8,128)} %matrix_hbm.1), custom_call_target="tpu_custom_call" | custom-call | bytes 12000000 | tf_op jit(solution)/shard_map/pallas_call | solution.py:708
  42.0 0.0 collective-permute-done.6.refs_1_
  42.0 0.0 collective-permute-done.7.refs_2_
  42.1 0.3 shard_map.133
  42.4 1.2 %collective-permute-start.9 = (bf16[416,128]{1,0:T(8,128)(2,1)S(1)}, bf16[416,128]{1,0:T(8,128)(2,1)S(1)}, u32[]{:S(2)}, u32[]{:S(2)}) collective-permute-start(bf16[416,128]{1,0:T(8,128)(2,1)S(1)} %get-tuple-element.76), channel_id=1, source_target_pairs={{0,1},{1,2},{2,3},{3,4},{4,5},{5,6},{6,7},{7,0},{8,9},{9,10},{10,1... | collective-permute-start | bytes 319496 | tf_op jit(solution)/shard_map/ppermute | solution.py:32
  43.6 2.4 %collective-permute-start.8 = (bf16[176,128]{1,0:T(8,128)(2,1)S(1)}, bf16[176,128]{1,0:T(8,128)(2,1)S(1)}, u32[]{:S(2)}, u32[]{:S(2)}) collective-permute-start(bf16[176,128]{1,0:T(8,128)(2,1)S(1)} %get-tuple-element.75), channel_id=1, source_target_pairs={{0,7},{1,0},{2,1},{3,2},{4,3},{5,4},{6,5},{7,6},{8,15},{9,8},{10,9... | collective-permute-start | bytes 135176 | tf_op jit(solution)/shard_map/ppermute | solution.py:32
  46.0 0.5 %shard_map.134.refs_0_ = f32[768,128]{1,0:T(8,128)S(1)} custom-call(f32[768,128]{1,0:T(8,128)S(1)} %get-tuple-element.74.refs_0_, f32[768,128]{1,0:T(8,128)S(1)} %get-tuple-element.69.refs_0_.refs_8_.refs_1_, f32[768,128]{1,0:T(8,128)S(1)} %get-tuple-element.45.refs_1_.refs_2_, f32[768,128]{1,0:T(8,128)S(1)} %get-tuple-element.73.refs_7_.refs_3_, ...), custom_call_target="tpu_custom_call" | custom-call | bytes 6000000 | tf_op jit(solution)/shard_map/pallas_call | solution.py:306
  46.5 1.2 %collective-permute-done.8.refs_1_ = bf16[176,128]{1,0:T(8,128)(2,1)S(1)} collective-permute-done((bf16[176,128]{1,0:T(8,128)(2,1)S(1)}, bf16[176,128]{1,0:T(8,128)(2,1)S(1)}, u32[]{:S(2)}, u32[]{:S(2)}) %collective-permute-start.8) | collective-permute-done | bytes 45088 | tf_op jit(solution)/shard_map/ppermute | solution.py:32
  47.7 0.7 %collective-permute-done.9.refs_2_ = bf16[416,128]{1,0:T(8,128)(2,1)S(1)} collective-permute-done((bf16[416,128]{1,0:T(8,128)(2,1)S(1)}, bf16[416,128]{1,0:T(8,128)(2,1)S(1)}, u32[]{:S(2)}, u32[]{:S(2)}) %collective-permute-start.9) | collective-permute-done | bytes 106528 | tf_op jit(solution)/shard_map/ppermute | solution.py:32
  48.4 1.0 %shard_map.135 = (f32[768,128]{1,0:T(8,128)}, f32[6,128]{1,0:T(8,128)}) custom-call(f32[768,128]{1,0:T(8,128)S(1)} %shard_map.134.refs_0_, bf16[176,128]{1,0:T(8,128)(2,1)S(1)} %collective-permute-done.8.refs_1_, bf16[416,128]{1,0:T(8,128)(2,1)S(1)} %collective-permute-done.9.refs_2_, bf16[304,176]{1,0:T(8,128)(2,1)S(1)} %get-tuple-element.52.refs_5_.refs_3_, ...), custom_call_target="tpu_custom_call" | custom-call | bytes 3000000 | tf_op jit(solution)/shard_map/pallas_call | solution.py:454
Async XLA Ops:
  1.9 7.2 %collective-permute-start.1 = (bf16[464,128]{1,0:T(8,128)(2,1)S(1)}, bf16[464,128]{1,0:T(8,128)(2,1)S(1)}, u32[]{:S(2)}, u32[]{:S(2)}) collective-permute-start(bf16[464,128]{1,0:T(8,128)(2,1)S(1)} %get-tuple-element.51), channel_id=1, source_target_pairs={{0,1},{1,2},{2,3},{3,4},{4,5},{5,6},{6,7},{7,0},{8,9},{9,10},{10,1... | collective-permute-start | bytes 356360 | tf_op jit(solution)/shard_map/ppermute | solution.py:32
  2.5 6.3 %collective-permute-start = (bf16[176,128]{1,0:T(8,128)(2,1)S(1)}, bf16[176,128]{1,0:T(8,128)(2,1)S(1)}, u32[]{:S(2)}, u32[]{:S(2)}) collective-permute-start(bf16[176,128]{1,0:T(8,128)(2,1)S(1)} %get-tuple-element.50.refs_3_), channel_id=1, source_target_pairs={{0,7},{1,0},{2,1},{3,2},{4,3},{5,4},{6,5},{7,6},{8,15},{9,8},{10,9... | collective-permute-start | bytes 135176 | tf_op jit(solution)/shard_map/ppermute | solution.py:32
  10.1 6.4 %collective-permute-start.3 = (bf16[416,128]{1,0:T(8,128)(2,1)S(1)}, bf16[416,128]{1,0:T(8,128)(2,1)S(1)}, u32[]{:S(2)}, u32[]{:S(2)}) collective-permute-start(bf16[416,128]{1,0:T(8,128)(2,1)S(1)} %get-tuple-element.58), channel_id=1, source_target_pairs={{0,1},{1,2},{2,3},{3,4},{4,5},{5,6},{6,7},{7,0},{8,9},{9,10},{10,1... | collective-permute-start | bytes 319496 | tf_op jit(solution)/shard_map/ppermute | solution.py:32
  10.4 5.0 %collective-permute-start.2 = (bf16[176,128]{1,0:T(8,128)(2,1)S(1)}, bf16[176,128]{1,0:T(8,128)(2,1)S(1)}, u32[]{:S(2)}, u32[]{:S(2)}) collective-permute-start(bf16[176,128]{1,0:T(8,128)(2,1)S(1)} %get-tuple-element.57), channel_id=1, source_target_pairs={{0,7},{1,0},{2,1},{3,2},{4,3},{5,4},{6,5},{7,6},{8,15},{9,8},{10,9... | collective-permute-start | bytes 135176 | tf_op jit(solution)/shard_map/ppermute | solution.py:32
  16.8 6.1 %collective-permute-start.5 = (bf16[416,128]{1,0:T(8,128)(2,1)S(1)}, bf16[416,128]{1,0:T(8,128)(2,1)S(1)}, u32[]{:S(2)}, u32[]{:S(2)}) collective-permute-start(bf16[416,128]{1,0:T(8,128)(2,1)S(1)} %get-tuple-element.63), channel_id=1, source_target_pairs={{0,1},{1,2},{2,3},{3,4},{4,5},{5,6},{6,7},{7,0},{8,9},{9,10},{10,1... | collective-permute-start | bytes 319496 | tf_op jit(solution)/shard_map/ppermute | solution.py:32
  16.8 5.2 %collective-permute-start.4 = (bf16[176,128]{1,0:T(8,128)(2,1)S(1)}, bf16[176,128]{1,0:T(8,128)(2,1)S(1)}, u32[]{:S(2)}, u32[]{:S(2)}) collective-permute-start(bf16[176,128]{1,0:T(8,128)(2,1)S(1)} %get-tuple-element.62), channel_id=1, source_target_pairs={{0,7},{1,0},{2,1},{3,2},{4,3},{5,4},{6,5},{7,6},{8,15},{9,8},{10,9... | collective-permute-start | bytes 135176 | tf_op jit(solution)/shard_map/ppermute | solution.py:32
  24.2 14.3 %all-to-all-start = ((f32[32,1,1408]{2,1,0:T(1,128)}), f32[32,1,1408]{2,1,0:T(1,128)S(1)}, u32[]{:S(2)}, u32[]{:S(2)}) async-start(f32[32,1,1408]{2,1,0:T(1,128)} %get-tuple-element.72), calls=%async_computation | async-start | bytes 360448 | tf_op jit(solution)/shard_map/all_to_all | solution.py:835
  29.8 12.3 %collective-permute-start.7 = (bf16[416,128]{1,0:T(8,128)(2,1)S(1)}, bf16[416,128]{1,0:T(8,128)(2,1)S(1)}, u32[]{:S(2)}, u32[]{:S(2)}) collective-permute-start(bf16[416,128]{1,0:T(8,128)(2,1)S(1)} %get-tuple-element.71), channel_id=1, source_target_pairs={{0,1},{1,2},{2,3},{3,4},{4,5},{5,6},{6,7},{7,0},{8,9},{9,10},{10,1... | collective-permute-start | bytes 319496 | tf_op jit(solution)/shard_map/ppermute | solution.py:32
  30.1 11.9 %collective-permute-start.6 = (bf16[176,128]{1,0:T(8,128)(2,1)S(1)}, bf16[176,128]{1,0:T(8,128)(2,1)S(1)}, u32[]{:S(2)}, u32[]{:S(2)}) collective-permute-start(bf16[176,128]{1,0:T(8,128)(2,1)S(1)} %get-tuple-element.70), channel_id=1, source_target_pairs={{0,7},{1,0},{2,1},{3,2},{4,3},{5,4},{6,5},{7,6},{8,15},{9,8},{10,9... | collective-permute-start | bytes 135176 | tf_op jit(solution)/shard_map/ppermute | solution.py:32
  42.4 6.1 %collective-permute-start.9 = (bf16[416,128]{1,0:T(8,128)(2,1)S(1)}, bf16[416,128]{1,0:T(8,128)(2,1)S(1)}, u32[]{:S(2)}, u32[]{:S(2)}) collective-permute-start(bf16[416,128]{1,0:T(8,128)(2,1)S(1)} %get-tuple-element.76), channel_id=1, source_target_pairs={{0,1},{1,2},{2,3},{3,4},{4,5},{5,6},{6,7},{7,0},{8,9},{9,10},{10,1... | collective-permute-start | bytes 319496 | tf_op jit(solution)/shard_map/ppermute | solution.py:32
  43.6 4.1 %collective-permute-start.8 = (bf16[176,128]{1,0:T(8,128)(2,1)S(1)}, bf16[176,128]{1,0:T(8,128)(2,1)S(1)}, u32[]{:S(2)}, u32[]{:S(2)}) collective-permute-start(bf16[176,128]{1,0:T(8,128)(2,1)S(1)} %get-tuple-element.75), channel_id=1, source_target_pairs={{0,7},{1,0},{2,1},{3,2},{4,3},{5,4},{6,5},{7,6},{8,15},{9,8},{10,9... | collective-permute-start | bytes 135176 | tf_op jit(solution)/shard_map/ppermute | solution.py:32
